TPU v7x, 256 devices: a whole 4x4x8 slice. The times are simulated.
256 devices in a mesh: grp: 16 (over y, z_hi, core), dev: 16 (over z_lo, x).
Axes of the slice: x: 4, y: 4, z: 8 (z_hi: 2, z_lo: 4; z = z_hi * 4 + z_lo), core: 2. Of those that a mesh axis runs over, the one named last changes fastest.
Arguments:
- panels: bfloat16 [256, 1536, 512], P(('grp', 'dev')), may hold values from -0.19921875 to 0.19921875
- panel_owner: int32 [16, 3], replicated, may hold values from 0 to 15, as said below
- interface_cols: bfloat16 [1536, 65536], P(None, ('grp', 'dev')), may hold values from -6 to 6
- border: bfloat16 [16384, 1536], P('grp', 'dev'), may hold values from -0.15625 to 0.15625
- block_rows: int32 [16, 8], replicated, may hold values from 0 to 31, as said below
- pattern: int32 [32, 32], P('grp', 'dev'), may hold values 0 or 1
- block_x: bfloat16 [4096, 256], P('dev'), may hold values from -0.09375 to 0.09375
Outputs:
- schur: bfloat16 [4096, 4096], P('grp', 'dev')
- product: float32 [4096, 256], P('grp')
Inputs may be any that keep to these rules, and one draw needn't show every extreme that they name: `panel_owner`: in each row the values are distinct. `block_rows`: in each row the values are distinct; for each subdomain the block rows with the same value of block // 2 (their owner group) come exactly 2 at a time; in every draw some owner group receives 2 block rows from every subdomain.
All inputs are finite; a program needn't handle non-finite values. No bound on the sum of `pattern` on one device may be relied on, other than what follows from the above.
Results may differ from a plain program's by a relative error of at most 0.017.
Values may be sent and summed in bfloat16 or wider, within the bound.
No kernel may reach another device: no remote copies, remote signals or barrier semaphores. Data moves between devices by JAX's collectives and lax.ppermute only.
A program may use at most 64 MiB of HBM per device.

v0:
```python
import jax
import jax.numpy as jnp
from jax import lax
from jax.experimental import pallas as pl
from jax.experimental.pallas import tpu as pltpu
from jax.sharding import PartitionSpec as P


F32 = jnp.float32
BF16 = jnp.bfloat16
ANY = pl.BlockSpec(memory_space=pl.ANY)
VMEM = pl.BlockSpec(memory_space=pltpu.VMEM)
SMEM = pl.BlockSpec(memory_space=pltpu.SMEM)


def hop_x(value, dx):
    perm = [(z * 4 + x, z * 4 + (x + dx) % 4) for z in range(4) for x in range(4)]
    return lax.ppermute(value, "dev", perm)


def hop_z(value, bits):
    perm = [(z * 4 + x, (z ^ bits) * 4 + x) for z in range(4) for x in range(4)]
    return lax.ppermute(value, "dev", perm)


def hop_y(value, dy):
    perm = [(y * 4 + r, ((y + dy) % 4) * 4 + r) for y in range(4) for r in range(4)]
    return lax.ppermute(value, "grp", perm)


def swap_grp(value, bits):
    return lax.ppermute(value, "grp", [(g, g ^ bits) for g in range(16)])


def gather_blocks(block):
    near = [hop_z(block, bits) for bits in (1, 2, 3)]
    low = jnp.stack([block, near[0]])
    high = jnp.stack([near[1], near[2]])
    low_left = hop_x(low, 1)
    high_right = hop_x(high, -1)
    high_left = hop_x(high, 1)
    low_right = hop_x(low, -1)
    low_far = hop_x(low_left, 1)
    high_far = hop_x(high_right, -1)
    return [low, high, low_left, high_left, low_right, high_right, low_far, high_far]


def block_source(part):
    dev = lax.axis_index("dev")
    return ((dev >> 2) ^ (part % 4)) * 4 + ((dev + (0, 3, 1, 2)[part // 4]) & 3)


HEIGHTS = (80, 48, 16)
OFFSETS = (0, 80, 128)
PIECE = 144


def pack_kernel(owners, slot, *refs):
    outs, (held, load_sem, sem) = refs[:4], refs[4:]
    group, dev = lax.axis_index("grp"), lax.axis_index("dev")
    x, z = dev & 3, dev >> 2
    row = lax.broadcasted_iota(jnp.int32, (256, 256), 0)
    col = lax.broadcasted_iota(jnp.int32, (256, 256), 1)
    for step in range(3):

        @pl.when(owners[group, step] == dev)
        def _():
            top = 512 * step
            load = pltpu.make_async_copy(slot.at[0, pl.ds(top, 1536 - top)], held.at[pl.ds(top, 1536 - top)], load_sem)
            load.start()
            load.wait()
            first = held[top : top + 256, :256].astype(F32)
            second = held[top + 256 : top + 512, 256:].astype(F32).T
            held[top + 256 : top + 512, 256:] = jnp.where(row > col, first, second).astype(BF16)
            height = HEIGHTS[step]
            copies = []
            for dx in range(4):
                for bits in range(4):
                    chunk = (z ^ bits) * 4 + ((x + dx) & 3)
                    start = pl.multiple_of(top + 256 + chunk * height, 16)
                    copies.append(
                        pltpu.make_async_copy(
                            held.at[pl.ds(start, height)],
                            outs[dx].at[bits, pl.ds(0, height)],
                            sem.at[dx * 4 + bits],
                        )
                    )
            for copy in copies:
                copy.start()
            for copy in copies:
                copy.wait()


def pack(owners, panels):
    return pl.pallas_call(
        pack_kernel,
        out_shape=[jax.ShapeDtypeStruct((4, HEIGHTS[0], 512), BF16)] * 4,
        in_specs=[SMEM, ANY],
        out_specs=[ANY] * 4,
        scratch_shapes=[
            pltpu.VMEM((1536, 512), BF16),
            pltpu.SemaphoreType.DMA,
            pltpu.SemaphoreType.DMA((16,)),
        ],
        cost_estimate=pl.CostEstimate(flops=1_000_000, bytes_accessed=2_800_000, transcendentals=0),
        compiler_params=pltpu.CompilerParams(vmem_limit_bytes=16 << 20),
        name="pack",
    )(owners, panels)


def pick_kernel(owners, *refs):
    chunks, outs, sem = refs[:4], refs[4:8], refs[8]
    group, dev = lax.axis_index("grp"), lax.axis_index("dev")

    def each(act):
        for step in range(3):
            owner = owners[group, step]
            for dx in range(4):

                @pl.when(owner == (dev >> 2) * 4 + ((dev - dx) & 3))
                def _():
                    for bits in range(4):
                        act(
                            pltpu.make_async_copy(
                                chunks[dx].at[bits, pl.ds(0, HEIGHTS[step])],
                                outs[bits].at[pl.ds(OFFSETS[step], HEIGHTS[step])],
                                sem.at[step * 4 + bits],
                            )
                        )

    each(lambda copy: copy.start())
    each(lambda copy: copy.wait())


def pick(owners, chunks):
    return pl.pallas_call(
        pick_kernel,
        out_shape=[jax.ShapeDtypeStruct((PIECE, 512), BF16)] * 4,
        in_specs=[SMEM] + [ANY] * 4,
        out_specs=[VMEM] * 4,
        scratch_shapes=[pltpu.SemaphoreType.DMA((12,))],
        cost_estimate=pl.CostEstimate(flops=1_000_000, bytes_accessed=1_200_000, transcendentals=0),
        compiler_params=pltpu.CompilerParams(vmem_limit_bytes=8 << 20),
        name="pick",
    )(owners, *chunks)


def tile_kernel(*refs):
    panels, strips, (cols, out, pan0, pan1, pan2, border, answer, sem) = refs[:8], refs[8:16], refs[16:]
    half = 256
    pans = (pan0, pan1, pan2)
    copies = [[], [], [], []]
    for part in range(16):
        source = block_source(part)
        for step in range(3):
            rows = HEIGHTS[step]
            start = pl.multiple_of(source * rows, 16)
            copies[step].append(
                pltpu.make_async_copy(
                    panels[part // 2].at[part % 2, pl.ds(OFFSETS[step], rows)],
                    pans[step].at[pl.ds(start, rows)],
                    sem.at[part * 4 + step],
                )
            )
        start = pl.multiple_of(source * 96, 32)
        copies[3].append(
            pltpu.make_async_copy(
                strips[part // 2].at[part % 2], border.at[pl.ds(start, 96)], sem.at[part * 4 + 3]
            )
        )
    for group in copies:
        for copy in group:
            copy.start()
    row = lax.broadcasted_iota(jnp.int32, (half, half), 0)
    col = lax.broadcasted_iota(jnp.int32, (half, half), 1)

    def dot(a, b):
        return jnp.dot(a, b, preferred_element_type=F32)

    def unit(below):
        return jnp.where(row > col, below, jnp.where(row == col, 1.0, 0.0)).astype(BF16)

    def inverse_times(step, current):
        pan = pans[step]
        for copy in copies[step]:
            copy.wait()
        shared = pan[:half, half:].astype(F32)
        high, low = current[:half], current[half:]
        upper = dot(unit(shared), high)
        lower = dot(pan[:half, :half], high) + dot(unit(shared.T), low)
        result = jnp.concatenate([upper, lower], axis=0).astype(BF16)
        answer[step * 512 : step * 512 + 512] = result
        return result

    first = inverse_times(0, cols[:512])
    rest = cols[512:].astype(F32) - dot(pan0[half:], first)
    second = inverse_times(1, rest[:512].astype(BF16))
    rest = rest[512:] - dot(pan1[half:], second)
    inverse_times(2, rest.astype(BF16))
    for copy in copies[3]:
        copy.wait()
    tile = lax.dot_general(answer[...], border[...], (((0,), (0,)), ((), ())), preferred_element_type=F32)
    for block in range(8):
        out[block] = tile[:, block * 128 : block * 128 + 128].astype(BF16)


def make_tile(panels, strips, cols):
    return pl.pallas_call(
        tile_kernel,
        out_shape=jax.ShapeDtypeStruct((8, 256, 128), BF16),
        in_specs=[ANY] * 16 + [VMEM],
        out_specs=VMEM,
        scratch_shapes=[
            pltpu.VMEM((1280, 512), BF16),
            pltpu.VMEM((768, 512), BF16),
            pltpu.VMEM((256, 512), BF16),
            pltpu.VMEM((1536, 1024), BF16),
            pltpu.VMEM((1536, 256), BF16),
            pltpu.SemaphoreType.DMA((64,)),
        ],
        cost_estimate=pl.CostEstimate(flops=1_500_000_000, bytes_accessed=8_000_000, transcendentals=0),
        compiler_params=pltpu.CompilerParams(vmem_limit_bytes=32 << 20),
        name="tile",
    )(*panels, *strips, cols)


def place_kernel(block_rows, own, other, *refs):
    outs, total = refs[:8], refs[8]
    group = lax.axis_index("grp")
    core = group & 1
    total[...] = jnp.zeros_like(total)
    for part in range(16):
        source, giver = (own, group) if part < 8 else (other, group ^ 1)
        target = block_rows[giver, part % 8]
        owner = target >> 1
        slot = (((owner >> 2) - (group >> 2)) & 3) * 4 + (((owner ^ group) >> 1) & 1) * 2 + (target & 1)

        @pl.when((owner & 1) == core)
        def _():
            total[slot] += source[part % 8].astype(F32)

    for dy in range(4):
        for half in range(2):
            outs[half * 4 + dy][...] = total[dy * 4 + half * 2 : dy * 4 + half * 2 + 2].astype(BF16)


def place(block_rows, own, other):
    return pl.pallas_call(
        place_kernel,
        out_shape=[jax.ShapeDtypeStruct((2, 256, 128), BF16)] * 8,
        in_specs=[SMEM, VMEM, VMEM],
        out_specs=[VMEM] * 8,
        scratch_shapes=[pltpu.VMEM((16, 256, 128), F32)],
        cost_estimate=pl.CostEstimate(flops=1_000_000, bytes_accessed=2_000_000, transcendentals=0),
        compiler_params=pltpu.CompilerParams(vmem_limit_bytes=32 << 20),
        name="place",
    )(block_rows, own, other)


def add_y(parts):
    moved = [part.astype(F32) for part in [parts[0]] + [hop_y(parts[dy], dy) for dy in (1, 2, 3)]]
    return (moved[0] + moved[2]) + (moved[1] + moved[3])


def step(panels, panel_owner, interface_cols, border, block_rows, pattern, block_x):
    group = lax.axis_index("grp")
    dev = lax.axis_index("dev")

    strips = gather_blocks(border.T)

    chunks = pack(panel_owner, panels)
    chunks = [chunks[0]] + [hop_x(chunks[dx], dx) for dx in (1, 2, 3)]
    pieces = pick(panel_owner, chunks)
    pieces = [pieces[0]] + [hop_z(pieces[bits], bits) for bits in (1, 2, 3)]
    owners = lax.dynamic_slice_in_dim(panel_owner, group, 1, 0)[0]
    near = owners // 4 ^ dev // 4
    row = lax.broadcasted_iota(jnp.int32, (PIECE, 1), 0)
    from_z = jnp.where(row < OFFSETS[1], near[0], jnp.where(row < OFFSETS[2], near[1], near[2]))
    piece = pieces[3]
    for bits in (0, 1, 2):
        piece = jnp.where(from_z == bits, pieces[bits], piece)
    tile = make_tile(gather_blocks(piece), strips, interface_cols)

    placed = place(block_rows, tile, swap_grp(tile, 1))
    other = add_y(placed[4:])
    mine = add_y(placed[:4])
    other = swap_grp(other.astype(BF16), 2)
    own_rows = (mine + other.astype(F32)).transpose(0, 2, 1)
    masked = own_rows.reshape(2, 128, 2, 128) * pattern.astype(F32)[:, None, :, None]
    schur = masked.reshape(256, 256).astype(BF16)

    partial = jnp.dot(schur, block_x, preferred_element_type=F32).astype(BF16)
    moved = [part.astype(F32) for part in [partial] + [hop_x(partial, dx) for dx in (1, 2, 3)]]
    row_sum = ((moved[0] + moved[2]) + (moved[1] + moved[3])).astype(BF16)
    moved = [part.astype(F32) for part in [row_sum] + [hop_z(row_sum, bits) for bits in (1, 2, 3)]]
    product = (moved[0] + moved[1]) + (moved[2] + moved[3])
    return (schur, product)


def solution(mesh):
    return jax.shard_map(
        step,
        mesh=mesh,
        in_specs=(
            P(("grp", "dev"), None, None),
            P(),
            P(None, ("grp", "dev")),
            P("grp", "dev"),
            P(),
            P("grp", "dev"),
            P("dev", None),
        ),
        out_specs=(P("grp", "dev"), P("grp", None)),
        check_vma=False,
    )
```

profile of v0, /device:TPU:8, one launch (start us, length us, event | category | flops | bytes accessed | tf_op | source)
XLA Modules:
  0.0 158.5 jit_solution(7313648126031022467)
XLA Ops:
  0.7 3.4 %collective-permute-start.16 = (bf16[96,1024]{1,0:T(8,128)(2,1)}, bf16[96,1024]{1,0:T(8,128)(2,1)S(1)}, u32[]{:S(2)}, u32[]{:S(2)}) collective-permute-start(bf16[96,1024]{1,0:T(8,128)(2,1)} %bitcast.27), channel_id=1, source_target_pairs={{0,8},{1,9},{2,10},{3,11},{4,12},{5,13},{6,14},{7,15},{8,0},{9,1},... | collective-permute-start | bytes 589832 | tf_op jit(solution)/shard_map/ppermute | solution.py:23
  8.5 2.9 %collective-permute-start = (bf16[4,80,512]{2,1,0:T(8,128)(2,1)S(1)}, bf16[4,80,512]{2,1,0:T(8,128)(2,1)S(1)}, u32[]{:S(2)}, u32[]{:S(2)}) collective-permute-start(bf16[4,80,512]{2,1,0:T(8,128)(2,1)S(1)} %get-tuple-element.19), channel_id=1, source_target_pairs={{0,1},{1,2},{2,3},{3,0},{4,5},{5,6},{6,7},{7,4},{8,9},{9,10},{10,1... | collective-permute-start | bytes 983048 | tf_op jit(solution)/shard_map/ppermute | solution.py:18
  16.9 2.6 %collective-permute-done.refs_1_ = bf16[4,80,512]{2,1,0:T(8,128)(2,1)S(1)} collective-permute-done((bf16[4,80,512]{2,1,0:T(8,128)(2,1)S(1)}, bf16[4,80,512]{2,1,0:T(8,128)(2,1)S(1)}, u32[]{:S(2)}, u32[]{:S(2)}) %collective-permute-start) | collective-permute-done | bytes 327712 | tf_op jit(solution)/shard_map/ppermute | solution.py:18
  19.5 8.0 %collective-permute-done.1.refs_2_ = bf16[4,80,512]{2,1,0:T(8,128)(2,1)S(1)} collective-permute-done((bf16[4,80,512]{2,1,0:T(8,128)(2,1)S(1)}, bf16[4,80,512]{2,1,0:T(8,128)(2,1)S(1)}, u32[]{:S(2)}, u32[]{:S(2)}) %collective-permute-start.1) | collective-permute-done | bytes 327712 | tf_op jit(solution)/shard_map/ppermute | solution.py:18
  30.7 2.5 %collective-permute-start.5 = (bf16[144,512]{1,0:T(8,128)(2,1)S(1)}, bf16[144,512]{1,0:T(8,128)(2,1)S(1)}, u32[]{:S(2)}, u32[]{:S(2)}) collective-permute-start(bf16[144,512]{1,0:T(8,128)(2,1)S(1)} %get-tuple-element.25), channel_id=1, source_target_pairs={{0,12},{1,13},{2,14},{3,15},{4,8},{5,9},{6,10},{7,11},{8,4},{9,5},... | collective-permute-start | bytes 442376 | tf_op jit(solution)/shard_map/ppermute | solution.py:23
  36.0 2.7 %collective-permute-start.21 = (bf16[2,96,1024]{2,1,0:T(8,128)(2,1)S(1)}, bf16[2,96,1024]{2,1,0:T(8,128)(2,1)S(1)}, u32[]{:S(2)}, u32[]{:S(2)}) collective-permute-start(bf16[2,96,1024]{2,1,0:T(8,128)(2,1)S(1)} %pad_maximum_fusion.1.refs_9_), channel_id=1, source_target_pairs={{0,3},{1,0},{2,1},{3,2},{4,7},{5,4},{6,5},{7,6},{8,11},{9,8},{10,9... | collective-permute-start | bytes 1179656 | tf_op jit(solution)/shard_map/ppermute | solution.py:18
  41.2 2.7 %collective-permute-done.5 = bf16[144,512]{1,0:T(8,128)(2,1)S(1)} collective-permute-done((bf16[144,512]{1,0:T(8,128)(2,1)S(1)}, bf16[144,512]{1,0:T(8,128)(2,1)S(1)}, u32[]{:S(2)}, u32[]{:S(2)}) %collective-permute-start.5) | collective-permute-done | bytes 147488 | tf_op jit(solution)/shard_map/ppermute | solution.py:23
  44.8 2.4 %collective-permute-start.8 = (bf16[144,512]{1,0:T(8,128)(2,1)S(1)}, bf16[144,512]{1,0:T(8,128)(2,1)S(1)}, u32[]{:S(2)}, u32[]{:S(2)}) collective-permute-start(bf16[144,512]{1,0:T(8,128)(2,1)S(1)} %select_select_fusion), channel_id=1, source_target_pairs={{0,12},{1,13},{2,14},{3,15},{4,8},{5,9},{6,10},{7,11},{8,4},{9,5},... | collective-permute-start | bytes 442376 | tf_op jit(solution)/shard_map/ppermute | solution.py:23
  47.7 8.8 %collective-permute-done.7 = bf16[144,512]{1,0:T(8,128)(2,1)S(1)} collective-permute-done((bf16[144,512]{1,0:T(8,128)(2,1)S(1)}, bf16[144,512]{1,0:T(8,128)(2,1)S(1)}, u32[]{:S(2)}, u32[]{:S(2)}) %collective-permute-start.7) | collective-permute-done | bytes 147488 | tf_op jit(solution)/shard_map/ppermute | solution.py:23
  57.6 2.1 %collective-permute-start.20 = (bf16[2,96,1024]{2,1,0:T(8,128)(2,1)S(1)}, bf16[2,96,1024]{2,1,0:T(8,128)(2,1)S(1)}, u32[]{:S(2)}, u32[]{:S(2)}) collective-permute-start(bf16[2,96,1024]{2,1,0:T(8,128)(2,1)S(1)} %pad_maximum_fusion.refs_8_), channel_id=1, source_target_pairs={{0,3},{1,0},{2,1},{3,2},{4,7},{5,4},{6,5},{7,6},{8,11},{9,8},{10,9... | collective-permute-start | bytes 1179656 | tf_op jit(solution)/shard_map/ppermute | solution.py:18
  62.3 7.4 %collective-permute-done.18.refs_10_ = bf16[2,96,1024]{2,1,0:T(8,128)(2,1)S(1)} collective-permute-done((bf16[2,96,1024]{2,1,0:T(8,128)(2,1)S(1)}, bf16[2,96,1024]{2,1,0:T(8,128)(2,1)S(1)}, u32[]{:S(2)}, u32[]{:S(2)}) %collective-permute-start.18) | collective-permute-done | bytes 393248 | tf_op jit(solution)/shard_map/ppermute | solution.py:18
  71.7 3.8 %collective-permute-done.12.refs_5_ = bf16[2,144,512]{2,1,0:T(8,128)(2,1)S(1)} collective-permute-done((bf16[2,144,512]{2,1,0:T(8,128)(2,1)S(1)}, bf16[2,144,512]{2,1,0:T(8,128)(2,1)S(1)}, u32[]{:S(2)}, u32[]{:S(2)}) %collective-permute-start.12) | collective-permute-done | bytes 294944 | tf_op jit(solution)/shard_map/ppermute | solution.py:18
  75.5 3.7 %collective-permute-start.11 = (bf16[2,144,512]{2,1,0:T(8,128)(2,1)S(1)}, bf16[2,144,512]{2,1,0:T(8,128)(2,1)S(1)}, u32[]{:S(2)}, u32[]{:S(2)}) collective-permute-start(bf16[2,144,512]{2,1,0:T(8,128)(2,1)S(1)} %pad_maximum_fusion.2.refs_0_), channel_id=1, source_target_pairs={{0,3},{1,0},{2,1},{3,2},{4,7},{5,4},{6,5},{7,6},{8,11},{9,8},{10,9... | collective-permute-start | bytes 884744 | tf_op jit(solution)/shard_map/ppermute | solution.py:18
  79.8 2.5 %collective-permute-done.9.refs_2_ = bf16[2,144,512]{2,1,0:T(8,128)(2,1)S(1)} collective-permute-done((bf16[2,144,512]{2,1,0:T(8,128)(2,1)S(1)}, bf16[2,144,512]{2,1,0:T(8,128)(2,1)S(1)}, u32[]{:S(2)}, u32[]{:S(2)}) %collective-permute-start.9) | collective-permute-done | bytes 294944 | tf_op jit(solution)/shard_map/ppermute | solution.py:18
  82.3 8.0 %collective-permute-done.11.refs_4_ = bf16[2,144,512]{2,1,0:T(8,128)(2,1)S(1)} collective-permute-done((bf16[2,144,512]{2,1,0:T(8,128)(2,1)S(1)}, bf16[2,144,512]{2,1,0:T(8,128)(2,1)S(1)}, u32[]{:S(2)}, u32[]{:S(2)}) %collective-permute-start.11) | collective-permute-done | bytes 294944 | tf_op jit(solution)/shard_map/ppermute | solution.py:18
  90.7 3.0 %collective-permute-done.14.refs_7_ = bf16[2,144,512]{2,1,0:T(8,128)(2,1)S(1)} collective-permute-done((bf16[2,144,512]{2,1,0:T(8,128)(2,1)S(1)}, bf16[2,144,512]{2,1,0:T(8,128)(2,1)S(1)}, u32[]{:S(2)}, u32[]{:S(2)}) %collective-permute-start.14) | collective-permute-done | bytes 294944 | tf_op jit(solution)/shard_map/ppermute | solution.py:18
  94.5 12.1 %tile.1.own = bf16[8,256,128]{2,1,0:T(8,128)(2,1)S(1)} custom-call(bf16[2,144,512]{2,1,0:T(8,128)(2,1)S(1)} %pad_maximum_fusion.2.refs_0_, bf16[2,144,512]{2,1,0:T(8,128)(2,1)S(1)} %pad_maximum_fusion.3.refs_1_, bf16[2,144,512]{2,1,0:T(8,128)(2,1)S(1)} %collective-permute-done.9.refs_2_, bf16[2,144,512]{2,1,0:T(8,128)(2,1)S(1)} %collective-permute-done.10.refs_3_, ...), custom_call_target="tpu_custom_call" | custom-call | flops 1500000000 | bytes 8000000 | tf_op jit(solution)/shard_map/tile/pallas_call | solution.py:208
  109.9 3.0 %collective-permute-start.28 = (bf16[2,256,128]{2,1,0:T(8,128)(2,1)S(1)}, bf16[2,256,128]{2,1,0:T(8,128)(2,1)S(1)}, u32[]{:S(2)}, u32[]{:S(2)}) collective-permute-start(bf16[2,256,128]{2,1,0:T(8,128)(2,1)S(1)} %get-tuple-element.31), channel_id=1, source_target_pairs={{0,128},{16,144},{32,160},{48,176},{64,192},{80,208},{96,224},{112... | collective-permute-start | bytes 393224 | tf_op jit(solution)/shard_map/ppermute | solution.py:28
  119.1 2.9 %collective-permute-done.30 = bf16[2,256,128]{2,1,0:T(8,128)(2,1)S(1)} collective-permute-done((bf16[2,256,128]{2,1,0:T(8,128)(2,1)S(1)}, bf16[2,256,128]{2,1,0:T(8,128)(2,1)S(1)}, u32[]{:S(2)}, u32[]{:S(2)}) %collective-permute-start.30) | collective-permute-done | bytes 131104 | tf_op jit(solution)/shard_map/ppermute | solution.py:28
  122.1 4.6 %collective-permute-start.31 = (bf16[2,256,128]{2,1,0:T(8,128)(2,1)S(1)}, bf16[2,256,128]{2,1,0:T(8,128)(2,1)S(1)}, u32[]{:S(2)}, u32[]{:S(2)}) collective-permute-start(bf16[2,256,128]{2,1,0:T(8,128)(2,1)S(1)} %add_convert_fusion.1), channel_id=1, source_target_pairs={{0,32},{16,48},{32,0},{48,16},{64,96},{80,112},{96,64},{112,80},{1... | collective-permute-start | bytes 393224 | tf_op jit(solution)/shard_map/ppermute | solution.py:32
  126.7 4.5 %collective-permute-done.31 = bf16[2,256,128]{2,1,0:T(8,128)(2,1)S(1)} collective-permute-done((bf16[2,256,128]{2,1,0:T(8,128)(2,1)S(1)}, bf16[2,256,128]{2,1,0:T(8,128)(2,1)S(1)}, u32[]{:S(2)}, u32[]{:S(2)}) %collective-permute-start.31) | collective-permute-done | bytes 131104 | tf_op jit(solution)/shard_map/ppermute | solution.py:32
  140.7 5.0 %collective-permute-start.35 = (bf16[256,256]{1,0:T(8,128)(2,1)S(1)}, bf16[256,256]{1,0:T(8,128)(2,1)S(1)}, u32[]{:S(2)}, u32[]{:S(2)}) collective-permute-start(bf16[256,256]{1,0:T(8,128)(2,1)S(1)} %add_convert_fusion), channel_id=1, source_target_pairs={{0,4},{1,5},{2,6},{3,7},{4,0},{5,1},{6,2},{7,3},{8,12},{9,13},{10,... | collective-permute-start | bytes 393224 | tf_op jit(solution)/shard_map/ppermute | solution.py:23
  145.7 2.5 %collective-permute-start.37 = (bf16[256,256]{1,0:T(8,128)(2,1)S(1)}, bf16[256,256]{1,0:T(8,128)(2,1)S(1)}, u32[]{:S(2)}, u32[]{:S(2)}) collective-permute-start(bf16[256,256]{1,0:T(8,128)(2,1)S(1)} %add_convert_fusion), channel_id=1, source_target_pairs={{0,12},{1,13},{2,14},{3,15},{4,8},{5,9},{6,10},{7,11},{8,4},{9,5},... | collective-permute-start | bytes 393224 | tf_op jit(solution)/shard_map/ppermute | solution.py:23
  149.6 8.1 %collective-permute-done.36 = bf16[256,256]{1,0:T(8,128)(2,1)S(1)} collective-permute-done((bf16[256,256]{1,0:T(8,128)(2,1)S(1)}, bf16[256,256]{1,0:T(8,128)(2,1)S(1)}, u32[]{:S(2)}, u32[]{:S(2)}) %collective-permute-start.36) | collective-permute-done | bytes 131104 | tf_op jit(solution)/shard_map/ppermute | solution.py:23
  (93 shorter events, 48.4 us)
Async XLA Ops:
  0.7 34.4 %collective-permute-start.16 = (bf16[96,1024]{1,0:T(8,128)(2,1)}, bf16[96,1024]{1,0:T(8,128)(2,1)S(1)}, u32[]{:S(2)}, u32[]{:S(2)}) collective-permute-start(bf16[96,1024]{1,0:T(8,128)(2,1)} %bitcast.27), channel_id=1, source_target_pairs={{0,8},{1,9},{2,10},{3,11},{4,12},{5,13},{6,14},{7,15},{8,0},{9,1},... | collective-permute-start | bytes 589832 | tf_op jit(solution)/shard_map/ppermute | solution.py:23
  4.0 32.0 %collective-permute-start.17 = (bf16[96,1024]{1,0:T(8,128)(2,1)}, bf16[96,1024]{1,0:T(8,128)(2,1)S(1)}, u32[]{:S(2)}, u32[]{:S(2)}) collective-permute-start(bf16[96,1024]{1,0:T(8,128)(2,1)} %bitcast.28), channel_id=1, source_target_pairs={{0,12},{1,13},{2,14},{3,15},{4,8},{5,9},{6,10},{7,11},{8,4},{9,5},... | collective-permute-start | bytes 589832 | tf_op jit(solution)/shard_map/ppermute | solution.py:23
  11.4 16.1 %collective-permute-start.1 = (bf16[4,80,512]{2,1,0:T(8,128)(2,1)S(1)}, bf16[4,80,512]{2,1,0:T(8,128)(2,1)S(1)}, u32[]{:S(2)}, u32[]{:S(2)}) collective-permute-start(bf16[4,80,512]{2,1,0:T(8,128)(2,1)S(1)} %get-tuple-element.20), channel_id=1, source_target_pairs={{0,2},{1,3},{2,0},{3,1},{4,6},{5,7},{6,4},{7,5},{8,10},{9,11},{10,... | collective-permute-start | bytes 983048 | tf_op jit(solution)/shard_map/ppermute | solution.py:18
  12.8 14.7 %collective-permute-start.2 = (bf16[4,80,512]{2,1,0:T(8,128)(2,1)S(1)}, bf16[4,80,512]{2,1,0:T(8,128)(2,1)S(1)}, u32[]{:S(2)}, u32[]{:S(2)}) collective-permute-start(bf16[4,80,512]{2,1,0:T(8,128)(2,1)S(1)} %get-tuple-element.21), channel_id=1, source_target_pairs={{0,3},{1,0},{2,1},{3,2},{4,7},{5,4},{6,5},{7,6},{8,11},{9,8},{10,9... | collective-permute-start | bytes 983048 | tf_op jit(solution)/shard_map/ppermute | solution.py:18
  28.7 12.0 %collective-permute-start.3 = (bf16[144,512]{1,0:T(8,128)(2,1)S(1)}, bf16[144,512]{1,0:T(8,128)(2,1)S(1)}, u32[]{:S(2)}, u32[]{:S(2)}) collective-permute-start(bf16[144,512]{1,0:T(8,128)(2,1)S(1)} %get-tuple-element.22), channel_id=1, source_target_pairs={{0,8},{1,9},{2,10},{3,11},{4,12},{5,13},{6,14},{7,15},{8,0},{9,1},... | collective-permute-start | bytes 442376 | tf_op jit(solution)/shard_map/ppermute | solution.py:23
  30.7 13.2 %collective-permute-start.5 = (bf16[144,512]{1,0:T(8,128)(2,1)S(1)}, bf16[144,512]{1,0:T(8,128)(2,1)S(1)}, u32[]{:S(2)}, u32[]{:S(2)}) collective-permute-start(bf16[144,512]{1,0:T(8,128)(2,1)S(1)} %get-tuple-element.25), channel_id=1, source_target_pairs={{0,12},{1,13},{2,14},{3,15},{4,8},{5,9},{6,10},{7,11},{8,4},{9,5},... | collective-permute-start | bytes 442376 | tf_op jit(solution)/shard_map/ppermute | solution.py:23
  35.1 12.2 %collective-permute-start.15 = (bf16[96,1024]{1,0:T(8,128)(2,1)S(1)}, bf16[96,1024]{1,0:T(8,128)(2,1)S(1)}, u32[]{:S(2)}, u32[]{:S(2)}) collective-permute-start(bf16[96,1024]{1,0:T(8,128)(2,1)S(1)} %bitcast.29), channel_id=1, source_target_pairs={{0,4},{1,5},{2,6},{3,7},{4,0},{5,1},{6,2},{7,3},{8,12},{9,13},{10,... | collective-permute-start | bytes 589832 | tf_op jit(solution)/shard_map/ppermute | solution.py:23
  36.0 25.9 %collective-permute-start.21 = (bf16[2,96,1024]{2,1,0:T(8,128)(2,1)S(1)}, bf16[2,96,1024]{2,1,0:T(8,128)(2,1)S(1)}, u32[]{:S(2)}, u32[]{:S(2)}) collective-permute-start(bf16[2,96,1024]{2,1,0:T(8,128)(2,1)S(1)} %pad_maximum_fusion.1.refs_9_), channel_id=1, source_target_pairs={{0,3},{1,0},{2,1},{3,2},{4,7},{5,4},{6,5},{7,6},{8,11},{9,8},{10,9... | collective-permute-start | bytes 1179656 | tf_op jit(solution)/shard_map/ppermute | solution.py:18
  40.7 21.5 %collective-permute-start.19 = (bf16[2,96,1024]{2,1,0:T(8,128)(2,1)S(1)}, bf16[2,96,1024]{2,1,0:T(8,128)(2,1)S(1)}, u32[]{:S(2)}, u32[]{:S(2)}) collective-permute-start(bf16[2,96,1024]{2,1,0:T(8,128)(2,1)S(1)} %pad_maximum_fusion.1.refs_9_), channel_id=1, source_target_pairs={{0,1},{1,2},{2,3},{3,0},{4,5},{5,6},{6,7},{7,4},{8,9},{9,10},{10,1... | collective-permute-start | bytes 1179656 | tf_op jit(solution)/shard_map/ppermute | solution.py:18
  44.0 12.4 %collective-permute-start.7 = (bf16[144,512]{1,0:T(8,128)(2,1)S(1)}, bf16[144,512]{1,0:T(8,128)(2,1)S(1)}, u32[]{:S(2)}, u32[]{:S(2)}) collective-permute-start(bf16[144,512]{1,0:T(8,128)(2,1)S(1)} %select_select_fusion), channel_id=1, source_target_pairs={{0,8},{1,9},{2,10},{3,11},{4,12},{5,13},{6,14},{7,15},{8,0},{9,1},... | collective-permute-start | bytes 442376 | tf_op jit(solution)/shard_map/ppermute | solution.py:23
  44.8 12.8 %collective-permute-start.8 = (bf16[144,512]{1,0:T(8,128)(2,1)S(1)}, bf16[144,512]{1,0:T(8,128)(2,1)S(1)}, u32[]{:S(2)}, u32[]{:S(2)}) collective-permute-start(bf16[144,512]{1,0:T(8,128)(2,1)S(1)} %select_select_fusion), channel_id=1, source_target_pairs={{0,12},{1,13},{2,14},{3,15},{4,8},{5,9},{6,10},{7,11},{8,4},{9,5},... | collective-permute-start | bytes 442376 | tf_op jit(solution)/shard_map/ppermute | solution.py:23
  47.3 12.5 %collective-permute-start.6 = (bf16[144,512]{1,0:T(8,128)(2,1)S(1)}, bf16[144,512]{1,0:T(8,128)(2,1)S(1)}, u32[]{:S(2)}, u32[]{:S(2)}) collective-permute-start(bf16[144,512]{1,0:T(8,128)(2,1)S(1)} %select_select_fusion), channel_id=1, source_target_pairs={{0,4},{1,5},{2,6},{3,7},{4,0},{5,1},{6,2},{7,3},{8,12},{9,13},{10,... | collective-permute-start | bytes 442376 | tf_op jit(solution)/shard_map/ppermute | solution.py:23
  56.5 13.2 %collective-permute-start.18 = (bf16[2,96,1024]{2,1,0:T(8,128)(2,1)S(1)}, bf16[2,96,1024]{2,1,0:T(8,128)(2,1)S(1)}, u32[]{:S(2)}, u32[]{:S(2)}) collective-permute-start(bf16[2,96,1024]{2,1,0:T(8,128)(2,1)S(1)} %pad_maximum_fusion.refs_8_), channel_id=1, source_target_pairs={{0,1},{1,2},{2,3},{3,0},{4,5},{5,6},{6,7},{7,4},{8,9},{9,10},{10,1... | collective-permute-start | bytes 1179656 | tf_op jit(solution)/shard_map/ppermute | solution.py:18
  57.6 13.9 %collective-permute-start.20 = (bf16[2,96,1024]{2,1,0:T(8,128)(2,1)S(1)}, bf16[2,96,1024]{2,1,0:T(8,128)(2,1)S(1)}, u32[]{:S(2)}, u32[]{:S(2)}) collective-permute-start(bf16[2,96,1024]{2,1,0:T(8,128)(2,1)S(1)} %pad_maximum_fusion.refs_8_), channel_id=1, source_target_pairs={{0,3},{1,0},{2,1},{3,2},{4,7},{5,4},{6,5},{7,6},{8,11},{9,8},{10,9... | collective-permute-start | bytes 1179656 | tf_op jit(solution)/shard_map/ppermute | solution.py:18
  59.8 15.8 %collective-permute-start.12 = (bf16[2,144,512]{2,1,0:T(8,128)(2,1)S(1)}, bf16[2,144,512]{2,1,0:T(8,128)(2,1)S(1)}, u32[]{:S(2)}, u32[]{:S(2)}) collective-permute-start(bf16[2,144,512]{2,1,0:T(8,128)(2,1)S(1)} %pad_maximum_fusion.3.refs_1_), channel_id=1, source_target_pairs={{0,3},{1,0},{2,1},{3,2},{4,7},{5,4},{6,5},{7,6},{8,11},{9,8},{10,9... | collective-permute-start | bytes 884744 | tf_op jit(solution)/shard_map/ppermute | solution.py:18
  61.9 17.4 %collective-permute-start.10 = (bf16[2,144,512]{2,1,0:T(8,128)(2,1)S(1)}, bf16[2,144,512]{2,1,0:T(8,128)(2,1)S(1)}, u32[]{:S(2)}, u32[]{:S(2)}) collective-permute-start(bf16[2,144,512]{2,1,0:T(8,128)(2,1)S(1)} %pad_maximum_fusion.3.refs_1_), channel_id=1, source_target_pairs={{0,1},{1,2},{2,3},{3,0},{4,5},{5,6},{6,7},{7,4},{8,9},{9,10},{10,1... | collective-permute-start | bytes 884744 | tf_op jit(solution)/shard_map/ppermute | solution.py:18
  62.2 20.1 %collective-permute-start.9 = (bf16[2,144,512]{2,1,0:T(8,128)(2,1)S(1)}, bf16[2,144,512]{2,1,0:T(8,128)(2,1)S(1)}, u32[]{:S(2)}, u32[]{:S(2)}) collective-permute-start(bf16[2,144,512]{2,1,0:T(8,128)(2,1)S(1)} %pad_maximum_fusion.2.refs_0_), channel_id=1, source_target_pairs={{0,1},{1,2},{2,3},{3,0},{4,5},{5,6},{6,7},{7,4},{8,9},{9,10},{10,1... | collective-permute-start | bytes 884744 | tf_op jit(solution)/shard_map/ppermute | solution.py:18
  69.7 20.6 %collective-permute-start.23 = (bf16[2,96,1024]{2,1,0:T(8,128)(2,1)S(1)}, bf16[2,96,1024]{2,1,0:T(8,128)(2,1)S(1)}, u32[]{:S(2)}, u32[]{:S(2)}) collective-permute-start(bf16[2,96,1024]{2,1,0:T(8,128)(2,1)S(1)} %collective-permute-done.21.refs_13_), channel_id=1, source_target_pairs={{0,3},{1,0},{2,1},{3,2},{4,7},{5,4},{6,5},{7,6},{8,11},{9,8},{10,9... | collective-permute-start | bytes 1179656 | tf_op jit(solution)/shard_map/ppermute | solution.py:18
  71.5 19.3 %collective-permute-start.22 = (bf16[2,96,1024]{2,1,0:T(8,128)(2,1)S(1)}, bf16[2,96,1024]{2,1,0:T(8,128)(2,1)S(1)}, u32[]{:S(2)}, u32[]{:S(2)}) collective-permute-start(bf16[2,96,1024]{2,1,0:T(8,128)(2,1)S(1)} %collective-permute-done.18.refs_10_), channel_id=1, source_target_pairs={{0,1},{1,2},{2,3},{3,0},{4,5},{5,6},{6,7},{7,4},{8,9},{9,10},{10,1... | collective-permute-start | bytes 1179656 | tf_op jit(solution)/shard_map/ppermute | solution.py:18
  75.5 14.7 %collective-permute-start.11 = (bf16[2,144,512]{2,1,0:T(8,128)(2,1)S(1)}, bf16[2,144,512]{2,1,0:T(8,128)(2,1)S(1)}, u32[]{:S(2)}, u32[]{:S(2)}) collective-permute-start(bf16[2,144,512]{2,1,0:T(8,128)(2,1)S(1)} %pad_maximum_fusion.2.refs_0_), channel_id=1, source_target_pairs={{0,3},{1,0},{2,1},{3,2},{4,7},{5,4},{6,5},{7,6},{8,11},{9,8},{10,9... | collective-permute-start | bytes 884744 | tf_op jit(solution)/shard_map/ppermute | solution.py:18
  79.2 14.5 %collective-permute-start.14 = (bf16[2,144,512]{2,1,0:T(8,128)(2,1)S(1)}, bf16[2,144,512]{2,1,0:T(8,128)(2,1)S(1)}, u32[]{:S(2)}, u32[]{:S(2)}) collective-permute-start(bf16[2,144,512]{2,1,0:T(8,128)(2,1)S(1)} %collective-permute-done.12.refs_5_), channel_id=1, source_target_pairs={{0,3},{1,0},{2,1},{3,2},{4,7},{5,4},{6,5},{7,6},{8,11},{9,8},{10,9... | collective-permute-start | bytes 884744 | tf_op jit(solution)/shard_map/ppermute | solution.py:18
  82.3 12.2 %collective-permute-start.13 = (bf16[2,144,512]{2,1,0:T(8,128)(2,1)S(1)}, bf16[2,144,512]{2,1,0:T(8,128)(2,1)S(1)}, u32[]{:S(2)}, u32[]{:S(2)}) collective-permute-start(bf16[2,144,512]{2,1,0:T(8,128)(2,1)S(1)} %collective-permute-done.9.refs_2_), channel_id=1, source_target_pairs={{0,1},{1,2},{2,3},{3,0},{4,5},{5,6},{6,7},{7,4},{8,9},{9,10},{10,1... | collective-permute-start | bytes 884744 | tf_op jit(solution)/shard_map/ppermute | solution.py:18
  145.7 12.0 %collective-permute-start.36 = (bf16[256,256]{1,0:T(8,128)(2,1)S(1)}, bf16[256,256]{1,0:T(8,128)(2,1)S(1)}, u32[]{:S(2)}, u32[]{:S(2)}) collective-permute-start(bf16[256,256]{1,0:T(8,128)(2,1)S(1)} %add_convert_fusion), channel_id=1, source_target_pairs={{0,8},{1,9},{2,10},{3,11},{4,12},{5,13},{6,14},{7,15},{8,0},{9,1},... | collective-permute-start | bytes 393224 | tf_op jit(solution)/shard_map/ppermute | solution.py:23
  145.7 12.0 %collective-permute-start.37 = (bf16[256,256]{1,0:T(8,128)(2,1)S(1)}, bf16[256,256]{1,0:T(8,128)(2,1)S(1)}, u32[]{:S(2)}, u32[]{:S(2)}) collective-permute-start(bf16[256,256]{1,0:T(8,128)(2,1)S(1)} %add_convert_fusion), channel_id=1, source_target_pairs={{0,12},{1,13},{2,14},{3,15},{4,8},{5,9},{6,10},{7,11},{8,4},{9,5},... | collective-permute-start | bytes 393224 | tf_op jit(solution)/shard_map/ppermute | solution.py:23
  (22 other events, 439.8 us)
where the time goes:
time: 159 us; the launch traced here: 158 us
  waiting for transfers between devices  74.1 us (47%)
  starting transfers between devices  59.6 us (37%)
  Pallas kernels  15.4 us (10%)
  other arithmetic  4.98 us (3%)
  local copies, waits for them, and re-layouts  3.31 us (2%)
    ppermute x18, waiting for transfers between devices, hop_x(): return lax.ppermute(value, 'dev', perm)  40.2 us
    ppermute x18, starting transfers between devices, hop_x(): return lax.ppermute(value, 'dev', perm)  26.2 us
    ppermute x12, waiting for transfers between devices, hop_z(): return lax.ppermute(value, 'dev', perm)  23.1 us
    ppermute x12, starting transfers between devices, hop_z(): return lax.ppermute(value, 'dev', perm)  21.2 us
    pallas_call x1, Pallas kernels, make_tile(): pl.pallas_call(tile_kernel, out_shape=jax.ShapeDtypeStruct((8, 256, 128),...  12.1 us
    ppermute x6, starting transfers between devices, hop_y(): return lax.ppermute(value, 'grp', perm)  7.59 us
    ppermute x2, waiting for transfers between devices, swap_grp(): return lax.ppermute(value, 'grp', [(g, g ^ bits) for g in range(16)])  6.28 us
    ppermute x2, starting transfers between devices, swap_grp(): return lax.ppermute(value, 'grp', [(g, g ^ bits) for g in range(16)])  4.65 us
  transfers between devices with their start and end apart: 38, of which 22 were waited for; matrix products, arithmetic and copies ran while one was open for 4% of the time, Pallas kernels for 1%

commit v1 on v0

--- a/solution.py
+++ b/solution.py
@@ -8,7 +8,6 @@
 
 F32 = jnp.float32
 BF16 = jnp.bfloat16
-ANY = pl.BlockSpec(memory_space=pl.ANY)
 VMEM = pl.BlockSpec(memory_space=pltpu.VMEM)
 SMEM = pl.BlockSpec(memory_space=pltpu.SMEM)
 
@@ -56,52 +55,38 @@
 
 
 def pack_kernel(owners, slot, *refs):
-    outs, (held, load_sem, sem) = refs[:4], refs[4:]
+    outs, (held, sem) = refs[:4], refs[4:]
     group, dev = lax.axis_index("grp"), lax.axis_index("dev")
-    x, z = dev & 3, dev >> 2
     row = lax.broadcasted_iota(jnp.int32, (256, 256), 0)
     col = lax.broadcasted_iota(jnp.int32, (256, 256), 1)
     for step in range(3):
 
-        @pl.when(owners[group, step] == dev)
+        @pl.when(owners[step, group] == dev)
         def _():
             top = 512 * step
-            load = pltpu.make_async_copy(slot.at[0, pl.ds(top, 1536 - top)], held.at[pl.ds(top, 1536 - top)], load_sem)
+            load = pltpu.make_async_copy(
+                slot.at[0, pl.ds(top, 1536 - top)], held.at[pl.ds(top, 1536 - top)], sem
+            )
             load.start()
             load.wait()
             first = held[top : top + 256, :256].astype(F32)
             second = held[top + 256 : top + 512, 256:].astype(F32).T
             held[top + 256 : top + 512, 256:] = jnp.where(row > col, first, second).astype(BF16)
             height = HEIGHTS[step]
-            copies = []
             for dx in range(4):
                 for bits in range(4):
-                    chunk = (z ^ bits) * 4 + ((x + dx) & 3)
+                    chunk = ((dev >> 2) ^ bits) * 4 + ((dev + dx) & 3)
                     start = pl.multiple_of(top + 256 + chunk * height, 16)
-                    copies.append(
-                        pltpu.make_async_copy(
-                            held.at[pl.ds(start, height)],
-                            outs[dx].at[bits, pl.ds(0, height)],
-                            sem.at[dx * 4 + bits],
-                        )
-                    )
-            for copy in copies:
-                copy.start()
-            for copy in copies:
-                copy.wait()
+                    outs[dx][bits, :height] = held[pl.ds(start, height)]
 
 
 def pack(owners, panels):
     return pl.pallas_call(
         pack_kernel,
         out_shape=[jax.ShapeDtypeStruct((4, HEIGHTS[0], 512), BF16)] * 4,
-        in_specs=[SMEM, ANY],
-        out_specs=[ANY] * 4,
-        scratch_shapes=[
-            pltpu.VMEM((1536, 512), BF16),
-            pltpu.SemaphoreType.DMA,
-            pltpu.SemaphoreType.DMA((16,)),
-        ],
+        in_specs=[SMEM, pl.BlockSpec(memory_space=pltpu.HBM)],
+        out_specs=[VMEM] * 4,
+        scratch_shapes=[pltpu.VMEM((1536, 512), BF16), pltpu.SemaphoreType.DMA],
         cost_estimate=pl.CostEstimate(flops=1_000_000, bytes_accessed=2_800_000, transcendentals=0),
         compiler_params=pltpu.CompilerParams(vmem_limit_bytes=16 << 20),
         name="pack",
@@ -109,36 +94,25 @@
 
 
 def pick_kernel(owners, *refs):
-    chunks, outs, sem = refs[:4], refs[4:8], refs[8]
+    chunks, outs = refs[:4], refs[4:]
     group, dev = lax.axis_index("grp"), lax.axis_index("dev")
-
-    def each(act):
-        for step in range(3):
-            owner = owners[group, step]
-            for dx in range(4):
-
-                @pl.when(owner == (dev >> 2) * 4 + ((dev - dx) & 3))
-                def _():
-                    for bits in range(4):
-                        act(
-                            pltpu.make_async_copy(
-                                chunks[dx].at[bits, pl.ds(0, HEIGHTS[step])],
-                                outs[bits].at[pl.ds(OFFSETS[step], HEIGHTS[step])],
-                                sem.at[step * 4 + bits],
-                            )
-                        )
-
-    each(lambda copy: copy.start())
-    each(lambda copy: copy.wait())
+    for step in range(3):
+        first, rows = OFFSETS[step], HEIGHTS[step]
+        owner = owners[step, group]
+        for dx in range(4):
+
+            @pl.when(owner == (dev >> 2) * 4 + ((dev - dx) & 3))
+            def _():
+                for bits in range(4):
+                    outs[bits][first : first + rows] = chunks[dx][bits, :rows]
 
 
 def pick(owners, chunks):
     return pl.pallas_call(
         pick_kernel,
         out_shape=[jax.ShapeDtypeStruct((PIECE, 512), BF16)] * 4,
-        in_specs=[SMEM] + [ANY] * 4,
+        in_specs=[SMEM] + [VMEM] * 4,
         out_specs=[VMEM] * 4,
-        scratch_shapes=[pltpu.SemaphoreType.DMA((12,))],
         cost_estimate=pl.CostEstimate(flops=1_000_000, bytes_accessed=1_200_000, transcendentals=0),
         compiler_params=pltpu.CompilerParams(vmem_limit_bytes=8 << 20),
         name="pick",
@@ -146,31 +120,10 @@
 
 
 def tile_kernel(*refs):
-    panels, strips, (cols, out, pan0, pan1, pan2, border, answer, sem) = refs[:8], refs[8:16], refs[16:]
+    panels, strips, (cols, out, pan0, pan1, pan2, border, answer) = refs[:8], refs[8:16], refs[16:]
     half = 256
     pans = (pan0, pan1, pan2)
-    copies = [[], [], [], []]
-    for part in range(16):
-        source = block_source(part)
-        for step in range(3):
-            rows = HEIGHTS[step]
-            start = pl.multiple_of(source * rows, 16)
-            copies[step].append(
-                pltpu.make_async_copy(
-                    panels[part // 2].at[part % 2, pl.ds(OFFSETS[step], rows)],
-                    pans[step].at[pl.ds(start, rows)],
-                    sem.at[part * 4 + step],
-                )
-            )
-        start = pl.multiple_of(source * 96, 32)
-        copies[3].append(
-            pltpu.make_async_copy(
-                strips[part // 2].at[part % 2], border.at[pl.ds(start, 96)], sem.at[part * 4 + 3]
-            )
-        )
-    for group in copies:
-        for copy in group:
-            copy.start()
+    sources = [block_source(part) for part in range(16)]
     row = lax.broadcasted_iota(jnp.int32, (half, half), 0)
     col = lax.broadcasted_iota(jnp.int32, (half, half), 1)
 
@@ -181,9 +134,9 @@
         return jnp.where(row > col, below, jnp.where(row == col, 1.0, 0.0)).astype(BF16)
 
     def inverse_times(step, current):
-        pan = pans[step]
-        for copy in copies[step]:
-            copy.wait()
+        pan, first, rows = pans[step], OFFSETS[step], HEIGHTS[step]
+        for part, source in enumerate(sources):
+            pan[pl.ds(pl.multiple_of(source * rows, 16), rows)] = panels[part // 2][part % 2, first : first + rows]
         shared = pan[:half, half:].astype(F32)
         high, low = current[:half], current[half:]
         upper = dot(unit(shared), high)
@@ -197,8 +150,8 @@
     second = inverse_times(1, rest[:512].astype(BF16))
     rest = rest[512:] - dot(pan1[half:], second)
     inverse_times(2, rest.astype(BF16))
-    for copy in copies[3]:
-        copy.wait()
+    for part, source in enumerate(sources):
+        border[pl.ds(pl.multiple_of(source * 96, 32), 96)] = strips[part // 2][part % 2]
     tile = lax.dot_general(answer[...], border[...], (((0,), (0,)), ((), ())), preferred_element_type=F32)
     for block in range(8):
         out[block] = tile[:, block * 128 : block * 128 + 128].astype(BF16)
@@ -208,7 +161,7 @@
     return pl.pallas_call(
         tile_kernel,
         out_shape=jax.ShapeDtypeStruct((8, 256, 128), BF16),
-        in_specs=[ANY] * 16 + [VMEM],
+        in_specs=[VMEM] * 17,
         out_specs=VMEM,
         scratch_shapes=[
             pltpu.VMEM((1280, 512), BF16),
@@ -216,7 +169,6 @@
             pltpu.VMEM((256, 512), BF16),
             pltpu.VMEM((1536, 1024), BF16),
             pltpu.VMEM((1536, 256), BF16),
-            pltpu.SemaphoreType.DMA((64,)),
         ],
         cost_estimate=pl.CostEstimate(flops=1_500_000_000, bytes_accessed=8_000_000, transcendentals=0),
         compiler_params=pltpu.CompilerParams(vmem_limit_bytes=32 << 20),
@@ -231,7 +183,7 @@
     total[...] = jnp.zeros_like(total)
     for part in range(16):
         source, giver = (own, group) if part < 8 else (other, group ^ 1)
-        target = block_rows[giver, part % 8]
+        target = block_rows[part % 8, giver]
         owner = target >> 1
         slot = (((owner >> 2) - (group >> 2)) & 3) * 4 + (((owner ^ group) >> 1) & 1) * 2 + (target & 1)
 
@@ -268,9 +220,10 @@
 
     strips = gather_blocks(border.T)
 
-    chunks = pack(panel_owner, panels)
-    chunks = [chunks[0]] + [hop_x(chunks[dx], dx) for dx in (1, 2, 3)]
-    pieces = pick(panel_owner, chunks)
+    chunks = pack(panel_owner.T, panels)
+    far = hop_x(chunks[2], 2)
+    chunks = [chunks[0], hop_x(chunks[1], 1), far, hop_x(chunks[3], 3)]
+    pieces = pick(panel_owner.T, chunks)
     pieces = [pieces[0]] + [hop_z(pieces[bits], bits) for bits in (1, 2, 3)]
     owners = lax.dynamic_slice_in_dim(panel_owner, group, 1, 0)[0]
     near = owners // 4 ^ dev // 4
@@ -281,7 +234,7 @@
         piece = jnp.where(from_z == bits, pieces[bits], piece)
     tile = make_tile(gather_blocks(piece), strips, interface_cols)
 
-    placed = place(block_rows, tile, swap_grp(tile, 1))
+    placed = place(block_rows.T, tile, swap_grp(tile, 1))
     other = add_y(placed[4:])
     mine = add_y(placed[:4])
     other = swap_grp(other.astype(BF16), 2)

time: 159 us -> 148 us (0.931)
  Pallas kernels: 15.4 us -> 4.94 us
  waiting for transfers between devices: 74.1 us -> 69 us
  starting transfers between devices: 59.6 us -> 64 us
    pallas_call x1, Pallas kernels: 12.1 us -> 2.54 us  [make_tile(): pl.pallas_call(tile_kernel, out_shape=jax.ShapeDtypeStruct((8, 256, 128),...]
    ppermute x18, waiting for transfers between devices: 40.2 us -> 36.7 us  [hop_x(): return lax.ppermute(value, 'dev', perm)]
    ppermute x6, starting transfers between devices: 7.59 us -> 10.6 us  [hop_y(): return lax.ppermute(value, 'grp', perm)]
    ppermute x18, starting transfers between devices: 26.2 us -> 28.3 us  [hop_x(): return lax.ppermute(value, 'dev', perm)]
  transfers between devices with their start and end apart: 38 -> 38, of which waited for: 22 -> 21; matrix products, arithmetic and copies ran while one was open for 4% -> 3% of each run, Pallas kernels for 1% -> 1%
where the time goes in v1:
time: 148 us; the launch traced here: 147 us
  waiting for transfers between devices  69 us (47%)
  starting transfers between devices  64 us (43%)
  other arithmetic  5.16 us (3%)
  Pallas kernels  4.94 us (3%)
  local copies, waits for them, and re-layouts  3.19 us (2%)
    ppermute x18, waiting for transfers between devices, hop_x(): return lax.ppermute(value, 'dev', perm)  36.7 us
    ppermute x18, starting transfers between devices, hop_x(): return lax.ppermute(value, 'dev', perm)  28.3 us
    ppermute x12, waiting for transfers between devices, hop_z(): return lax.ppermute(value, 'dev', perm)  21.8 us
    ppermute x12, starting transfers between devices, hop_z(): return lax.ppermute(value, 'dev', perm)  20.8 us
    ppermute x6, starting transfers between devices, hop_y(): return lax.ppermute(value, 'grp', perm)  10.6 us
    ppermute x2, waiting for transfers between devices, swap_grp(): return lax.ppermute(value, 'grp', [(g, g ^ bits) for g in range(16)])  6.76 us
    ppermute x2, starting transfers between devices, swap_grp(): return lax.ppermute(value, 'grp', [(g, g ^ bits) for g in range(16)])  4.27 us
    eq x2, other arithmetic, step(): piece = jnp.where(from_z == bits, pieces[bits], piece)  3.86 us
  transfers between devices with their start and end apart: 38, of which 21 were waited for; matrix products, arithmetic and copies ran while one was open for 3% of the time, Pallas kernels for 1%

profile of v1, /device:TPU:8, one launch (start us, length us, event | category | flops | bytes accessed | tf_op | source)
XLA Modules:
  0.0 147.4 jit_solution(1663058080913762120)
XLA Ops:
  0.7 3.4 %collective-permute-start.16 = (bf16[96,1024]{1,0:T(8,128)(2,1)}, bf16[96,1024]{1,0:T(8,128)(2,1)S(1)}, u32[]{:S(2)}, u32[]{:S(2)}) collective-permute-start(bf16[96,1024]{1,0:T(8,128)(2,1)} %bitcast.32), channel_id=1, source_target_pairs={{0,8},{1,9},{2,10},{3,11},{4,12},{5,13},{6,14},{7,15},{8,0},{9,1},... | collective-permute-start | bytes 589832 | tf_op jit(solution)/shard_map/ppermute | solution.py:22
  10.0 2.5 %collective-permute-start.1 = (bf16[4,80,512]{2,1,0:T(8,128)(2,1)S(1)}, bf16[4,80,512]{2,1,0:T(8,128)(2,1)S(1)}, u32[]{:S(2)}, u32[]{:S(2)}) collective-permute-start(bf16[4,80,512]{2,1,0:T(8,128)(2,1)S(1)} %get-tuple-element.20), channel_id=1, source_target_pairs={{0,2},{1,3},{2,0},{3,1},{4,6},{5,7},{6,4},{7,5},{8,10},{9,11},{10,... | collective-permute-start | bytes 983048 | tf_op jit(solution)/shard_map/ppermute | solution.py:17
  18.7 8.1 %collective-permute-done.1.refs_2_ = bf16[4,80,512]{2,1,0:T(8,128)(2,1)S(1)} collective-permute-done((bf16[4,80,512]{2,1,0:T(8,128)(2,1)S(1)}, bf16[4,80,512]{2,1,0:T(8,128)(2,1)S(1)}, u32[]{:S(2)}, u32[]{:S(2)}) %collective-permute-start.1) | collective-permute-done | bytes 327712 | tf_op jit(solution)/shard_map/ppermute | solution.py:17
  34.1 2.2 %collective-permute-start.21 = (bf16[2,96,1024]{2,1,0:T(8,128)(2,1)S(1)}, bf16[2,96,1024]{2,1,0:T(8,128)(2,1)S(1)}, u32[]{:S(2)}, u32[]{:S(2)}) collective-permute-start(bf16[2,96,1024]{2,1,0:T(8,128)(2,1)S(1)} %pad_maximum_fusion.1.refs_9_), channel_id=1, source_target_pairs={{0,3},{1,0},{2,1},{3,2},{4,7},{5,4},{6,5},{7,6},{8,11},{9,8},{10,9... | collective-permute-start | bytes 1179656 | tf_op jit(solution)/shard_map/ppermute | solution.py:17
  36.3 2.1 %collective-permute-done.3 = bf16[144,512]{1,0:T(8,128)(2,1)S(1)} collective-permute-done((bf16[144,512]{1,0:T(8,128)(2,1)S(1)}, bf16[144,512]{1,0:T(8,128)(2,1)S(1)}, u32[]{:S(2)}, u32[]{:S(2)}) %collective-permute-start.3) | collective-permute-done | bytes 147488 | tf_op jit(solution)/shard_map/ppermute | solution.py:22
  43.5 2.2 %collective-permute-start.8 = (bf16[144,512]{1,0:T(8,128)(2,1)S(1)}, bf16[144,512]{1,0:T(8,128)(2,1)S(1)}, u32[]{:S(2)}, u32[]{:S(2)}) collective-permute-start(bf16[144,512]{1,0:T(8,128)(2,1)S(1)} %select_select_fusion), channel_id=1, source_target_pairs={{0,12},{1,13},{2,14},{3,15},{4,8},{5,9},{6,10},{7,11},{8,4},{9,5},... | collective-permute-start | bytes 442376 | tf_op jit(solution)/shard_map/ppermute | solution.py:22
  45.8 8.8 %collective-permute-done.7 = bf16[144,512]{1,0:T(8,128)(2,1)S(1)} collective-permute-done((bf16[144,512]{1,0:T(8,128)(2,1)S(1)}, bf16[144,512]{1,0:T(8,128)(2,1)S(1)}, u32[]{:S(2)}, u32[]{:S(2)}) %collective-permute-start.7) | collective-permute-done | bytes 147488 | tf_op jit(solution)/shard_map/ppermute | solution.py:22
  54.6 2.4 %collective-permute-start.18 = (bf16[2,96,1024]{2,1,0:T(8,128)(2,1)S(1)}, bf16[2,96,1024]{2,1,0:T(8,128)(2,1)S(1)}, u32[]{:S(2)}, u32[]{:S(2)}) collective-permute-start(bf16[2,96,1024]{2,1,0:T(8,128)(2,1)S(1)} %pad_maximum_fusion.refs_8_), channel_id=1, source_target_pairs={{0,1},{1,2},{2,3},{3,0},{4,5},{5,6},{6,7},{7,4},{8,9},{9,10},{10,1... | collective-permute-start | bytes 1179656 | tf_op jit(solution)/shard_map/ppermute | solution.py:17
  58.3 2.1 %collective-permute-start.12 = (bf16[2,144,512]{2,1,0:T(8,128)(2,1)S(1)}, bf16[2,144,512]{2,1,0:T(8,128)(2,1)S(1)}, u32[]{:S(2)}, u32[]{:S(2)}) collective-permute-start(bf16[2,144,512]{2,1,0:T(8,128)(2,1)S(1)} %pad_maximum_fusion.3.refs_1_), channel_id=1, source_target_pairs={{0,3},{1,0},{2,1},{3,2},{4,7},{5,4},{6,5},{7,6},{8,11},{9,8},{10,9... | collective-permute-start | bytes 884744 | tf_op jit(solution)/shard_map/ppermute | solution.py:17
  61.5 6.8 %collective-permute-done.18.refs_10_ = bf16[2,96,1024]{2,1,0:T(8,128)(2,1)S(1)} collective-permute-done((bf16[2,96,1024]{2,1,0:T(8,128)(2,1)S(1)}, bf16[2,96,1024]{2,1,0:T(8,128)(2,1)S(1)}, u32[]{:S(2)}, u32[]{:S(2)}) %collective-permute-start.18) | collective-permute-done | bytes 393248 | tf_op jit(solution)/shard_map/ppermute | solution.py:17
  70.3 5.0 %collective-permute-done.12.refs_5_ = bf16[2,144,512]{2,1,0:T(8,128)(2,1)S(1)} collective-permute-done((bf16[2,144,512]{2,1,0:T(8,128)(2,1)S(1)}, bf16[2,144,512]{2,1,0:T(8,128)(2,1)S(1)}, u32[]{:S(2)}, u32[]{:S(2)}) %collective-permute-start.12) | collective-permute-done | bytes 294944 | tf_op jit(solution)/shard_map/ppermute | solution.py:17
  75.3 2.5 %collective-permute-start.11 = (bf16[2,144,512]{2,1,0:T(8,128)(2,1)S(1)}, bf16[2,144,512]{2,1,0:T(8,128)(2,1)S(1)}, u32[]{:S(2)}, u32[]{:S(2)}) collective-permute-start(bf16[2,144,512]{2,1,0:T(8,128)(2,1)S(1)} %pad_maximum_fusion.2.refs_0_), channel_id=1, source_target_pairs={{0,3},{1,0},{2,1},{3,2},{4,7},{5,4},{6,5},{7,6},{8,11},{9,8},{10,9... | collective-permute-start | bytes 884744 | tf_op jit(solution)/shard_map/ppermute | solution.py:17
  78.6 2.3 %collective-permute-done.9.refs_2_ = bf16[2,144,512]{2,1,0:T(8,128)(2,1)S(1)} collective-permute-done((bf16[2,144,512]{2,1,0:T(8,128)(2,1)S(1)}, bf16[2,144,512]{2,1,0:T(8,128)(2,1)S(1)}, u32[]{:S(2)}, u32[]{:S(2)}) %collective-permute-start.9) | collective-permute-done | bytes 294944 | tf_op jit(solution)/shard_map/ppermute | solution.py:17
  81.6 6.3 %collective-permute-done.11.refs_4_ = bf16[2,144,512]{2,1,0:T(8,128)(2,1)S(1)} collective-permute-done((bf16[2,144,512]{2,1,0:T(8,128)(2,1)S(1)}, bf16[2,144,512]{2,1,0:T(8,128)(2,1)S(1)}, u32[]{:S(2)}, u32[]{:S(2)}) %collective-permute-start.11) | collective-permute-done | bytes 294944 | tf_op jit(solution)/shard_map/ppermute | solution.py:17
  88.1 3.0 %collective-permute-done.14.refs_7_ = bf16[2,144,512]{2,1,0:T(8,128)(2,1)S(1)} collective-permute-done((bf16[2,144,512]{2,1,0:T(8,128)(2,1)S(1)}, bf16[2,144,512]{2,1,0:T(8,128)(2,1)S(1)}, u32[]{:S(2)}, u32[]{:S(2)}) %collective-permute-start.14) | collective-permute-done | bytes 294944 | tf_op jit(solution)/shard_map/ppermute | solution.py:17
  91.2 2.5 %tile.1.own = bf16[8,256,128]{2,1,0:T(8,128)(2,1)S(1)} custom-call(bf16[2,144,512]{2,1,0:T(8,128)(2,1)S(1)} %pad_maximum_fusion.2.refs_0_, bf16[2,144,512]{2,1,0:T(8,128)(2,1)S(1)} %pad_maximum_fusion.3.refs_1_, bf16[2,144,512]{2,1,0:T(8,128)(2,1)S(1)} %collective-permute-done.9.refs_2_, bf16[2,144,512]{2,1,0:T(8,128)(2,1)S(1)} %collective-permute-done.10.refs_3_, ...), custom_call_target="tpu_custom_call" | custom-call | flops 1500000000 | bytes 8000000 | tf_op jit(solution)/shard_map/tile/pallas_call | solution.py:161
  96.9 5.1 %collective-permute-start.28 = (bf16[2,256,128]{2,1,0:T(8,128)(2,1)S(1)}, bf16[2,256,128]{2,1,0:T(8,128)(2,1)S(1)}, u32[]{:S(2)}, u32[]{:S(2)}) collective-permute-start(bf16[2,256,128]{2,1,0:T(8,128)(2,1)S(1)} %get-tuple-element.31), channel_id=1, source_target_pairs={{0,128},{16,144},{32,160},{48,176},{64,192},{80,208},{96,224},{112... | collective-permute-start | bytes 393224 | tf_op jit(solution)/shard_map/ppermute | solution.py:27
  108.4 2.8 %collective-permute-done.30 = bf16[2,256,128]{2,1,0:T(8,128)(2,1)S(1)} collective-permute-done((bf16[2,256,128]{2,1,0:T(8,128)(2,1)S(1)}, bf16[2,256,128]{2,1,0:T(8,128)(2,1)S(1)}, u32[]{:S(2)}, u32[]{:S(2)}) %collective-permute-start.30) | collective-permute-done | bytes 131104 | tf_op jit(solution)/shard_map/ppermute | solution.py:27
  111.2 4.2 %collective-permute-start.31 = (bf16[2,256,128]{2,1,0:T(8,128)(2,1)S(1)}, bf16[2,256,128]{2,1,0:T(8,128)(2,1)S(1)}, u32[]{:S(2)}, u32[]{:S(2)}) collective-permute-start(bf16[2,256,128]{2,1,0:T(8,128)(2,1)S(1)} %add_convert_fusion.1), channel_id=1, source_target_pairs={{0,32},{16,48},{32,0},{48,16},{64,96},{80,112},{96,64},{112,80},{1... | collective-permute-start | bytes 393224 | tf_op jit(solution)/shard_map/ppermute | solution.py:31
  115.4 4.9 %collective-permute-done.31 = bf16[2,256,128]{2,1,0:T(8,128)(2,1)S(1)} collective-permute-done((bf16[2,256,128]{2,1,0:T(8,128)(2,1)S(1)}, bf16[2,256,128]{2,1,0:T(8,128)(2,1)S(1)}, u32[]{:S(2)}, u32[]{:S(2)}) %collective-permute-start.31) | collective-permute-done | bytes 131104 | tf_op jit(solution)/shard_map/ppermute | solution.py:31
  120.9 2.4 %collective-permute-start.32 = (bf16[256,256]{1,0:T(8,128)(2,1)S(1)}, bf16[256,256]{1,0:T(8,128)(2,1)S(1)}, u32[]{:S(2)}, u32[]{:S(2)}) collective-permute-start(bf16[256,256]{1,0:T(8,128)(2,1)S(1)} %convolution_convert_fusion), channel_id=1, source_target_pairs={{0,2},{1,3},{2,0},{3,1},{4,6},{5,7},{6,4},{7,5},{8,10},{9,11},{10,... | collective-permute-start | bytes 393224 | tf_op jit(solution)/shard_map/ppermute | solution.py:17
  124.2 2.3 %collective-permute-start.34 = (bf16[256,256]{1,0:T(8,128)(2,1)S(1)}, bf16[256,256]{1,0:T(8,128)(2,1)S(1)}, u32[]{:S(2)}, u32[]{:S(2)}) collective-permute-start(bf16[256,256]{1,0:T(8,128)(2,1)S(1)} %convolution_convert_fusion), channel_id=1, source_target_pairs={{0,3},{1,0},{2,1},{3,2},{4,7},{5,4},{6,5},{7,6},{8,11},{9,8},{10,9... | collective-permute-start | bytes 393224 | tf_op jit(solution)/shard_map/ppermute | solution.py:17
  129.5 4.8 %collective-permute-start.35 = (bf16[256,256]{1,0:T(8,128)(2,1)S(1)}, bf16[256,256]{1,0:T(8,128)(2,1)S(1)}, u32[]{:S(2)}, u32[]{:S(2)}) collective-permute-start(bf16[256,256]{1,0:T(8,128)(2,1)S(1)} %add_convert_fusion), channel_id=1, source_target_pairs={{0,4},{1,5},{2,6},{3,7},{4,0},{5,1},{6,2},{7,3},{8,12},{9,13},{10,... | collective-permute-start | bytes 393224 | tf_op jit(solution)/shard_map/ppermute | solution.py:22
  138.5 8.1 %collective-permute-done.36 = bf16[256,256]{1,0:T(8,128)(2,1)S(1)} collective-permute-done((bf16[256,256]{1,0:T(8,128)(2,1)S(1)}, bf16[256,256]{1,0:T(8,128)(2,1)S(1)}, u32[]{:S(2)}, u32[]{:S(2)}) %collective-permute-start.36) | collective-permute-done | bytes 131104 | tf_op jit(solution)/shard_map/ppermute | solution.py:22
  (93 shorter events, 49.9 us)
Async XLA Ops:
  0.7 33.2 %collective-permute-start.16 = (bf16[96,1024]{1,0:T(8,128)(2,1)}, bf16[96,1024]{1,0:T(8,128)(2,1)S(1)}, u32[]{:S(2)}, u32[]{:S(2)}) collective-permute-start(bf16[96,1024]{1,0:T(8,128)(2,1)} %bitcast.32), channel_id=1, source_target_pairs={{0,8},{1,9},{2,10},{3,11},{4,12},{5,13},{6,14},{7,15},{8,0},{9,1},... | collective-permute-start | bytes 589832 | tf_op jit(solution)/shard_map/ppermute | solution.py:22
  4.0 30.0 %collective-permute-start.17 = (bf16[96,1024]{1,0:T(8,128)(2,1)}, bf16[96,1024]{1,0:T(8,128)(2,1)S(1)}, u32[]{:S(2)}, u32[]{:S(2)}) collective-permute-start(bf16[96,1024]{1,0:T(8,128)(2,1)} %bitcast.33), channel_id=1, source_target_pairs={{0,12},{1,13},{2,14},{3,15},{4,8},{5,9},{6,10},{7,11},{8,4},{9,5},... | collective-permute-start | bytes 589832 | tf_op jit(solution)/shard_map/ppermute | solution.py:22
  10.0 16.8 %collective-permute-start.1 = (bf16[4,80,512]{2,1,0:T(8,128)(2,1)S(1)}, bf16[4,80,512]{2,1,0:T(8,128)(2,1)S(1)}, u32[]{:S(2)}, u32[]{:S(2)}) collective-permute-start(bf16[4,80,512]{2,1,0:T(8,128)(2,1)S(1)} %get-tuple-element.20), channel_id=1, source_target_pairs={{0,2},{1,3},{2,0},{3,1},{4,6},{5,7},{6,4},{7,5},{8,10},{9,11},{10,... | collective-permute-start | bytes 983048 | tf_op jit(solution)/shard_map/ppermute | solution.py:17
  12.5 14.3 %collective-permute-start.2 = (bf16[4,80,512]{2,1,0:T(8,128)(2,1)S(1)}, bf16[4,80,512]{2,1,0:T(8,128)(2,1)S(1)}, u32[]{:S(2)}, u32[]{:S(2)}) collective-permute-start(bf16[4,80,512]{2,1,0:T(8,128)(2,1)S(1)} %get-tuple-element.21), channel_id=1, source_target_pairs={{0,3},{1,0},{2,1},{3,2},{4,7},{5,4},{6,5},{7,6},{8,11},{9,8},{10,9... | collective-permute-start | bytes 983048 | tf_op jit(solution)/shard_map/ppermute | solution.py:17
  29.0 11.2 %collective-permute-start.4 = (bf16[144,512]{1,0:T(8,128)(2,1)S(1)}, bf16[144,512]{1,0:T(8,128)(2,1)S(1)}, u32[]{:S(2)}, u32[]{:S(2)}) collective-permute-start(bf16[144,512]{1,0:T(8,128)(2,1)S(1)} %get-tuple-element.23), channel_id=1, source_target_pairs={{0,4},{1,5},{2,6},{3,7},{4,0},{5,1},{6,2},{7,3},{8,12},{9,13},{10,... | collective-permute-start | bytes 442376 | tf_op jit(solution)/shard_map/ppermute | solution.py:22
  30.0 11.5 %collective-permute-start.5 = (bf16[144,512]{1,0:T(8,128)(2,1)S(1)}, bf16[144,512]{1,0:T(8,128)(2,1)S(1)}, u32[]{:S(2)}, u32[]{:S(2)}) collective-permute-start(bf16[144,512]{1,0:T(8,128)(2,1)S(1)} %get-tuple-element.25), channel_id=1, source_target_pairs={{0,12},{1,13},{2,14},{3,15},{4,8},{5,9},{6,10},{7,11},{8,4},{9,5},... | collective-permute-start | bytes 442376 | tf_op jit(solution)/shard_map/ppermute | solution.py:22
  33.9 11.8 %collective-permute-start.15 = (bf16[96,1024]{1,0:T(8,128)(2,1)S(1)}, bf16[96,1024]{1,0:T(8,128)(2,1)S(1)}, u32[]{:S(2)}, u32[]{:S(2)}) collective-permute-start(bf16[96,1024]{1,0:T(8,128)(2,1)S(1)} %bitcast.34), channel_id=1, source_target_pairs={{0,4},{1,5},{2,6},{3,7},{4,0},{5,1},{6,2},{7,3},{8,12},{9,13},{10,... | collective-permute-start | bytes 589832 | tf_op jit(solution)/shard_map/ppermute | solution.py:22
  34.1 26.4 %collective-permute-start.21 = (bf16[2,96,1024]{2,1,0:T(8,128)(2,1)S(1)}, bf16[2,96,1024]{2,1,0:T(8,128)(2,1)S(1)}, u32[]{:S(2)}, u32[]{:S(2)}) collective-permute-start(bf16[2,96,1024]{2,1,0:T(8,128)(2,1)S(1)} %pad_maximum_fusion.1.refs_9_), channel_id=1, source_target_pairs={{0,3},{1,0},{2,1},{3,2},{4,7},{5,4},{6,5},{7,6},{8,11},{9,8},{10,9... | collective-permute-start | bytes 1179656 | tf_op jit(solution)/shard_map/ppermute | solution.py:17
  38.4 22.4 %collective-permute-start.19 = (bf16[2,96,1024]{2,1,0:T(8,128)(2,1)S(1)}, bf16[2,96,1024]{2,1,0:T(8,128)(2,1)S(1)}, u32[]{:S(2)}, u32[]{:S(2)}) collective-permute-start(bf16[2,96,1024]{2,1,0:T(8,128)(2,1)S(1)} %pad_maximum_fusion.1.refs_9_), channel_id=1, source_target_pairs={{0,1},{1,2},{2,3},{3,0},{4,5},{5,6},{6,7},{7,4},{8,9},{9,10},{10,1... | collective-permute-start | bytes 1179656 | tf_op jit(solution)/shard_map/ppermute | solution.py:17
  41.7 12.9 %collective-permute-start.7 = (bf16[144,512]{1,0:T(8,128)(2,1)S(1)}, bf16[144,512]{1,0:T(8,128)(2,1)S(1)}, u32[]{:S(2)}, u32[]{:S(2)}) collective-permute-start(bf16[144,512]{1,0:T(8,128)(2,1)S(1)} %select_select_fusion), channel_id=1, source_target_pairs={{0,8},{1,9},{2,10},{3,11},{4,12},{5,13},{6,14},{7,15},{8,0},{9,1},... | collective-permute-start | bytes 442376 | tf_op jit(solution)/shard_map/ppermute | solution.py:22
  43.5 13.5 %collective-permute-start.8 = (bf16[144,512]{1,0:T(8,128)(2,1)S(1)}, bf16[144,512]{1,0:T(8,128)(2,1)S(1)}, u32[]{:S(2)}, u32[]{:S(2)}) collective-permute-start(bf16[144,512]{1,0:T(8,128)(2,1)S(1)} %select_select_fusion), channel_id=1, source_target_pairs={{0,12},{1,13},{2,14},{3,15},{4,8},{5,9},{6,10},{7,11},{8,4},{9,5},... | collective-permute-start | bytes 442376 | tf_op jit(solution)/shard_map/ppermute | solution.py:22
  45.7 12.6 %collective-permute-start.6 = (bf16[144,512]{1,0:T(8,128)(2,1)S(1)}, bf16[144,512]{1,0:T(8,128)(2,1)S(1)}, u32[]{:S(2)}, u32[]{:S(2)}) collective-permute-start(bf16[144,512]{1,0:T(8,128)(2,1)S(1)} %select_select_fusion), channel_id=1, source_target_pairs={{0,4},{1,5},{2,6},{3,7},{4,0},{5,1},{6,2},{7,3},{8,12},{9,13},{10,... | collective-permute-start | bytes 442376 | tf_op jit(solution)/shard_map/ppermute | solution.py:22
  54.6 13.7 %collective-permute-start.18 = (bf16[2,96,1024]{2,1,0:T(8,128)(2,1)S(1)}, bf16[2,96,1024]{2,1,0:T(8,128)(2,1)S(1)}, u32[]{:S(2)}, u32[]{:S(2)}) collective-permute-start(bf16[2,96,1024]{2,1,0:T(8,128)(2,1)S(1)} %pad_maximum_fusion.refs_8_), channel_id=1, source_target_pairs={{0,1},{1,2},{2,3},{3,0},{4,5},{5,6},{6,7},{7,4},{8,9},{9,10},{10,1... | collective-permute-start | bytes 1179656 | tf_op jit(solution)/shard_map/ppermute | solution.py:17
  57.0 13.3 %collective-permute-start.20 = (bf16[2,96,1024]{2,1,0:T(8,128)(2,1)S(1)}, bf16[2,96,1024]{2,1,0:T(8,128)(2,1)S(1)}, u32[]{:S(2)}, u32[]{:S(2)}) collective-permute-start(bf16[2,96,1024]{2,1,0:T(8,128)(2,1)S(1)} %pad_maximum_fusion.refs_8_), channel_id=1, source_target_pairs={{0,3},{1,0},{2,1},{3,2},{4,7},{5,4},{6,5},{7,6},{8,11},{9,8},{10,9... | collective-permute-start | bytes 1179656 | tf_op jit(solution)/shard_map/ppermute | solution.py:17
  58.3 17.0 %collective-permute-start.12 = (bf16[2,144,512]{2,1,0:T(8,128)(2,1)S(1)}, bf16[2,144,512]{2,1,0:T(8,128)(2,1)S(1)}, u32[]{:S(2)}, u32[]{:S(2)}) collective-permute-start(bf16[2,144,512]{2,1,0:T(8,128)(2,1)S(1)} %pad_maximum_fusion.3.refs_1_), channel_id=1, source_target_pairs={{0,3},{1,0},{2,1},{3,2},{4,7},{5,4},{6,5},{7,6},{8,11},{9,8},{10,9... | collective-permute-start | bytes 884744 | tf_op jit(solution)/shard_map/ppermute | solution.py:17
  60.5 17.3 %collective-permute-start.10 = (bf16[2,144,512]{2,1,0:T(8,128)(2,1)S(1)}, bf16[2,144,512]{2,1,0:T(8,128)(2,1)S(1)}, u32[]{:S(2)}, u32[]{:S(2)}) collective-permute-start(bf16[2,144,512]{2,1,0:T(8,128)(2,1)S(1)} %pad_maximum_fusion.3.refs_1_), channel_id=1, source_target_pairs={{0,1},{1,2},{2,3},{3,0},{4,5},{5,6},{6,7},{7,4},{8,9},{9,10},{10,1... | collective-permute-start | bytes 884744 | tf_op jit(solution)/shard_map/ppermute | solution.py:17
  60.8 20.1 %collective-permute-start.9 = (bf16[2,144,512]{2,1,0:T(8,128)(2,1)S(1)}, bf16[2,144,512]{2,1,0:T(8,128)(2,1)S(1)}, u32[]{:S(2)}, u32[]{:S(2)}) collective-permute-start(bf16[2,144,512]{2,1,0:T(8,128)(2,1)S(1)} %pad_maximum_fusion.2.refs_0_), channel_id=1, source_target_pairs={{0,1},{1,2},{2,3},{3,0},{4,5},{5,6},{6,7},{7,4},{8,9},{9,10},{10,1... | collective-permute-start | bytes 884744 | tf_op jit(solution)/shard_map/ppermute | solution.py:17
  68.2 19.6 %collective-permute-start.23 = (bf16[2,96,1024]{2,1,0:T(8,128)(2,1)S(1)}, bf16[2,96,1024]{2,1,0:T(8,128)(2,1)S(1)}, u32[]{:S(2)}, u32[]{:S(2)}) collective-permute-start(bf16[2,96,1024]{2,1,0:T(8,128)(2,1)S(1)} %collective-permute-done.21.refs_13_), channel_id=1, source_target_pairs={{0,3},{1,0},{2,1},{3,2},{4,7},{5,4},{6,5},{7,6},{8,11},{9,8},{10,9... | collective-permute-start | bytes 1179656 | tf_op jit(solution)/shard_map/ppermute | solution.py:17
  70.3 17.8 %collective-permute-start.22 = (bf16[2,96,1024]{2,1,0:T(8,128)(2,1)S(1)}, bf16[2,96,1024]{2,1,0:T(8,128)(2,1)S(1)}, u32[]{:S(2)}, u32[]{:S(2)}) collective-permute-start(bf16[2,96,1024]{2,1,0:T(8,128)(2,1)S(1)} %collective-permute-done.18.refs_10_), channel_id=1, source_target_pairs={{0,1},{1,2},{2,3},{3,0},{4,5},{5,6},{6,7},{7,4},{8,9},{9,10},{10,1... | collective-permute-start | bytes 1179656 | tf_op jit(solution)/shard_map/ppermute | solution.py:17
  75.3 12.6 %collective-permute-start.11 = (bf16[2,144,512]{2,1,0:T(8,128)(2,1)S(1)}, bf16[2,144,512]{2,1,0:T(8,128)(2,1)S(1)}, u32[]{:S(2)}, u32[]{:S(2)}) collective-permute-start(bf16[2,144,512]{2,1,0:T(8,128)(2,1)S(1)} %pad_maximum_fusion.2.refs_0_), channel_id=1, source_target_pairs={{0,3},{1,0},{2,1},{3,2},{4,7},{5,4},{6,5},{7,6},{8,11},{9,8},{10,9... | collective-permute-start | bytes 884744 | tf_op jit(solution)/shard_map/ppermute | solution.py:17
  77.8 13.2 %collective-permute-start.14 = (bf16[2,144,512]{2,1,0:T(8,128)(2,1)S(1)}, bf16[2,144,512]{2,1,0:T(8,128)(2,1)S(1)}, u32[]{:S(2)}, u32[]{:S(2)}) collective-permute-start(bf16[2,144,512]{2,1,0:T(8,128)(2,1)S(1)} %collective-permute-done.12.refs_5_), channel_id=1, source_target_pairs={{0,3},{1,0},{2,1},{3,2},{4,7},{5,4},{6,5},{7,6},{8,11},{9,8},{10,9... | collective-permute-start | bytes 884744 | tf_op jit(solution)/shard_map/ppermute | solution.py:17
  104.0 11.4 %collective-permute-start.25 = (bf16[2,256,128]{2,1,0:T(8,128)(2,1)S(1)}, bf16[2,256,128]{2,1,0:T(8,128)(2,1)S(1)}, u32[]{:S(2)}, u32[]{:S(2)}) collective-permute-start(bf16[2,256,128]{2,1,0:T(8,128)(2,1)S(1)} %get-tuple-element.27), channel_id=1, source_target_pairs={{0,128},{16,144},{32,160},{48,176},{64,192},{80,208},{96,224},{112... | collective-permute-start | bytes 393224 | tf_op jit(solution)/shard_map/ppermute | solution.py:27
  104.1 11.3 %collective-permute-start.26 = (bf16[2,256,128]{2,1,0:T(8,128)(2,1)S(1)}, bf16[2,256,128]{2,1,0:T(8,128)(2,1)S(1)}, u32[]{:S(2)}, u32[]{:S(2)}) collective-permute-start(bf16[2,256,128]{2,1,0:T(8,128)(2,1)S(1)} %get-tuple-element.28), channel_id=1, source_target_pairs={{0,64},{16,80},{32,96},{48,112},{64,128},{80,144},{96,160},{112,17... | collective-permute-start | bytes 393224 | tf_op jit(solution)/shard_map/ppermute | solution.py:27
  134.3 12.3 %collective-permute-start.36 = (bf16[256,256]{1,0:T(8,128)(2,1)S(1)}, bf16[256,256]{1,0:T(8,128)(2,1)S(1)}, u32[]{:S(2)}, u32[]{:S(2)}) collective-permute-start(bf16[256,256]{1,0:T(8,128)(2,1)S(1)} %add_convert_fusion), channel_id=1, source_target_pairs={{0,8},{1,9},{2,10},{3,11},{4,12},{5,13},{6,14},{7,15},{8,0},{9,1},... | collective-permute-start | bytes 393224 | tf_op jit(solution)/shard_map/ppermute | solution.py:22
  (23 other events, 417.5 us)

commit v2 on v1

--- a/solution.py
+++ b/solution.py
@@ -31,7 +31,24 @@
     return lax.ppermute(value, "grp", [(g, g ^ bits) for g in range(16)])
 
 
-def gather_blocks(block):
+def pass_kernel(first, second, out_first, out_second):
+    out_first[...] = first[...]
+    out_second[...] = second[...]
+
+
+def pass_on(first, second):
+    return pl.pallas_call(
+        pass_kernel,
+        out_shape=[jax.ShapeDtypeStruct(value.shape, value.dtype) for value in (first, second)],
+        in_specs=[VMEM] * 2,
+        out_specs=[VMEM] * 2,
+        cost_estimate=pl.CostEstimate(flops=1_000_000, bytes_accessed=1_600_000, transcendentals=0),
+        compiler_params=pltpu.CompilerParams(vmem_limit_bytes=4 << 20),
+        name="pass_on",
+    )(first, second)
+
+
+def gather_blocks(block, name):
     near = [hop_z(block, bits) for bits in (1, 2, 3)]
     low = jnp.stack([block, near[0]])
     high = jnp.stack([near[1], near[2]])
@@ -39,8 +56,12 @@
     high_right = hop_x(high, -1)
     high_left = hop_x(high, 1)
     low_right = hop_x(low, -1)
-    low_far = hop_x(low_left, 1)
-    high_far = hop_x(high_right, -1)
+    if name == "border":
+        sent_left, sent_right = pass_on(low_left, high_right)
+    else:
+        sent_left, sent_right = low_left, high_right
+    low_far = hop_x(sent_left, 1)
+    high_far = hop_x(sent_right, -1)
     return [low, high, low_left, high_left, low_right, high_right, low_far, high_far]
 
 
@@ -55,7 +76,7 @@
 
 
 def pack_kernel(owners, slot, *refs):
-    outs, (held, sem) = refs[:4], refs[4:]
+    outs, held = refs[:4], refs[4]
     group, dev = lax.axis_index("grp"), lax.axis_index("dev")
     row = lax.broadcasted_iota(jnp.int32, (256, 256), 0)
     col = lax.broadcasted_iota(jnp.int32, (256, 256), 1)
@@ -64,13 +85,9 @@
         @pl.when(owners[step, group] == dev)
         def _():
             top = 512 * step
-            load = pltpu.make_async_copy(
-                slot.at[0, pl.ds(top, 1536 - top)], held.at[pl.ds(top, 1536 - top)], sem
-            )
-            load.start()
-            load.wait()
-            first = held[top : top + 256, :256].astype(F32)
-            second = held[top + 256 : top + 512, 256:].astype(F32).T
+            held[top + 256 :] = slot[0, top + 256 :]
+            first = slot[0, top : top + 256, :256].astype(F32)
+            second = slot[0, top + 256 : top + 512, 256:].astype(F32).T
             held[top + 256 : top + 512, 256:] = jnp.where(row > col, first, second).astype(BF16)
             height = HEIGHTS[step]
             for dx in range(4):
@@ -84,9 +101,9 @@
     return pl.pallas_call(
         pack_kernel,
         out_shape=[jax.ShapeDtypeStruct((4, HEIGHTS[0], 512), BF16)] * 4,
-        in_specs=[SMEM, pl.BlockSpec(memory_space=pltpu.HBM)],
+        in_specs=[SMEM, VMEM],
         out_specs=[VMEM] * 4,
-        scratch_shapes=[pltpu.VMEM((1536, 512), BF16), pltpu.SemaphoreType.DMA],
+        scratch_shapes=[pltpu.VMEM((1536, 512), BF16)],
         cost_estimate=pl.CostEstimate(flops=1_000_000, bytes_accessed=2_800_000, transcendentals=0),
         compiler_params=pltpu.CompilerParams(vmem_limit_bytes=16 << 20),
         name="pack",
@@ -117,6 +134,31 @@
         compiler_params=pltpu.CompilerParams(vmem_limit_bytes=8 << 20),
         name="pick",
     )(owners, *chunks)
+
+
+def pick_z_kernel(owners, *refs):
+    pieces, out = refs[:4], refs[4]
+    group, dev = lax.axis_index("grp"), lax.axis_index("dev")
+    for step in range(3):
+        first, rows = OFFSETS[step], HEIGHTS[step]
+        distance = (owners[step, group] ^ dev) >> 2
+        for bits in range(4):
+
+            @pl.when(distance == bits)
+            def _():
+                out[first : first + rows] = pieces[bits][first : first + rows]
+
+
+def pick_z(owners, pieces):
+    return pl.pallas_call(
+        pick_z_kernel,
+        out_shape=jax.ShapeDtypeStruct((PIECE, 512), BF16),
+        in_specs=[SMEM] + [VMEM] * 4,
+        out_specs=VMEM,
+        cost_estimate=pl.CostEstimate(flops=1_000_000, bytes_accessed=300_000, transcendentals=0),
+        compiler_params=pltpu.CompilerParams(vmem_limit_bytes=4 << 20),
+        name="pick_z",
+    )(owners, *pieces)
 
 
 def tile_kernel(*refs):
@@ -215,24 +257,15 @@
 
 
 def step(panels, panel_owner, interface_cols, border, block_rows, pattern, block_x):
-    group = lax.axis_index("grp")
-    dev = lax.axis_index("dev")
-
-    strips = gather_blocks(border.T)
+    strips = gather_blocks(border.T, "border")
 
     chunks = pack(panel_owner.T, panels)
     far = hop_x(chunks[2], 2)
     chunks = [chunks[0], hop_x(chunks[1], 1), far, hop_x(chunks[3], 3)]
     pieces = pick(panel_owner.T, chunks)
     pieces = [pieces[0]] + [hop_z(pieces[bits], bits) for bits in (1, 2, 3)]
-    owners = lax.dynamic_slice_in_dim(panel_owner, group, 1, 0)[0]
-    near = owners // 4 ^ dev // 4
-    row = lax.broadcasted_iota(jnp.int32, (PIECE, 1), 0)
-    from_z = jnp.where(row < OFFSETS[1], near[0], jnp.where(row < OFFSETS[2], near[1], near[2]))
-    piece = pieces[3]
-    for bits in (0, 1, 2):
-        piece = jnp.where(from_z == bits, pieces[bits], piece)
-    tile = make_tile(gather_blocks(piece), strips, interface_cols)
+    piece = pick_z(panel_owner.T, pieces)
+    tile = make_tile(gather_blocks(piece, "panel"), strips, interface_cols)
 
     placed = place(block_rows.T, tile, swap_grp(tile, 1))
     other = add_y(placed[4:])

time: 148 us -> 146 us (0.986)
  other arithmetic: 5.16 us -> 1.16 us
  waiting for transfers between devices: 69 us -> 72.6 us
  starting transfers between devices: 64 us -> 62.2 us
    ppermute x12, waiting for transfers between devices: 21.8 us -> 27.6 us  [hop_z(): return lax.ppermute(value, 'dev', perm)]
    eq x2 -> x0, other arithmetic: 3.86 us -> none  [step(): piece = jnp.where(from_z == bits, pieces[bits], piece)]
    ppermute x12, starting transfers between devices: 20.8 us -> 24.3 us  [hop_z(): return lax.ppermute(value, 'dev', perm)]
    ppermute x18, starting transfers between devices: 28.3 us -> 24.9 us  [hop_x(): return lax.ppermute(value, 'dev', perm)]
    ppermute x6, starting transfers between devices: 10.6 us -> 8.43 us  [hop_y(): return lax.ppermute(value, 'grp', perm)]
  transfers between devices with their start and end apart: 38 -> 38, of which waited for: 21 -> 19; matrix products, arithmetic and copies ran while one was open for 3% -> 0% of each run, Pallas kernels for 1% -> 1%
where the time goes in v2:
time: 146 us; the launch traced here: 145 us
  waiting for transfers between devices  72.6 us (50%)
  starting transfers between devices  62.2 us (43%)
  Pallas kernels  5.63 us (4%)
  local copies, waits for them, and re-layouts  2.42 us (2%)
    ppermute x18, waiting for transfers between devices, hop_x(): return lax.ppermute(value, 'dev', perm)  35.9 us
    ppermute x12, waiting for transfers between devices, hop_z(): return lax.ppermute(value, 'dev', perm)  27.6 us
    ppermute x18, starting transfers between devices, hop_x(): return lax.ppermute(value, 'dev', perm)  24.9 us
    ppermute x12, starting transfers between devices, hop_z(): return lax.ppermute(value, 'dev', perm)  24.3 us
    ppermute x6, starting transfers between devices, hop_y(): return lax.ppermute(value, 'grp', perm)  8.43 us
    ppermute x2, waiting for transfers between devices, swap_grp(): return lax.ppermute(value, 'grp', [(g, g ^ bits) for g in range(16)])  6.39 us
    ppermute x2, starting transfers between devices, swap_grp(): return lax.ppermute(value, 'grp', [(g, g ^ bits) for g in range(16)])  4.6 us
  transfers between devices with their start and end apart: 38, of which 19 were waited for; matrix products, arithmetic and copies ran while one was open for 0% of the time, Pallas kernels for 1%

profile of v2, /device:TPU:8, one launch (start us, length us, event | category | flops | bytes accessed | tf_op | source)
XLA Modules:
  0.0 145.1 jit_solution(13468049218626341681)
XLA Ops:
  5.1 2.6 %collective-permute-start.1 = (bf16[4,80,512]{2,1,0:T(8,128)(2,1)S(1)}, bf16[4,80,512]{2,1,0:T(8,128)(2,1)S(1)}, u32[]{:S(2)}, u32[]{:S(2)}) collective-permute-start(bf16[4,80,512]{2,1,0:T(8,128)(2,1)S(1)} %get-tuple-element.22), channel_id=1, source_target_pairs={{0,2},{1,3},{2,0},{3,1},{4,6},{5,7},{6,4},{7,5},{8,10},{9,11},{10,... | collective-permute-start | bytes 983048 | tf_op jit(solution)/shard_map/ppermute | solution.py:17
  9.1 4.6 %collective-permute-start.17 = (bf16[96,1024]{1,0:T(8,128)(2,1)S(1)}, bf16[96,1024]{1,0:T(8,128)(2,1)S(1)}, u32[]{:S(2)}, u32[]{:S(2)}) collective-permute-start(bf16[96,1024]{1,0:T(8,128)(2,1)S(1)} %bitcast.30), channel_id=1, source_target_pairs={{0,12},{1,13},{2,14},{3,15},{4,8},{5,9},{6,10},{7,11},{8,4},{9,5},... | collective-permute-start | bytes 589832 | tf_op jit(solution)/shard_map/ppermute | solution.py:22
  16.0 6.2 %collective-permute-done.1.refs_2_ = bf16[4,80,512]{2,1,0:T(8,128)(2,1)S(1)} collective-permute-done((bf16[4,80,512]{2,1,0:T(8,128)(2,1)S(1)}, bf16[4,80,512]{2,1,0:T(8,128)(2,1)S(1)}, u32[]{:S(2)}, u32[]{:S(2)}) %collective-permute-start.1) | collective-permute-done | bytes 327712 | tf_op jit(solution)/shard_map/ppermute | solution.py:17
  25.0 3.1 %collective-permute-start.4 = (bf16[144,512]{1,0:T(8,128)(2,1)S(1)}, bf16[144,512]{1,0:T(8,128)(2,1)S(1)}, u32[]{:S(2)}, u32[]{:S(2)}) collective-permute-start(bf16[144,512]{1,0:T(8,128)(2,1)S(1)} %get-tuple-element.26), channel_id=1, source_target_pairs={{0,8},{1,9},{2,10},{3,11},{4,12},{5,13},{6,14},{7,15},{8,0},{9,1},... | collective-permute-start | bytes 442376 | tf_op jit(solution)/shard_map/ppermute | solution.py:22
  28.1 8.8 %collective-permute-done.16 = bf16[96,1024]{1,0:T(8,128)(2,1)S(1)} collective-permute-done((bf16[96,1024]{1,0:T(8,128)(2,1)S(1)}, bf16[96,1024]{1,0:T(8,128)(2,1)S(1)}, u32[]{:S(2)}, u32[]{:S(2)}) %collective-permute-start.16) | collective-permute-done | bytes 196640 | tf_op jit(solution)/shard_map/ppermute | solution.py:22
  40.7 3.5 %collective-permute-start.7 = (bf16[144,512]{1,0:T(8,128)(2,1)S(1)}, bf16[144,512]{1,0:T(8,128)(2,1)S(1)}, u32[]{:S(2)}, u32[]{:S(2)}) collective-permute-start(bf16[144,512]{1,0:T(8,128)(2,1)S(1)} %pick_z.1), channel_id=1, source_target_pairs={{0,8},{1,9},{2,10},{3,11},{4,12},{5,13},{6,14},{7,15},{8,0},{9,1},... | collective-permute-start | bytes 442376 | tf_op jit(solution)/shard_map/ppermute | solution.py:22
  45.4 8.8 %collective-permute-done.7 = bf16[144,512]{1,0:T(8,128)(2,1)S(1)} collective-permute-done((bf16[144,512]{1,0:T(8,128)(2,1)S(1)}, bf16[144,512]{1,0:T(8,128)(2,1)S(1)}, u32[]{:S(2)}, u32[]{:S(2)}) %collective-permute-start.7) | collective-permute-done | bytes 147488 | tf_op jit(solution)/shard_map/ppermute | solution.py:22
  60.1 7.2 %collective-permute-done.19.refs_11_ = bf16[2,96,1024]{2,1,0:T(8,128)(2,1)S(1)} collective-permute-done((bf16[2,96,1024]{2,1,0:T(8,128)(2,1)S(1)}, bf16[2,96,1024]{2,1,0:T(8,128)(2,1)S(1)}, u32[]{:S(2)}, u32[]{:S(2)}) %collective-permute-start.19) | collective-permute-done | bytes 393248 | tf_op jit(solution)/shard_map/ppermute | solution.py:17
  67.3 3.4 %collective-permute-start.23 = (bf16[2,96,1024]{2,1,0:T(8,128)(2,1)S(1)}, bf16[2,96,1024]{2,1,0:T(8,128)(2,1)S(1)}, u32[]{:S(2)}, u32[]{:S(2)}) collective-permute-start(bf16[2,96,1024]{2,1,0:T(8,128)(2,1)S(1)} %get-tuple-element.29), channel_id=1, source_target_pairs={{0,3},{1,0},{2,1},{3,2},{4,7},{5,4},{6,5},{7,6},{8,11},{9,8},{10,9... | collective-permute-start | bytes 1179656 | tf_op jit(solution)/shard_map/ppermute | solution.py:17
  70.7 2.9 %collective-permute-done.12.refs_5_ = bf16[2,144,512]{2,1,0:T(8,128)(2,1)S(1)} collective-permute-done((bf16[2,144,512]{2,1,0:T(8,128)(2,1)S(1)}, bf16[2,144,512]{2,1,0:T(8,128)(2,1)S(1)}, u32[]{:S(2)}, u32[]{:S(2)}) %collective-permute-start.12) | collective-permute-done | bytes 294944 | tf_op jit(solution)/shard_map/ppermute | solution.py:17
  73.6 3.4 %collective-permute-start.11 = (bf16[2,144,512]{2,1,0:T(8,128)(2,1)S(1)}, bf16[2,144,512]{2,1,0:T(8,128)(2,1)S(1)}, u32[]{:S(2)}, u32[]{:S(2)}) collective-permute-start(bf16[2,144,512]{2,1,0:T(8,128)(2,1)S(1)} %pad_maximum_fusion.2.refs_0_), channel_id=1, source_target_pairs={{0,3},{1,0},{2,1},{3,2},{4,7},{5,4},{6,5},{7,6},{8,11},{9,8},{10,9... | collective-permute-start | bytes 884744 | tf_op jit(solution)/shard_map/ppermute | solution.py:17
  77.0 2.9 %collective-permute-done.9.refs_2_ = bf16[2,144,512]{2,1,0:T(8,128)(2,1)S(1)} collective-permute-done((bf16[2,144,512]{2,1,0:T(8,128)(2,1)S(1)}, bf16[2,144,512]{2,1,0:T(8,128)(2,1)S(1)}, u32[]{:S(2)}, u32[]{:S(2)}) %collective-permute-start.9) | collective-permute-done | bytes 294944 | tf_op jit(solution)/shard_map/ppermute | solution.py:17
  80.0 8.4 %collective-permute-done.11.refs_4_ = bf16[2,144,512]{2,1,0:T(8,128)(2,1)S(1)} collective-permute-done((bf16[2,144,512]{2,1,0:T(8,128)(2,1)S(1)}, bf16[2,144,512]{2,1,0:T(8,128)(2,1)S(1)}, u32[]{:S(2)}, u32[]{:S(2)}) %collective-permute-start.11) | collective-permute-done | bytes 294944 | tf_op jit(solution)/shard_map/ppermute | solution.py:17
  88.3 3.8 %collective-permute-done.14.refs_7_ = bf16[2,144,512]{2,1,0:T(8,128)(2,1)S(1)} collective-permute-done((bf16[2,144,512]{2,1,0:T(8,128)(2,1)S(1)}, bf16[2,144,512]{2,1,0:T(8,128)(2,1)S(1)}, u32[]{:S(2)}, u32[]{:S(2)}) %collective-permute-start.14) | collective-permute-done | bytes 294944 | tf_op jit(solution)/shard_map/ppermute | solution.py:17
  92.2 2.5 %tile.1.own = bf16[8,256,128]{2,1,0:T(8,128)(2,1)S(1)} custom-call(bf16[2,144,512]{2,1,0:T(8,128)(2,1)S(1)} %pad_maximum_fusion.2.refs_0_, bf16[2,144,512]{2,1,0:T(8,128)(2,1)S(1)} %pad_maximum_fusion.3.refs_1_, bf16[2,144,512]{2,1,0:T(8,128)(2,1)S(1)} %collective-permute-done.9.refs_2_, bf16[2,144,512]{2,1,0:T(8,128)(2,1)S(1)} %collective-permute-done.10.refs_3_, ...), custom_call_target="tpu_custom_call" | custom-call | flops 1500000000 | bytes 8000000 | tf_op jit(solution)/shard_map/tile/pallas_call | solution.py:203
  97.9 2.3 %collective-permute-start.28 = (bf16[2,256,128]{2,1,0:T(8,128)(2,1)S(1)}, bf16[2,256,128]{2,1,0:T(8,128)(2,1)S(1)}, u32[]{:S(2)}, u32[]{:S(2)}) collective-permute-start(bf16[2,256,128]{2,1,0:T(8,128)(2,1)S(1)} %get-tuple-element.35), channel_id=1, source_target_pairs={{0,128},{16,144},{32,160},{48,176},{64,192},{80,208},{96,224},{112... | collective-permute-start | bytes 393224 | tf_op jit(solution)/shard_map/ppermute | solution.py:27
  103.7 2.6 %collective-permute-start.26 = (bf16[2,256,128]{2,1,0:T(8,128)(2,1)S(1)}, bf16[2,256,128]{2,1,0:T(8,128)(2,1)S(1)}, u32[]{:S(2)}, u32[]{:S(2)}) collective-permute-start(bf16[2,256,128]{2,1,0:T(8,128)(2,1)S(1)} %get-tuple-element.32), channel_id=1, source_target_pairs={{0,64},{16,80},{32,96},{48,112},{64,128},{80,144},{96,160},{112,17... | collective-permute-start | bytes 393224 | tf_op jit(solution)/shard_map/ppermute | solution.py:27
  106.3 2.5 %collective-permute-done.29 = bf16[2,256,128]{2,1,0:T(8,128)(2,1)S(1)} collective-permute-done((bf16[2,256,128]{2,1,0:T(8,128)(2,1)S(1)}, bf16[2,256,128]{2,1,0:T(8,128)(2,1)S(1)}, u32[]{:S(2)}, u32[]{:S(2)}) %collective-permute-start.29) | collective-permute-done | bytes 131104 | tf_op jit(solution)/shard_map/ppermute | solution.py:27
  108.9 4.5 %collective-permute-start.31 = (bf16[2,256,128]{2,1,0:T(8,128)(2,1)S(1)}, bf16[2,256,128]{2,1,0:T(8,128)(2,1)S(1)}, u32[]{:S(2)}, u32[]{:S(2)}) collective-permute-start(bf16[2,256,128]{2,1,0:T(8,128)(2,1)S(1)} %add_convert_fusion.1), channel_id=1, source_target_pairs={{0,32},{16,48},{32,0},{48,16},{64,96},{80,112},{96,64},{112,80},{1... | collective-permute-start | bytes 393224 | tf_op jit(solution)/shard_map/ppermute | solution.py:31
  113.6 4.5 %collective-permute-done.31 = bf16[2,256,128]{2,1,0:T(8,128)(2,1)S(1)} collective-permute-done((bf16[2,256,128]{2,1,0:T(8,128)(2,1)S(1)}, bf16[2,256,128]{2,1,0:T(8,128)(2,1)S(1)}, u32[]{:S(2)}, u32[]{:S(2)}) %collective-permute-start.31) | collective-permute-done | bytes 131104 | tf_op jit(solution)/shard_map/ppermute | solution.py:31
  123.2 2.7 %collective-permute-done.32 = bf16[256,256]{1,0:T(8,128)(2,1)S(1)} collective-permute-done((bf16[256,256]{1,0:T(8,128)(2,1)S(1)}, bf16[256,256]{1,0:T(8,128)(2,1)S(1)}, u32[]{:S(2)}, u32[]{:S(2)}) %collective-permute-start.32) | collective-permute-done | bytes 131104 | tf_op jit(solution)/shard_map/ppermute | solution.py:17
  127.3 4.5 %collective-permute-start.35 = (bf16[256,256]{1,0:T(8,128)(2,1)S(1)}, bf16[256,256]{1,0:T(8,128)(2,1)S(1)}, u32[]{:S(2)}, u32[]{:S(2)}) collective-permute-start(bf16[256,256]{1,0:T(8,128)(2,1)S(1)} %add_convert_fusion), channel_id=1, source_target_pairs={{0,4},{1,5},{2,6},{3,7},{4,0},{5,1},{6,2},{7,3},{8,12},{9,13},{10,... | collective-permute-start | bytes 393224 | tf_op jit(solution)/shard_map/ppermute | solution.py:22
  135.2 2.7 %collective-permute-done.35 = bf16[256,256]{1,0:T(8,128)(2,1)S(1)} collective-permute-done((bf16[256,256]{1,0:T(8,128)(2,1)S(1)}, bf16[256,256]{1,0:T(8,128)(2,1)S(1)}, u32[]{:S(2)}, u32[]{:S(2)}) %collective-permute-start.35) | collective-permute-done | bytes 131104 | tf_op jit(solution)/shard_map/ppermute | solution.py:22
  139.0 5.3 %collective-permute-done.37 = bf16[256,256]{1,0:T(8,128)(2,1)S(1)} collective-permute-done((bf16[256,256]{1,0:T(8,128)(2,1)S(1)}, bf16[256,256]{1,0:T(8,128)(2,1)S(1)}, u32[]{:S(2)}, u32[]{:S(2)}) %collective-permute-start.37) | collective-permute-done | bytes 131104 | tf_op jit(solution)/shard_map/ppermute | solution.py:22
  (87 shorter events, 40.4 us)
Async XLA Ops:
  5.1 17.1 %collective-permute-start.1 = (bf16[4,80,512]{2,1,0:T(8,128)(2,1)S(1)}, bf16[4,80,512]{2,1,0:T(8,128)(2,1)S(1)}, u32[]{:S(2)}, u32[]{:S(2)}) collective-permute-start(bf16[4,80,512]{2,1,0:T(8,128)(2,1)S(1)} %get-tuple-element.22), channel_id=1, source_target_pairs={{0,2},{1,3},{2,0},{3,1},{4,6},{5,7},{6,4},{7,5},{8,10},{9,11},{10,... | collective-permute-start | bytes 983048 | tf_op jit(solution)/shard_map/ppermute | solution.py:17
  7.7 14.6 %collective-permute-start.2 = (bf16[4,80,512]{2,1,0:T(8,128)(2,1)S(1)}, bf16[4,80,512]{2,1,0:T(8,128)(2,1)S(1)}, u32[]{:S(2)}, u32[]{:S(2)}) collective-permute-start(bf16[4,80,512]{2,1,0:T(8,128)(2,1)S(1)} %get-tuple-element.23), channel_id=1, source_target_pairs={{0,3},{1,0},{2,1},{3,2},{4,7},{5,4},{6,5},{7,6},{8,11},{9,8},{10,9... | collective-permute-start | bytes 983048 | tf_op jit(solution)/shard_map/ppermute | solution.py:17
  9.1 18.9 %collective-permute-start.17 = (bf16[96,1024]{1,0:T(8,128)(2,1)S(1)}, bf16[96,1024]{1,0:T(8,128)(2,1)S(1)}, u32[]{:S(2)}, u32[]{:S(2)}) collective-permute-start(bf16[96,1024]{1,0:T(8,128)(2,1)S(1)} %bitcast.30), channel_id=1, source_target_pairs={{0,12},{1,13},{2,14},{3,15},{4,8},{5,9},{6,10},{7,11},{8,4},{9,5},... | collective-permute-start | bytes 589832 | tf_op jit(solution)/shard_map/ppermute | solution.py:22
  13.7 23.2 %collective-permute-start.16 = (bf16[96,1024]{1,0:T(8,128)(2,1)S(1)}, bf16[96,1024]{1,0:T(8,128)(2,1)S(1)}, u32[]{:S(2)}, u32[]{:S(2)}) collective-permute-start(bf16[96,1024]{1,0:T(8,128)(2,1)S(1)} %bitcast.31), channel_id=1, source_target_pairs={{0,8},{1,9},{2,10},{3,11},{4,12},{5,13},{6,14},{7,15},{8,0},{9,1},... | collective-permute-start | bytes 589832 | tf_op jit(solution)/shard_map/ppermute | solution.py:22
  14.1 22.9 %collective-permute-start.15 = (bf16[96,1024]{1,0:T(8,128)(2,1)S(1)}, bf16[96,1024]{1,0:T(8,128)(2,1)S(1)}, u32[]{:S(2)}, u32[]{:S(2)}) collective-permute-start(bf16[96,1024]{1,0:T(8,128)(2,1)S(1)} %bitcast.32), channel_id=1, source_target_pairs={{0,4},{1,5},{2,6},{3,7},{4,0},{5,1},{6,2},{7,3},{8,12},{9,13},{10,... | collective-permute-start | bytes 589832 | tf_op jit(solution)/shard_map/ppermute | solution.py:22
  22.9 16.3 %collective-permute-start.3 = (bf16[144,512]{1,0:T(8,128)(2,1)S(1)}, bf16[144,512]{1,0:T(8,128)(2,1)S(1)}, u32[]{:S(2)}, u32[]{:S(2)}) collective-permute-start(bf16[144,512]{1,0:T(8,128)(2,1)S(1)} %get-tuple-element.25), channel_id=1, source_target_pairs={{0,4},{1,5},{2,6},{3,7},{4,0},{5,1},{6,2},{7,3},{8,12},{9,13},{10,... | collective-permute-start | bytes 442376 | tf_op jit(solution)/shard_map/ppermute | solution.py:22
  25.0 15.1 %collective-permute-start.4 = (bf16[144,512]{1,0:T(8,128)(2,1)S(1)}, bf16[144,512]{1,0:T(8,128)(2,1)S(1)}, u32[]{:S(2)}, u32[]{:S(2)}) collective-permute-start(bf16[144,512]{1,0:T(8,128)(2,1)S(1)} %get-tuple-element.26), channel_id=1, source_target_pairs={{0,8},{1,9},{2,10},{3,11},{4,12},{5,13},{6,14},{7,15},{8,0},{9,1},... | collective-permute-start | bytes 442376 | tf_op jit(solution)/shard_map/ppermute | solution.py:22
  28.1 12.0 %collective-permute-start.5 = (bf16[144,512]{1,0:T(8,128)(2,1)S(1)}, bf16[144,512]{1,0:T(8,128)(2,1)S(1)}, u32[]{:S(2)}, u32[]{:S(2)}) collective-permute-start(bf16[144,512]{1,0:T(8,128)(2,1)S(1)} %get-tuple-element.27), channel_id=1, source_target_pairs={{0,12},{1,13},{2,14},{3,15},{4,8},{5,9},{6,10},{7,11},{8,4},{9,5},... | collective-permute-start | bytes 442376 | tf_op jit(solution)/shard_map/ppermute | solution.py:22
  36.9 21.8 %collective-permute-start.21 = (bf16[2,96,1024]{2,1,0:T(8,128)(2,1)S(1)}, bf16[2,96,1024]{2,1,0:T(8,128)(2,1)S(1)}, u32[]{:S(2)}, u32[]{:S(2)}) collective-permute-start(bf16[2,96,1024]{2,1,0:T(8,128)(2,1)S(1)} %pad_maximum_fusion.1.refs_9_), channel_id=1, source_target_pairs={{0,3},{1,0},{2,1},{3,2},{4,7},{5,4},{6,5},{7,6},{8,11},{9,8},{10,9... | collective-permute-start | bytes 1179656 | tf_op jit(solution)/shard_map/ppermute | solution.py:17
  37.1 22.8 %collective-permute-start.18 = (bf16[2,96,1024]{2,1,0:T(8,128)(2,1)S(1)}, bf16[2,96,1024]{2,1,0:T(8,128)(2,1)S(1)}, u32[]{:S(2)}, u32[]{:S(2)}) collective-permute-start(bf16[2,96,1024]{2,1,0:T(8,128)(2,1)S(1)} %pad_maximum_fusion.refs_8_), channel_id=1, source_target_pairs={{0,1},{1,2},{2,3},{3,0},{4,5},{5,6},{6,7},{7,4},{8,9},{9,10},{10,1... | collective-permute-start | bytes 1179656 | tf_op jit(solution)/shard_map/ppermute | solution.py:17
  40.7 13.5 %collective-permute-start.7 = (bf16[144,512]{1,0:T(8,128)(2,1)S(1)}, bf16[144,512]{1,0:T(8,128)(2,1)S(1)}, u32[]{:S(2)}, u32[]{:S(2)}) collective-permute-start(bf16[144,512]{1,0:T(8,128)(2,1)S(1)} %pick_z.1), channel_id=1, source_target_pairs={{0,8},{1,9},{2,10},{3,11},{4,12},{5,13},{6,14},{7,15},{8,0},{9,1},... | collective-permute-start | bytes 442376 | tf_op jit(solution)/shard_map/ppermute | solution.py:22
  44.3 11.0 %collective-permute-start.8 = (bf16[144,512]{1,0:T(8,128)(2,1)S(1)}, bf16[144,512]{1,0:T(8,128)(2,1)S(1)}, u32[]{:S(2)}, u32[]{:S(2)}) collective-permute-start(bf16[144,512]{1,0:T(8,128)(2,1)S(1)} %pick_z.1), channel_id=1, source_target_pairs={{0,12},{1,13},{2,14},{3,15},{4,8},{5,9},{6,10},{7,11},{8,4},{9,5},... | collective-permute-start | bytes 442376 | tf_op jit(solution)/shard_map/ppermute | solution.py:22
  45.4 12.1 %collective-permute-start.6 = (bf16[144,512]{1,0:T(8,128)(2,1)S(1)}, bf16[144,512]{1,0:T(8,128)(2,1)S(1)}, u32[]{:S(2)}, u32[]{:S(2)}) collective-permute-start(bf16[144,512]{1,0:T(8,128)(2,1)S(1)} %pick_z.1), channel_id=1, source_target_pairs={{0,4},{1,5},{2,6},{3,7},{4,0},{5,1},{6,2},{7,3},{8,12},{9,13},{10,... | collective-permute-start | bytes 442376 | tf_op jit(solution)/shard_map/ppermute | solution.py:22
  54.2 13.1 %collective-permute-start.19 = (bf16[2,96,1024]{2,1,0:T(8,128)(2,1)S(1)}, bf16[2,96,1024]{2,1,0:T(8,128)(2,1)S(1)}, u32[]{:S(2)}, u32[]{:S(2)}) collective-permute-start(bf16[2,96,1024]{2,1,0:T(8,128)(2,1)S(1)} %pad_maximum_fusion.1.refs_9_), channel_id=1, source_target_pairs={{0,1},{1,2},{2,3},{3,0},{4,5},{5,6},{6,7},{7,4},{8,9},{9,10},{10,1... | collective-permute-start | bytes 1179656 | tf_op jit(solution)/shard_map/ppermute | solution.py:17
  55.3 12.1 %collective-permute-start.20 = (bf16[2,96,1024]{2,1,0:T(8,128)(2,1)S(1)}, bf16[2,96,1024]{2,1,0:T(8,128)(2,1)S(1)}, u32[]{:S(2)}, u32[]{:S(2)}) collective-permute-start(bf16[2,96,1024]{2,1,0:T(8,128)(2,1)S(1)} %pad_maximum_fusion.refs_8_), channel_id=1, source_target_pairs={{0,3},{1,0},{2,1},{3,2},{4,7},{5,4},{6,5},{7,6},{8,11},{9,8},{10,9... | collective-permute-start | bytes 1179656 | tf_op jit(solution)/shard_map/ppermute | solution.py:17
  57.5 16.0 %collective-permute-start.12 = (bf16[2,144,512]{2,1,0:T(8,128)(2,1)S(1)}, bf16[2,144,512]{2,1,0:T(8,128)(2,1)S(1)}, u32[]{:S(2)}, u32[]{:S(2)}) collective-permute-start(bf16[2,144,512]{2,1,0:T(8,128)(2,1)S(1)} %pad_maximum_fusion.3.refs_1_), channel_id=1, source_target_pairs={{0,3},{1,0},{2,1},{3,2},{4,7},{5,4},{6,5},{7,6},{8,11},{9,8},{10,9... | collective-permute-start | bytes 884744 | tf_op jit(solution)/shard_map/ppermute | solution.py:17
  58.8 18.2 %collective-permute-start.10 = (bf16[2,144,512]{2,1,0:T(8,128)(2,1)S(1)}, bf16[2,144,512]{2,1,0:T(8,128)(2,1)S(1)}, u32[]{:S(2)}, u32[]{:S(2)}) collective-permute-start(bf16[2,144,512]{2,1,0:T(8,128)(2,1)S(1)} %pad_maximum_fusion.3.refs_1_), channel_id=1, source_target_pairs={{0,1},{1,2},{2,3},{3,0},{4,5},{5,6},{6,7},{7,4},{8,9},{9,10},{10,1... | collective-permute-start | bytes 884744 | tf_op jit(solution)/shard_map/ppermute | solution.py:17
  59.9 20.0 %collective-permute-start.9 = (bf16[2,144,512]{2,1,0:T(8,128)(2,1)S(1)}, bf16[2,144,512]{2,1,0:T(8,128)(2,1)S(1)}, u32[]{:S(2)}, u32[]{:S(2)}) collective-permute-start(bf16[2,144,512]{2,1,0:T(8,128)(2,1)S(1)} %pad_maximum_fusion.2.refs_0_), channel_id=1, source_target_pairs={{0,1},{1,2},{2,3},{3,0},{4,5},{5,6},{6,7},{7,4},{8,9},{9,10},{10,1... | collective-permute-start | bytes 884744 | tf_op jit(solution)/shard_map/ppermute | solution.py:17
  67.3 21.0 %collective-permute-start.22 = (bf16[2,96,1024]{2,1,0:T(8,128)(2,1)S(1)}, bf16[2,96,1024]{2,1,0:T(8,128)(2,1)S(1)}, u32[]{:S(2)}, u32[]{:S(2)}) collective-permute-start(bf16[2,96,1024]{2,1,0:T(8,128)(2,1)S(1)} %get-tuple-element.28), channel_id=1, source_target_pairs={{0,1},{1,2},{2,3},{3,0},{4,5},{5,6},{6,7},{7,4},{8,9},{9,10},{10,1... | collective-permute-start | bytes 1179656 | tf_op jit(solution)/shard_map/ppermute | solution.py:17
  67.3 21.0 %collective-permute-start.23 = (bf16[2,96,1024]{2,1,0:T(8,128)(2,1)S(1)}, bf16[2,96,1024]{2,1,0:T(8,128)(2,1)S(1)}, u32[]{:S(2)}, u32[]{:S(2)}) collective-permute-start(bf16[2,96,1024]{2,1,0:T(8,128)(2,1)S(1)} %get-tuple-element.29), channel_id=1, source_target_pairs={{0,3},{1,0},{2,1},{3,2},{4,7},{5,4},{6,5},{7,6},{8,11},{9,8},{10,9... | collective-permute-start | bytes 1179656 | tf_op jit(solution)/shard_map/ppermute | solution.py:17
  73.6 14.7 %collective-permute-start.11 = (bf16[2,144,512]{2,1,0:T(8,128)(2,1)S(1)}, bf16[2,144,512]{2,1,0:T(8,128)(2,1)S(1)}, u32[]{:S(2)}, u32[]{:S(2)}) collective-permute-start(bf16[2,144,512]{2,1,0:T(8,128)(2,1)S(1)} %pad_maximum_fusion.2.refs_0_), channel_id=1, source_target_pairs={{0,3},{1,0},{2,1},{3,2},{4,7},{5,4},{6,5},{7,6},{8,11},{9,8},{10,9... | collective-permute-start | bytes 884744 | tf_op jit(solution)/shard_map/ppermute | solution.py:17
  77.0 15.1 %collective-permute-start.14 = (bf16[2,144,512]{2,1,0:T(8,128)(2,1)S(1)}, bf16[2,144,512]{2,1,0:T(8,128)(2,1)S(1)}, u32[]{:S(2)}, u32[]{:S(2)}) collective-permute-start(bf16[2,144,512]{2,1,0:T(8,128)(2,1)S(1)} %collective-permute-done.12.refs_5_), channel_id=1, source_target_pairs={{0,3},{1,0},{2,1},{3,2},{4,7},{5,4},{6,5},{7,6},{8,11},{9,8},{10,9... | collective-permute-start | bytes 884744 | tf_op jit(solution)/shard_map/ppermute | solution.py:17
  80.0 12.2 %collective-permute-start.13 = (bf16[2,144,512]{2,1,0:T(8,128)(2,1)S(1)}, bf16[2,144,512]{2,1,0:T(8,128)(2,1)S(1)}, u32[]{:S(2)}, u32[]{:S(2)}) collective-permute-start(bf16[2,144,512]{2,1,0:T(8,128)(2,1)S(1)} %collective-permute-done.9.refs_2_), channel_id=1, source_target_pairs={{0,1},{1,2},{2,3},{3,0},{4,5},{5,6},{6,7},{7,4},{8,9},{9,10},{10,1... | collective-permute-start | bytes 884744 | tf_op jit(solution)/shard_map/ppermute | solution.py:17
  102.2 11.2 %collective-permute-start.25 = (bf16[2,256,128]{2,1,0:T(8,128)(2,1)S(1)}, bf16[2,256,128]{2,1,0:T(8,128)(2,1)S(1)}, u32[]{:S(2)}, u32[]{:S(2)}) collective-permute-start(bf16[2,256,128]{2,1,0:T(8,128)(2,1)S(1)} %get-tuple-element.31), channel_id=1, source_target_pairs={{0,128},{16,144},{32,160},{48,176},{64,192},{80,208},{96,224},{112... | collective-permute-start | bytes 393224 | tf_op jit(solution)/shard_map/ppermute | solution.py:27
  (22 other events, 368.9 us)

commit v3 on v2

--- a/solution.py
+++ b/solution.py
@@ -48,7 +48,7 @@
     )(first, second)
 
 
-def gather_blocks(block, name):
+def gather_border(block):
     near = [hop_z(block, bits) for bits in (1, 2, 3)]
     low = jnp.stack([block, near[0]])
     high = jnp.stack([near[1], near[2]])
@@ -56,12 +56,22 @@
     high_right = hop_x(high, -1)
     high_left = hop_x(high, 1)
     low_right = hop_x(low, -1)
-    if name == "border":
-        sent_left, sent_right = pass_on(low_left, high_right)
-    else:
-        sent_left, sent_right = low_left, high_right
+    sent_left, sent_right = pass_on(low_left, high_right)
     low_far = hop_x(sent_left, 1)
     high_far = hop_x(sent_right, -1)
+    return [low, high, low_left, high_left, low_right, high_right, low_far, high_far]
+
+
+def gather_panel(block):
+    near = hop_z(block, 1)
+    high = jnp.stack([hop_z(block, 2), hop_z(block, 3)])
+    low = jnp.stack([block, near])
+    low_left = hop_x(low, 1)
+    low_right = hop_x(low, -1)
+    high_right = hop_x(high, -1)
+    high_left = hop_x(high, 1)
+    low_far = hop_x(low_left, 1)
+    high_far = hop_x(high_right, -1)
     return [low, high, low_left, high_left, low_right, high_right, low_far, high_far]
 
 
@@ -257,7 +267,7 @@
 
 
 def step(panels, panel_owner, interface_cols, border, block_rows, pattern, block_x):
-    strips = gather_blocks(border.T, "border")
+    strips = gather_border(border.T)
 
     chunks = pack(panel_owner.T, panels)
     far = hop_x(chunks[2], 2)
@@ -265,7 +275,7 @@
     pieces = pick(panel_owner.T, chunks)
     pieces = [pieces[0]] + [hop_z(pieces[bits], bits) for bits in (1, 2, 3)]
     piece = pick_z(panel_owner.T, pieces)
-    tile = make_tile(gather_blocks(piece, "panel"), strips, interface_cols)
+    tile = make_tile(gather_panel(piece), strips, interface_cols)
 
     placed = place(block_rows.T, tile, swap_grp(tile, 1))
     other = add_y(placed[4:])

time: 146 us -> 146 us (level)
  no operation moved by 1% of the time
where the time goes in v3:
time: 146 us; the launch traced here: 145 us
  waiting for transfers between devices  72.6 us (50%)
  starting transfers between devices  62.2 us (43%)
  Pallas kernels  5.63 us (4%)
  local copies, waits for them, and re-layouts  2.42 us (2%)
    ppermute x18, waiting for transfers between devices, hop_x(): return lax.ppermute(value, 'dev', perm)  35.9 us
    ppermute x12, waiting for transfers between devices, hop_z(): return lax.ppermute(value, 'dev', perm)  27.6 us
    ppermute x18, starting transfers between devices, hop_x(): return lax.ppermute(value, 'dev', perm)  24.9 us
    ppermute x12, starting transfers between devices, hop_z(): return lax.ppermute(value, 'dev', perm)  24.3 us
    ppermute x6, starting transfers between devices, hop_y(): return lax.ppermute(value, 'grp', perm)  8.43 us
    ppermute x2, waiting for transfers between devices, swap_grp(): return lax.ppermute(value, 'grp', [(g, g ^ bits) for g in range(16)])  6.39 us
    ppermute x2, starting transfers between devices, swap_grp(): return lax.ppermute(value, 'grp', [(g, g ^ bits) for g in range(16)])  4.6 us
  transfers between devices with their start and end apart: 38, of which 19 were waited for; matrix products, arithmetic and copies ran while one was open for 0% of the time, Pallas kernels for 1%

profile of v3, /device:TPU:8, one launch (start us, length us, event | category | flops | bytes accessed | tf_op | source)
XLA Modules:
  0.0 145.1 jit_solution(13468049218626341681)
XLA Ops:
  5.1 2.6 %collective-permute-start.1 = (bf16[4,80,512]{2,1,0:T(8,128)(2,1)S(1)}, bf16[4,80,512]{2,1,0:T(8,128)(2,1)S(1)}, u32[]{:S(2)}, u32[]{:S(2)}) collective-permute-start(bf16[4,80,512]{2,1,0:T(8,128)(2,1)S(1)} %get-tuple-element.22), channel_id=1, source_target_pairs={{0,2},{1,3},{2,0},{3,1},{4,6},{5,7},{6,4},{7,5},{8,10},{9,11},{10,... | collective-permute-start | bytes 983048 | tf_op jit(solution)/shard_map/ppermute | solution.py:17
  9.1 4.6 %collective-permute-start.17 = (bf16[96,1024]{1,0:T(8,128)(2,1)S(1)}, bf16[96,1024]{1,0:T(8,128)(2,1)S(1)}, u32[]{:S(2)}, u32[]{:S(2)}) collective-permute-start(bf16[96,1024]{1,0:T(8,128)(2,1)S(1)} %bitcast.30), channel_id=1, source_target_pairs={{0,12},{1,13},{2,14},{3,15},{4,8},{5,9},{6,10},{7,11},{8,4},{9,5},... | collective-permute-start | bytes 589832 | tf_op jit(solution)/shard_map/ppermute | solution.py:22
  16.0 6.2 %collective-permute-done.1.refs_2_ = bf16[4,80,512]{2,1,0:T(8,128)(2,1)S(1)} collective-permute-done((bf16[4,80,512]{2,1,0:T(8,128)(2,1)S(1)}, bf16[4,80,512]{2,1,0:T(8,128)(2,1)S(1)}, u32[]{:S(2)}, u32[]{:S(2)}) %collective-permute-start.1) | collective-permute-done | bytes 327712 | tf_op jit(solution)/shard_map/ppermute | solution.py:17
  25.0 3.1 %collective-permute-start.4 = (bf16[144,512]{1,0:T(8,128)(2,1)S(1)}, bf16[144,512]{1,0:T(8,128)(2,1)S(1)}, u32[]{:S(2)}, u32[]{:S(2)}) collective-permute-start(bf16[144,512]{1,0:T(8,128)(2,1)S(1)} %get-tuple-element.26), channel_id=1, source_target_pairs={{0,8},{1,9},{2,10},{3,11},{4,12},{5,13},{6,14},{7,15},{8,0},{9,1},... | collective-permute-start | bytes 442376 | tf_op jit(solution)/shard_map/ppermute | solution.py:22
  28.1 8.8 %collective-permute-done.16 = bf16[96,1024]{1,0:T(8,128)(2,1)S(1)} collective-permute-done((bf16[96,1024]{1,0:T(8,128)(2,1)S(1)}, bf16[96,1024]{1,0:T(8,128)(2,1)S(1)}, u32[]{:S(2)}, u32[]{:S(2)}) %collective-permute-start.16) | collective-permute-done | bytes 196640 | tf_op jit(solution)/shard_map/ppermute | solution.py:22
  40.7 3.5 %collective-permute-start.7 = (bf16[144,512]{1,0:T(8,128)(2,1)S(1)}, bf16[144,512]{1,0:T(8,128)(2,1)S(1)}, u32[]{:S(2)}, u32[]{:S(2)}) collective-permute-start(bf16[144,512]{1,0:T(8,128)(2,1)S(1)} %pick_z.1), channel_id=1, source_target_pairs={{0,8},{1,9},{2,10},{3,11},{4,12},{5,13},{6,14},{7,15},{8,0},{9,1},... | collective-permute-start | bytes 442376 | tf_op jit(solution)/shard_map/ppermute | solution.py:22
  45.4 8.8 %collective-permute-done.7 = bf16[144,512]{1,0:T(8,128)(2,1)S(1)} collective-permute-done((bf16[144,512]{1,0:T(8,128)(2,1)S(1)}, bf16[144,512]{1,0:T(8,128)(2,1)S(1)}, u32[]{:S(2)}, u32[]{:S(2)}) %collective-permute-start.7) | collective-permute-done | bytes 147488 | tf_op jit(solution)/shard_map/ppermute | solution.py:22
  60.1 7.2 %collective-permute-done.19.refs_11_ = bf16[2,96,1024]{2,1,0:T(8,128)(2,1)S(1)} collective-permute-done((bf16[2,96,1024]{2,1,0:T(8,128)(2,1)S(1)}, bf16[2,96,1024]{2,1,0:T(8,128)(2,1)S(1)}, u32[]{:S(2)}, u32[]{:S(2)}) %collective-permute-start.19) | collective-permute-done | bytes 393248 | tf_op jit(solution)/shard_map/ppermute | solution.py:17
  67.3 3.4 %collective-permute-start.23 = (bf16[2,96,1024]{2,1,0:T(8,128)(2,1)S(1)}, bf16[2,96,1024]{2,1,0:T(8,128)(2,1)S(1)}, u32[]{:S(2)}, u32[]{:S(2)}) collective-permute-start(bf16[2,96,1024]{2,1,0:T(8,128)(2,1)S(1)} %get-tuple-element.29), channel_id=1, source_target_pairs={{0,3},{1,0},{2,1},{3,2},{4,7},{5,4},{6,5},{7,6},{8,11},{9,8},{10,9... | collective-permute-start | bytes 1179656 | tf_op jit(solution)/shard_map/ppermute | solution.py:17
  70.7 2.9 %collective-permute-done.12.refs_5_ = bf16[2,144,512]{2,1,0:T(8,128)(2,1)S(1)} collective-permute-done((bf16[2,144,512]{2,1,0:T(8,128)(2,1)S(1)}, bf16[2,144,512]{2,1,0:T(8,128)(2,1)S(1)}, u32[]{:S(2)}, u32[]{:S(2)}) %collective-permute-start.12) | collective-permute-done | bytes 294944 | tf_op jit(solution)/shard_map/ppermute | solution.py:17
  73.6 3.4 %collective-permute-start.11 = (bf16[2,144,512]{2,1,0:T(8,128)(2,1)S(1)}, bf16[2,144,512]{2,1,0:T(8,128)(2,1)S(1)}, u32[]{:S(2)}, u32[]{:S(2)}) collective-permute-start(bf16[2,144,512]{2,1,0:T(8,128)(2,1)S(1)} %pad_maximum_fusion.2.refs_0_), channel_id=1, source_target_pairs={{0,3},{1,0},{2,1},{3,2},{4,7},{5,4},{6,5},{7,6},{8,11},{9,8},{10,9... | collective-permute-start | bytes 884744 | tf_op jit(solution)/shard_map/ppermute | solution.py:17
  77.0 2.9 %collective-permute-done.9.refs_2_ = bf16[2,144,512]{2,1,0:T(8,128)(2,1)S(1)} collective-permute-done((bf16[2,144,512]{2,1,0:T(8,128)(2,1)S(1)}, bf16[2,144,512]{2,1,0:T(8,128)(2,1)S(1)}, u32[]{:S(2)}, u32[]{:S(2)}) %collective-permute-start.9) | collective-permute-done | bytes 294944 | tf_op jit(solution)/shard_map/ppermute | solution.py:17
  80.0 8.4 %collective-permute-done.11.refs_4_ = bf16[2,144,512]{2,1,0:T(8,128)(2,1)S(1)} collective-permute-done((bf16[2,144,512]{2,1,0:T(8,128)(2,1)S(1)}, bf16[2,144,512]{2,1,0:T(8,128)(2,1)S(1)}, u32[]{:S(2)}, u32[]{:S(2)}) %collective-permute-start.11) | collective-permute-done | bytes 294944 | tf_op jit(solution)/shard_map/ppermute | solution.py:17
  88.3 3.8 %collective-permute-done.14.refs_7_ = bf16[2,144,512]{2,1,0:T(8,128)(2,1)S(1)} collective-permute-done((bf16[2,144,512]{2,1,0:T(8,128)(2,1)S(1)}, bf16[2,144,512]{2,1,0:T(8,128)(2,1)S(1)}, u32[]{:S(2)}, u32[]{:S(2)}) %collective-permute-start.14) | collective-permute-done | bytes 294944 | tf_op jit(solution)/shard_map/ppermute | solution.py:17
  92.2 2.5 %tile.1.own = bf16[8,256,128]{2,1,0:T(8,128)(2,1)S(1)} custom-call(bf16[2,144,512]{2,1,0:T(8,128)(2,1)S(1)} %pad_maximum_fusion.2.refs_0_, bf16[2,144,512]{2,1,0:T(8,128)(2,1)S(1)} %pad_maximum_fusion.3.refs_1_, bf16[2,144,512]{2,1,0:T(8,128)(2,1)S(1)} %collective-permute-done.9.refs_2_, bf16[2,144,512]{2,1,0:T(8,128)(2,1)S(1)} %collective-permute-done.10.refs_3_, ...), custom_call_target="tpu_custom_call" | custom-call | flops 1500000000 | bytes 8000000 | tf_op jit(solution)/shard_map/tile/pallas_call | solution.py:213
  97.9 2.3 %collective-permute-start.28 = (bf16[2,256,128]{2,1,0:T(8,128)(2,1)S(1)}, bf16[2,256,128]{2,1,0:T(8,128)(2,1)S(1)}, u32[]{:S(2)}, u32[]{:S(2)}) collective-permute-start(bf16[2,256,128]{2,1,0:T(8,128)(2,1)S(1)} %get-tuple-element.35), channel_id=1, source_target_pairs={{0,128},{16,144},{32,160},{48,176},{64,192},{80,208},{96,224},{112... | collective-permute-start | bytes 393224 | tf_op jit(solution)/shard_map/ppermute | solution.py:27
  103.7 2.6 %collective-permute-start.26 = (bf16[2,256,128]{2,1,0:T(8,128)(2,1)S(1)}, bf16[2,256,128]{2,1,0:T(8,128)(2,1)S(1)}, u32[]{:S(2)}, u32[]{:S(2)}) collective-permute-start(bf16[2,256,128]{2,1,0:T(8,128)(2,1)S(1)} %get-tuple-element.32), channel_id=1, source_target_pairs={{0,64},{16,80},{32,96},{48,112},{64,128},{80,144},{96,160},{112,17... | collective-permute-start | bytes 393224 | tf_op jit(solution)/shard_map/ppermute | solution.py:27
  106.3 2.5 %collective-permute-done.29 = bf16[2,256,128]{2,1,0:T(8,128)(2,1)S(1)} collective-permute-done((bf16[2,256,128]{2,1,0:T(8,128)(2,1)S(1)}, bf16[2,256,128]{2,1,0:T(8,128)(2,1)S(1)}, u32[]{:S(2)}, u32[]{:S(2)}) %collective-permute-start.29) | collective-permute-done | bytes 131104 | tf_op jit(solution)/shard_map/ppermute | solution.py:27
  108.9 4.5 %collective-permute-start.31 = (bf16[2,256,128]{2,1,0:T(8,128)(2,1)S(1)}, bf16[2,256,128]{2,1,0:T(8,128)(2,1)S(1)}, u32[]{:S(2)}, u32[]{:S(2)}) collective-permute-start(bf16[2,256,128]{2,1,0:T(8,128)(2,1)S(1)} %add_convert_fusion.1), channel_id=1, source_target_pairs={{0,32},{16,48},{32,0},{48,16},{64,96},{80,112},{96,64},{112,80},{1... | collective-permute-start | bytes 393224 | tf_op jit(solution)/shard_map/ppermute | solution.py:31
  113.6 4.5 %collective-permute-done.31 = bf16[2,256,128]{2,1,0:T(8,128)(2,1)S(1)} collective-permute-done((bf16[2,256,128]{2,1,0:T(8,128)(2,1)S(1)}, bf16[2,256,128]{2,1,0:T(8,128)(2,1)S(1)}, u32[]{:S(2)}, u32[]{:S(2)}) %collective-permute-start.31) | collective-permute-done | bytes 131104 | tf_op jit(solution)/shard_map/ppermute | solution.py:31
  123.2 2.7 %collective-permute-done.32 = bf16[256,256]{1,0:T(8,128)(2,1)S(1)} collective-permute-done((bf16[256,256]{1,0:T(8,128)(2,1)S(1)}, bf16[256,256]{1,0:T(8,128)(2,1)S(1)}, u32[]{:S(2)}, u32[]{:S(2)}) %collective-permute-start.32) | collective-permute-done | bytes 131104 | tf_op jit(solution)/shard_map/ppermute | solution.py:17
  127.3 4.5 %collective-permute-start.35 = (bf16[256,256]{1,0:T(8,128)(2,1)S(1)}, bf16[256,256]{1,0:T(8,128)(2,1)S(1)}, u32[]{:S(2)}, u32[]{:S(2)}) collective-permute-start(bf16[256,256]{1,0:T(8,128)(2,1)S(1)} %add_convert_fusion), channel_id=1, source_target_pairs={{0,4},{1,5},{2,6},{3,7},{4,0},{5,1},{6,2},{7,3},{8,12},{9,13},{10,... | collective-permute-start | bytes 393224 | tf_op jit(solution)/shard_map/ppermute | solution.py:22
  135.2 2.7 %collective-permute-done.35 = bf16[256,256]{1,0:T(8,128)(2,1)S(1)} collective-permute-done((bf16[256,256]{1,0:T(8,128)(2,1)S(1)}, bf16[256,256]{1,0:T(8,128)(2,1)S(1)}, u32[]{:S(2)}, u32[]{:S(2)}) %collective-permute-start.35) | collective-permute-done | bytes 131104 | tf_op jit(solution)/shard_map/ppermute | solution.py:22
  139.0 5.3 %collective-permute-done.37 = bf16[256,256]{1,0:T(8,128)(2,1)S(1)} collective-permute-done((bf16[256,256]{1,0:T(8,128)(2,1)S(1)}, bf16[256,256]{1,0:T(8,128)(2,1)S(1)}, u32[]{:S(2)}, u32[]{:S(2)}) %collective-permute-start.37) | collective-permute-done | bytes 131104 | tf_op jit(solution)/shard_map/ppermute | solution.py:22
  (87 shorter events, 40.4 us)
Async XLA Ops:
  5.1 17.1 %collective-permute-start.1 = (bf16[4,80,512]{2,1,0:T(8,128)(2,1)S(1)}, bf16[4,80,512]{2,1,0:T(8,128)(2,1)S(1)}, u32[]{:S(2)}, u32[]{:S(2)}) collective-permute-start(bf16[4,80,512]{2,1,0:T(8,128)(2,1)S(1)} %get-tuple-element.22), channel_id=1, source_target_pairs={{0,2},{1,3},{2,0},{3,1},{4,6},{5,7},{6,4},{7,5},{8,10},{9,11},{10,... | collective-permute-start | bytes 983048 | tf_op jit(solution)/shard_map/ppermute | solution.py:17
  7.7 14.6 %collective-permute-start.2 = (bf16[4,80,512]{2,1,0:T(8,128)(2,1)S(1)}, bf16[4,80,512]{2,1,0:T(8,128)(2,1)S(1)}, u32[]{:S(2)}, u32[]{:S(2)}) collective-permute-start(bf16[4,80,512]{2,1,0:T(8,128)(2,1)S(1)} %get-tuple-element.23), channel_id=1, source_target_pairs={{0,3},{1,0},{2,1},{3,2},{4,7},{5,4},{6,5},{7,6},{8,11},{9,8},{10,9... | collective-permute-start | bytes 983048 | tf_op jit(solution)/shard_map/ppermute | solution.py:17
  9.1 18.9 %collective-permute-start.17 = (bf16[96,1024]{1,0:T(8,128)(2,1)S(1)}, bf16[96,1024]{1,0:T(8,128)(2,1)S(1)}, u32[]{:S(2)}, u32[]{:S(2)}) collective-permute-start(bf16[96,1024]{1,0:T(8,128)(2,1)S(1)} %bitcast.30), channel_id=1, source_target_pairs={{0,12},{1,13},{2,14},{3,15},{4,8},{5,9},{6,10},{7,11},{8,4},{9,5},... | collective-permute-start | bytes 589832 | tf_op jit(solution)/shard_map/ppermute | solution.py:22
  13.7 23.2 %collective-permute-start.16 = (bf16[96,1024]{1,0:T(8,128)(2,1)S(1)}, bf16[96,1024]{1,0:T(8,128)(2,1)S(1)}, u32[]{:S(2)}, u32[]{:S(2)}) collective-permute-start(bf16[96,1024]{1,0:T(8,128)(2,1)S(1)} %bitcast.31), channel_id=1, source_target_pairs={{0,8},{1,9},{2,10},{3,11},{4,12},{5,13},{6,14},{7,15},{8,0},{9,1},... | collective-permute-start | bytes 589832 | tf_op jit(solution)/shard_map/ppermute | solution.py:22
  14.1 22.9 %collective-permute-start.15 = (bf16[96,1024]{1,0:T(8,128)(2,1)S(1)}, bf16[96,1024]{1,0:T(8,128)(2,1)S(1)}, u32[]{:S(2)}, u32[]{:S(2)}) collective-permute-start(bf16[96,1024]{1,0:T(8,128)(2,1)S(1)} %bitcast.32), channel_id=1, source_target_pairs={{0,4},{1,5},{2,6},{3,7},{4,0},{5,1},{6,2},{7,3},{8,12},{9,13},{10,... | collective-permute-start | bytes 589832 | tf_op jit(solution)/shard_map/ppermute | solution.py:22
  22.9 16.3 %collective-permute-start.3 = (bf16[144,512]{1,0:T(8,128)(2,1)S(1)}, bf16[144,512]{1,0:T(8,128)(2,1)S(1)}, u32[]{:S(2)}, u32[]{:S(2)}) collective-permute-start(bf16[144,512]{1,0:T(8,128)(2,1)S(1)} %get-tuple-element.25), channel_id=1, source_target_pairs={{0,4},{1,5},{2,6},{3,7},{4,0},{5,1},{6,2},{7,3},{8,12},{9,13},{10,... | collective-permute-start | bytes 442376 | tf_op jit(solution)/shard_map/ppermute | solution.py:22
  25.0 15.1 %collective-permute-start.4 = (bf16[144,512]{1,0:T(8,128)(2,1)S(1)}, bf16[144,512]{1,0:T(8,128)(2,1)S(1)}, u32[]{:S(2)}, u32[]{:S(2)}) collective-permute-start(bf16[144,512]{1,0:T(8,128)(2,1)S(1)} %get-tuple-element.26), channel_id=1, source_target_pairs={{0,8},{1,9},{2,10},{3,11},{4,12},{5,13},{6,14},{7,15},{8,0},{9,1},... | collective-permute-start | bytes 442376 | tf_op jit(solution)/shard_map/ppermute | solution.py:22
  28.1 12.0 %collective-permute-start.5 = (bf16[144,512]{1,0:T(8,128)(2,1)S(1)}, bf16[144,512]{1,0:T(8,128)(2,1)S(1)}, u32[]{:S(2)}, u32[]{:S(2)}) collective-permute-start(bf16[144,512]{1,0:T(8,128)(2,1)S(1)} %get-tuple-element.27), channel_id=1, source_target_pairs={{0,12},{1,13},{2,14},{3,15},{4,8},{5,9},{6,10},{7,11},{8,4},{9,5},... | collective-permute-start | bytes 442376 | tf_op jit(solution)/shard_map/ppermute | solution.py:22
  36.9 21.8 %collective-permute-start.21 = (bf16[2,96,1024]{2,1,0:T(8,128)(2,1)S(1)}, bf16[2,96,1024]{2,1,0:T(8,128)(2,1)S(1)}, u32[]{:S(2)}, u32[]{:S(2)}) collective-permute-start(bf16[2,96,1024]{2,1,0:T(8,128)(2,1)S(1)} %pad_maximum_fusion.1.refs_9_), channel_id=1, source_target_pairs={{0,3},{1,0},{2,1},{3,2},{4,7},{5,4},{6,5},{7,6},{8,11},{9,8},{10,9... | collective-permute-start | bytes 1179656 | tf_op jit(solution)/shard_map/ppermute | solution.py:17
  37.1 22.8 %collective-permute-start.18 = (bf16[2,96,1024]{2,1,0:T(8,128)(2,1)S(1)}, bf16[2,96,1024]{2,1,0:T(8,128)(2,1)S(1)}, u32[]{:S(2)}, u32[]{:S(2)}) collective-permute-start(bf16[2,96,1024]{2,1,0:T(8,128)(2,1)S(1)} %pad_maximum_fusion.refs_8_), channel_id=1, source_target_pairs={{0,1},{1,2},{2,3},{3,0},{4,5},{5,6},{6,7},{7,4},{8,9},{9,10},{10,1... | collective-permute-start | bytes 1179656 | tf_op jit(solution)/shard_map/ppermute | solution.py:17
  40.7 13.5 %collective-permute-start.7 = (bf16[144,512]{1,0:T(8,128)(2,1)S(1)}, bf16[144,512]{1,0:T(8,128)(2,1)S(1)}, u32[]{:S(2)}, u32[]{:S(2)}) collective-permute-start(bf16[144,512]{1,0:T(8,128)(2,1)S(1)} %pick_z.1), channel_id=1, source_target_pairs={{0,8},{1,9},{2,10},{3,11},{4,12},{5,13},{6,14},{7,15},{8,0},{9,1},... | collective-permute-start | bytes 442376 | tf_op jit(solution)/shard_map/ppermute | solution.py:22
  44.3 11.0 %collective-permute-start.8 = (bf16[144,512]{1,0:T(8,128)(2,1)S(1)}, bf16[144,512]{1,0:T(8,128)(2,1)S(1)}, u32[]{:S(2)}, u32[]{:S(2)}) collective-permute-start(bf16[144,512]{1,0:T(8,128)(2,1)S(1)} %pick_z.1), channel_id=1, source_target_pairs={{0,12},{1,13},{2,14},{3,15},{4,8},{5,9},{6,10},{7,11},{8,4},{9,5},... | collective-permute-start | bytes 442376 | tf_op jit(solution)/shard_map/ppermute | solution.py:22
  45.4 12.1 %collective-permute-start.6 = (bf16[144,512]{1,0:T(8,128)(2,1)S(1)}, bf16[144,512]{1,0:T(8,128)(2,1)S(1)}, u32[]{:S(2)}, u32[]{:S(2)}) collective-permute-start(bf16[144,512]{1,0:T(8,128)(2,1)S(1)} %pick_z.1), channel_id=1, source_target_pairs={{0,4},{1,5},{2,6},{3,7},{4,0},{5,1},{6,2},{7,3},{8,12},{9,13},{10,... | collective-permute-start | bytes 442376 | tf_op jit(solution)/shard_map/ppermute | solution.py:22
  54.2 13.1 %collective-permute-start.19 = (bf16[2,96,1024]{2,1,0:T(8,128)(2,1)S(1)}, bf16[2,96,1024]{2,1,0:T(8,128)(2,1)S(1)}, u32[]{:S(2)}, u32[]{:S(2)}) collective-permute-start(bf16[2,96,1024]{2,1,0:T(8,128)(2,1)S(1)} %pad_maximum_fusion.1.refs_9_), channel_id=1, source_target_pairs={{0,1},{1,2},{2,3},{3,0},{4,5},{5,6},{6,7},{7,4},{8,9},{9,10},{10,1... | collective-permute-start | bytes 1179656 | tf_op jit(solution)/shard_map/ppermute | solution.py:17
  55.3 12.1 %collective-permute-start.20 = (bf16[2,96,1024]{2,1,0:T(8,128)(2,1)S(1)}, bf16[2,96,1024]{2,1,0:T(8,128)(2,1)S(1)}, u32[]{:S(2)}, u32[]{:S(2)}) collective-permute-start(bf16[2,96,1024]{2,1,0:T(8,128)(2,1)S(1)} %pad_maximum_fusion.refs_8_), channel_id=1, source_target_pairs={{0,3},{1,0},{2,1},{3,2},{4,7},{5,4},{6,5},{7,6},{8,11},{9,8},{10,9... | collective-permute-start | bytes 1179656 | tf_op jit(solution)/shard_map/ppermute | solution.py:17
  57.5 16.0 %collective-permute-start.12 = (bf16[2,144,512]{2,1,0:T(8,128)(2,1)S(1)}, bf16[2,144,512]{2,1,0:T(8,128)(2,1)S(1)}, u32[]{:S(2)}, u32[]{:S(2)}) collective-permute-start(bf16[2,144,512]{2,1,0:T(8,128)(2,1)S(1)} %pad_maximum_fusion.3.refs_1_), channel_id=1, source_target_pairs={{0,3},{1,0},{2,1},{3,2},{4,7},{5,4},{6,5},{7,6},{8,11},{9,8},{10,9... | collective-permute-start | bytes 884744 | tf_op jit(solution)/shard_map/ppermute | solution.py:17
  58.8 18.2 %collective-permute-start.10 = (bf16[2,144,512]{2,1,0:T(8,128)(2,1)S(1)}, bf16[2,144,512]{2,1,0:T(8,128)(2,1)S(1)}, u32[]{:S(2)}, u32[]{:S(2)}) collective-permute-start(bf16[2,144,512]{2,1,0:T(8,128)(2,1)S(1)} %pad_maximum_fusion.3.refs_1_), channel_id=1, source_target_pairs={{0,1},{1,2},{2,3},{3,0},{4,5},{5,6},{6,7},{7,4},{8,9},{9,10},{10,1... | collective-permute-start | bytes 884744 | tf_op jit(solution)/shard_map/ppermute | solution.py:17
  59.9 20.0 %collective-permute-start.9 = (bf16[2,144,512]{2,1,0:T(8,128)(2,1)S(1)}, bf16[2,144,512]{2,1,0:T(8,128)(2,1)S(1)}, u32[]{:S(2)}, u32[]{:S(2)}) collective-permute-start(bf16[2,144,512]{2,1,0:T(8,128)(2,1)S(1)} %pad_maximum_fusion.2.refs_0_), channel_id=1, source_target_pairs={{0,1},{1,2},{2,3},{3,0},{4,5},{5,6},{6,7},{7,4},{8,9},{9,10},{10,1... | collective-permute-start | bytes 884744 | tf_op jit(solution)/shard_map/ppermute | solution.py:17
  67.3 21.0 %collective-permute-start.22 = (bf16[2,96,1024]{2,1,0:T(8,128)(2,1)S(1)}, bf16[2,96,1024]{2,1,0:T(8,128)(2,1)S(1)}, u32[]{:S(2)}, u32[]{:S(2)}) collective-permute-start(bf16[2,96,1024]{2,1,0:T(8,128)(2,1)S(1)} %get-tuple-element.28), channel_id=1, source_target_pairs={{0,1},{1,2},{2,3},{3,0},{4,5},{5,6},{6,7},{7,4},{8,9},{9,10},{10,1... | collective-permute-start | bytes 1179656 | tf_op jit(solution)/shard_map/ppermute | solution.py:17
  67.3 21.0 %collective-permute-start.23 = (bf16[2,96,1024]{2,1,0:T(8,128)(2,1)S(1)}, bf16[2,96,1024]{2,1,0:T(8,128)(2,1)S(1)}, u32[]{:S(2)}, u32[]{:S(2)}) collective-permute-start(bf16[2,96,1024]{2,1,0:T(8,128)(2,1)S(1)} %get-tuple-element.29), channel_id=1, source_target_pairs={{0,3},{1,0},{2,1},{3,2},{4,7},{5,4},{6,5},{7,6},{8,11},{9,8},{10,9... | collective-permute-start | bytes 1179656 | tf_op jit(solution)/shard_map/ppermute | solution.py:17
  73.6 14.7 %collective-permute-start.11 = (bf16[2,144,512]{2,1,0:T(8,128)(2,1)S(1)}, bf16[2,144,512]{2,1,0:T(8,128)(2,1)S(1)}, u32[]{:S(2)}, u32[]{:S(2)}) collective-permute-start(bf16[2,144,512]{2,1,0:T(8,128)(2,1)S(1)} %pad_maximum_fusion.2.refs_0_), channel_id=1, source_target_pairs={{0,3},{1,0},{2,1},{3,2},{4,7},{5,4},{6,5},{7,6},{8,11},{9,8},{10,9... | collective-permute-start | bytes 884744 | tf_op jit(solution)/shard_map/ppermute | solution.py:17
  77.0 15.1 %collective-permute-start.14 = (bf16[2,144,512]{2,1,0:T(8,128)(2,1)S(1)}, bf16[2,144,512]{2,1,0:T(8,128)(2,1)S(1)}, u32[]{:S(2)}, u32[]{:S(2)}) collective-permute-start(bf16[2,144,512]{2,1,0:T(8,128)(2,1)S(1)} %collective-permute-done.12.refs_5_), channel_id=1, source_target_pairs={{0,3},{1,0},{2,1},{3,2},{4,7},{5,4},{6,5},{7,6},{8,11},{9,8},{10,9... | collective-permute-start | bytes 884744 | tf_op jit(solution)/shard_map/ppermute | solution.py:17
  80.0 12.2 %collective-permute-start.13 = (bf16[2,144,512]{2,1,0:T(8,128)(2,1)S(1)}, bf16[2,144,512]{2,1,0:T(8,128)(2,1)S(1)}, u32[]{:S(2)}, u32[]{:S(2)}) collective-permute-start(bf16[2,144,512]{2,1,0:T(8,128)(2,1)S(1)} %collective-permute-done.9.refs_2_), channel_id=1, source_target_pairs={{0,1},{1,2},{2,3},{3,0},{4,5},{5,6},{6,7},{7,4},{8,9},{9,10},{10,1... | collective-permute-start | bytes 884744 | tf_op jit(solution)/shard_map/ppermute | solution.py:17
  102.2 11.2 %collective-permute-start.25 = (bf16[2,256,128]{2,1,0:T(8,128)(2,1)S(1)}, bf16[2,256,128]{2,1,0:T(8,128)(2,1)S(1)}, u32[]{:S(2)}, u32[]{:S(2)}) collective-permute-start(bf16[2,256,128]{2,1,0:T(8,128)(2,1)S(1)} %get-tuple-element.31), channel_id=1, source_target_pairs={{0,128},{16,144},{32,160},{48,176},{64,192},{80,208},{96,224},{112... | collective-permute-start | bytes 393224 | tf_op jit(solution)/shard_map/ppermute | solution.py:27
  (22 other events, 368.9 us)

commit v4 on v3

--- a/solution.py
+++ b/solution.py
@@ -85,7 +85,22 @@
 PIECE = 144
 
 
-def pack_kernel(owners, slot, *refs):
+def early_kernel(out):
+    out[...] = jnp.zeros_like(out)
+
+
+def early():
+    return pl.pallas_call(
+        early_kernel,
+        out_shape=jax.ShapeDtypeStruct((8, 128), F32),
+        out_specs=VMEM,
+        cost_estimate=pl.CostEstimate(flops=4_000_000_000, bytes_accessed=4096, transcendentals=0),
+        compiler_params=pltpu.CompilerParams(vmem_limit_bytes=1 << 20),
+        name="early",
+    )()
+
+
+def pack_kernel(owners, slot, unused, *refs):
     outs, held = refs[:4], refs[4]
     group, dev = lax.axis_index("grp"), lax.axis_index("dev")
     row = lax.broadcasted_iota(jnp.int32, (256, 256), 0)
@@ -107,17 +122,17 @@
                     outs[dx][bits, :height] = held[pl.ds(start, height)]
 
 
-def pack(owners, panels):
+def pack(owners, panels, first):
     return pl.pallas_call(
         pack_kernel,
         out_shape=[jax.ShapeDtypeStruct((4, HEIGHTS[0], 512), BF16)] * 4,
-        in_specs=[SMEM, VMEM],
+        in_specs=[SMEM, VMEM, VMEM],
         out_specs=[VMEM] * 4,
         scratch_shapes=[pltpu.VMEM((1536, 512), BF16)],
         cost_estimate=pl.CostEstimate(flops=1_000_000, bytes_accessed=2_800_000, transcendentals=0),
         compiler_params=pltpu.CompilerParams(vmem_limit_bytes=16 << 20),
         name="pack",
-    )(owners, panels)
+    )(owners, panels, first)
 
 
 def pick_kernel(owners, *refs):
@@ -269,7 +284,7 @@
 def step(panels, panel_owner, interface_cols, border, block_rows, pattern, block_x):
     strips = gather_border(border.T)
 
-    chunks = pack(panel_owner.T, panels)
+    chunks = pack(panel_owner.T, panels, early())
     far = hop_x(chunks[2], 2)
     chunks = [chunks[0], hop_x(chunks[1], 1), far, hop_x(chunks[3], 3)]
     pieces = pick(panel_owner.T, chunks)

time: 146 us -> 146 us (level)
  no operation moved by 1% of the time
where the time goes in v4:
time: 146 us; the launch traced here: 144 us
  waiting for transfers between devices  72.6 us (50%)
  starting transfers between devices  62.2 us (43%)
  Pallas kernels  5.64 us (4%)
  local copies, waits for them, and re-layouts  1.72 us (1%)
    ppermute x18, waiting for transfers between devices, hop_x(): return lax.ppermute(value, 'dev', perm)  35.9 us
    ppermute x12, waiting for transfers between devices, hop_z(): return lax.ppermute(value, 'dev', perm)  27.6 us
    ppermute x18, starting transfers between devices, hop_x(): return lax.ppermute(value, 'dev', perm)  24.9 us
    ppermute x12, starting transfers between devices, hop_z(): return lax.ppermute(value, 'dev', perm)  24.3 us
    ppermute x6, starting transfers between devices, hop_y(): return lax.ppermute(value, 'grp', perm)  8.43 us
    ppermute x2, waiting for transfers between devices, swap_grp(): return lax.ppermute(value, 'grp', [(g, g ^ bits) for g in range(16)])  6.39 us
    ppermute x2, starting transfers between devices, swap_grp(): return lax.ppermute(value, 'grp', [(g, g ^ bits) for g in range(16)])  4.61 us
  transfers between devices with their start and end apart: 38, of which 19 were waited for; matrix products, arithmetic and copies ran while one was open for 0% of the time, Pallas kernels for 1%

profile of v4, /device:TPU:8, one launch (start us, length us, event | category | flops | bytes accessed | tf_op | source)
XLA Modules:
  0.0 144.4 jit_solution(8689314071477758382)
XLA Ops:
  4.4 2.6 %collective-permute-start.1 = (bf16[4,80,512]{2,1,0:T(8,128)(2,1)S(1)}, bf16[4,80,512]{2,1,0:T(8,128)(2,1)S(1)}, u32[]{:S(2)}, u32[]{:S(2)}) collective-permute-start(bf16[4,80,512]{2,1,0:T(8,128)(2,1)S(1)} %get-tuple-element.22), channel_id=1, source_target_pairs={{0,2},{1,3},{2,0},{3,1},{4,6},{5,7},{6,4},{7,5},{8,10},{9,11},{10,... | collective-permute-start | bytes 983048 | tf_op jit(solution)/shard_map/ppermute | solution.py:17
  8.5 4.6 %collective-permute-start.17 = (bf16[96,1024]{1,0:T(8,128)(2,1)S(1)}, bf16[96,1024]{1,0:T(8,128)(2,1)S(1)}, u32[]{:S(2)}, u32[]{:S(2)}) collective-permute-start(bf16[96,1024]{1,0:T(8,128)(2,1)S(1)} %bitcast.30), channel_id=1, source_target_pairs={{0,12},{1,13},{2,14},{3,15},{4,8},{5,9},{6,10},{7,11},{8,4},{9,5},... | collective-permute-start | bytes 589832 | tf_op jit(solution)/shard_map/ppermute | solution.py:22
  15.4 6.2 %collective-permute-done.1.refs_2_ = bf16[4,80,512]{2,1,0:T(8,128)(2,1)S(1)} collective-permute-done((bf16[4,80,512]{2,1,0:T(8,128)(2,1)S(1)}, bf16[4,80,512]{2,1,0:T(8,128)(2,1)S(1)}, u32[]{:S(2)}, u32[]{:S(2)}) %collective-permute-start.1) | collective-permute-done | bytes 327712 | tf_op jit(solution)/shard_map/ppermute | solution.py:17
  24.3 3.1 %collective-permute-start.4 = (bf16[144,512]{1,0:T(8,128)(2,1)S(1)}, bf16[144,512]{1,0:T(8,128)(2,1)S(1)}, u32[]{:S(2)}, u32[]{:S(2)}) collective-permute-start(bf16[144,512]{1,0:T(8,128)(2,1)S(1)} %get-tuple-element.26), channel_id=1, source_target_pairs={{0,8},{1,9},{2,10},{3,11},{4,12},{5,13},{6,14},{7,15},{8,0},{9,1},... | collective-permute-start | bytes 442376 | tf_op jit(solution)/shard_map/ppermute | solution.py:22
  27.4 8.8 %collective-permute-done.16 = bf16[96,1024]{1,0:T(8,128)(2,1)S(1)} collective-permute-done((bf16[96,1024]{1,0:T(8,128)(2,1)S(1)}, bf16[96,1024]{1,0:T(8,128)(2,1)S(1)}, u32[]{:S(2)}, u32[]{:S(2)}) %collective-permute-start.16) | collective-permute-done | bytes 196640 | tf_op jit(solution)/shard_map/ppermute | solution.py:22
  40.1 3.5 %collective-permute-start.7 = (bf16[144,512]{1,0:T(8,128)(2,1)S(1)}, bf16[144,512]{1,0:T(8,128)(2,1)S(1)}, u32[]{:S(2)}, u32[]{:S(2)}) collective-permute-start(bf16[144,512]{1,0:T(8,128)(2,1)S(1)} %pick_z.1), channel_id=1, source_target_pairs={{0,8},{1,9},{2,10},{3,11},{4,12},{5,13},{6,14},{7,15},{8,0},{9,1},... | collective-permute-start | bytes 442376 | tf_op jit(solution)/shard_map/ppermute | solution.py:22
  44.8 8.8 %collective-permute-done.7 = bf16[144,512]{1,0:T(8,128)(2,1)S(1)} collective-permute-done((bf16[144,512]{1,0:T(8,128)(2,1)S(1)}, bf16[144,512]{1,0:T(8,128)(2,1)S(1)}, u32[]{:S(2)}, u32[]{:S(2)}) %collective-permute-start.7) | collective-permute-done | bytes 147488 | tf_op jit(solution)/shard_map/ppermute | solution.py:22
  59.4 7.2 %collective-permute-done.19.refs_11_ = bf16[2,96,1024]{2,1,0:T(8,128)(2,1)S(1)} collective-permute-done((bf16[2,96,1024]{2,1,0:T(8,128)(2,1)S(1)}, bf16[2,96,1024]{2,1,0:T(8,128)(2,1)S(1)}, u32[]{:S(2)}, u32[]{:S(2)}) %collective-permute-start.19) | collective-permute-done | bytes 393248 | tf_op jit(solution)/shard_map/ppermute | solution.py:17
  66.7 3.4 %collective-permute-start.23 = (bf16[2,96,1024]{2,1,0:T(8,128)(2,1)S(1)}, bf16[2,96,1024]{2,1,0:T(8,128)(2,1)S(1)}, u32[]{:S(2)}, u32[]{:S(2)}) collective-permute-start(bf16[2,96,1024]{2,1,0:T(8,128)(2,1)S(1)} %get-tuple-element.29), channel_id=1, source_target_pairs={{0,3},{1,0},{2,1},{3,2},{4,7},{5,4},{6,5},{7,6},{8,11},{9,8},{10,9... | collective-permute-start | bytes 1179656 | tf_op jit(solution)/shard_map/ppermute | solution.py:17
  70.0 2.9 %collective-permute-done.12.refs_5_ = bf16[2,144,512]{2,1,0:T(8,128)(2,1)S(1)} collective-permute-done((bf16[2,144,512]{2,1,0:T(8,128)(2,1)S(1)}, bf16[2,144,512]{2,1,0:T(8,128)(2,1)S(1)}, u32[]{:S(2)}, u32[]{:S(2)}) %collective-permute-start.12) | collective-permute-done | bytes 294944 | tf_op jit(solution)/shard_map/ppermute | solution.py:17
  72.9 3.4 %collective-permute-start.11 = (bf16[2,144,512]{2,1,0:T(8,128)(2,1)S(1)}, bf16[2,144,512]{2,1,0:T(8,128)(2,1)S(1)}, u32[]{:S(2)}, u32[]{:S(2)}) collective-permute-start(bf16[2,144,512]{2,1,0:T(8,128)(2,1)S(1)} %pad_maximum_fusion.2.refs_0_), channel_id=1, source_target_pairs={{0,3},{1,0},{2,1},{3,2},{4,7},{5,4},{6,5},{7,6},{8,11},{9,8},{10,9... | collective-permute-start | bytes 884744 | tf_op jit(solution)/shard_map/ppermute | solution.py:17
  76.4 2.9 %collective-permute-done.9.refs_2_ = bf16[2,144,512]{2,1,0:T(8,128)(2,1)S(1)} collective-permute-done((bf16[2,144,512]{2,1,0:T(8,128)(2,1)S(1)}, bf16[2,144,512]{2,1,0:T(8,128)(2,1)S(1)}, u32[]{:S(2)}, u32[]{:S(2)}) %collective-permute-start.9) | collective-permute-done | bytes 294944 | tf_op jit(solution)/shard_map/ppermute | solution.py:17
  79.3 8.4 %collective-permute-done.11.refs_4_ = bf16[2,144,512]{2,1,0:T(8,128)(2,1)S(1)} collective-permute-done((bf16[2,144,512]{2,1,0:T(8,128)(2,1)S(1)}, bf16[2,144,512]{2,1,0:T(8,128)(2,1)S(1)}, u32[]{:S(2)}, u32[]{:S(2)}) %collective-permute-start.11) | collective-permute-done | bytes 294944 | tf_op jit(solution)/shard_map/ppermute | solution.py:17
  87.6 3.8 %collective-permute-done.14.refs_7_ = bf16[2,144,512]{2,1,0:T(8,128)(2,1)S(1)} collective-permute-done((bf16[2,144,512]{2,1,0:T(8,128)(2,1)S(1)}, bf16[2,144,512]{2,1,0:T(8,128)(2,1)S(1)}, u32[]{:S(2)}, u32[]{:S(2)}) %collective-permute-start.14) | collective-permute-done | bytes 294944 | tf_op jit(solution)/shard_map/ppermute | solution.py:17
  91.5 2.5 %tile.1.own = bf16[8,256,128]{2,1,0:T(8,128)(2,1)S(1)} custom-call(bf16[2,144,512]{2,1,0:T(8,128)(2,1)S(1)} %pad_maximum_fusion.2.refs_0_, bf16[2,144,512]{2,1,0:T(8,128)(2,1)S(1)} %pad_maximum_fusion.3.refs_1_, bf16[2,144,512]{2,1,0:T(8,128)(2,1)S(1)} %collective-permute-done.9.refs_2_, bf16[2,144,512]{2,1,0:T(8,128)(2,1)S(1)} %collective-permute-done.10.refs_3_, ...), custom_call_target="tpu_custom_call" | custom-call | flops 1500000000 | bytes 8000000 | tf_op jit(solution)/shard_map/tile/pallas_call | solution.py:228
  97.2 2.3 %collective-permute-start.28 = (bf16[2,256,128]{2,1,0:T(8,128)(2,1)S(1)}, bf16[2,256,128]{2,1,0:T(8,128)(2,1)S(1)}, u32[]{:S(2)}, u32[]{:S(2)}) collective-permute-start(bf16[2,256,128]{2,1,0:T(8,128)(2,1)S(1)} %get-tuple-element.35), channel_id=1, source_target_pairs={{0,128},{16,144},{32,160},{48,176},{64,192},{80,208},{96,224},{112... | collective-permute-start | bytes 393224 | tf_op jit(solution)/shard_map/ppermute | solution.py:27
  103.0 2.6 %collective-permute-start.26 = (bf16[2,256,128]{2,1,0:T(8,128)(2,1)S(1)}, bf16[2,256,128]{2,1,0:T(8,128)(2,1)S(1)}, u32[]{:S(2)}, u32[]{:S(2)}) collective-permute-start(bf16[2,256,128]{2,1,0:T(8,128)(2,1)S(1)} %get-tuple-element.32), channel_id=1, source_target_pairs={{0,64},{16,80},{32,96},{48,112},{64,128},{80,144},{96,160},{112,17... | collective-permute-start | bytes 393224 | tf_op jit(solution)/shard_map/ppermute | solution.py:27
  105.6 2.5 %collective-permute-done.29 = bf16[2,256,128]{2,1,0:T(8,128)(2,1)S(1)} collective-permute-done((bf16[2,256,128]{2,1,0:T(8,128)(2,1)S(1)}, bf16[2,256,128]{2,1,0:T(8,128)(2,1)S(1)}, u32[]{:S(2)}, u32[]{:S(2)}) %collective-permute-start.29) | collective-permute-done | bytes 131104 | tf_op jit(solution)/shard_map/ppermute | solution.py:27
  108.2 4.5 %collective-permute-start.31 = (bf16[2,256,128]{2,1,0:T(8,128)(2,1)S(1)}, bf16[2,256,128]{2,1,0:T(8,128)(2,1)S(1)}, u32[]{:S(2)}, u32[]{:S(2)}) collective-permute-start(bf16[2,256,128]{2,1,0:T(8,128)(2,1)S(1)} %add_convert_fusion.1), channel_id=1, source_target_pairs={{0,32},{16,48},{32,0},{48,16},{64,96},{80,112},{96,64},{112,80},{1... | collective-permute-start | bytes 393224 | tf_op jit(solution)/shard_map/ppermute | solution.py:31
  112.9 4.5 %collective-permute-done.31 = bf16[2,256,128]{2,1,0:T(8,128)(2,1)S(1)} collective-permute-done((bf16[2,256,128]{2,1,0:T(8,128)(2,1)S(1)}, bf16[2,256,128]{2,1,0:T(8,128)(2,1)S(1)}, u32[]{:S(2)}, u32[]{:S(2)}) %collective-permute-start.31) | collective-permute-done | bytes 131104 | tf_op jit(solution)/shard_map/ppermute | solution.py:31
  122.5 2.7 %collective-permute-done.32 = bf16[256,256]{1,0:T(8,128)(2,1)S(1)} collective-permute-done((bf16[256,256]{1,0:T(8,128)(2,1)S(1)}, bf16[256,256]{1,0:T(8,128)(2,1)S(1)}, u32[]{:S(2)}, u32[]{:S(2)}) %collective-permute-start.32) | collective-permute-done | bytes 131104 | tf_op jit(solution)/shard_map/ppermute | solution.py:17
  126.7 4.5 %collective-permute-start.35 = (bf16[256,256]{1,0:T(8,128)(2,1)S(1)}, bf16[256,256]{1,0:T(8,128)(2,1)S(1)}, u32[]{:S(2)}, u32[]{:S(2)}) collective-permute-start(bf16[256,256]{1,0:T(8,128)(2,1)S(1)} %add_convert_fusion), channel_id=1, source_target_pairs={{0,4},{1,5},{2,6},{3,7},{4,0},{5,1},{6,2},{7,3},{8,12},{9,13},{10,... | collective-permute-start | bytes 393224 | tf_op jit(solution)/shard_map/ppermute | solution.py:22
  134.6 2.7 %collective-permute-done.35 = bf16[256,256]{1,0:T(8,128)(2,1)S(1)} collective-permute-done((bf16[256,256]{1,0:T(8,128)(2,1)S(1)}, bf16[256,256]{1,0:T(8,128)(2,1)S(1)}, u32[]{:S(2)}, u32[]{:S(2)}) %collective-permute-start.35) | collective-permute-done | bytes 131104 | tf_op jit(solution)/shard_map/ppermute | solution.py:22
  138.2 5.4 %collective-permute-done.37 = bf16[256,256]{1,0:T(8,128)(2,1)S(1)} collective-permute-done((bf16[256,256]{1,0:T(8,128)(2,1)S(1)}, bf16[256,256]{1,0:T(8,128)(2,1)S(1)}, u32[]{:S(2)}, u32[]{:S(2)}) %collective-permute-start.37) | collective-permute-done | bytes 131104 | tf_op jit(solution)/shard_map/ppermute | solution.py:22
  (88 shorter events, 39.6 us)
Async XLA Ops:
  4.4 17.1 %collective-permute-start.1 = (bf16[4,80,512]{2,1,0:T(8,128)(2,1)S(1)}, bf16[4,80,512]{2,1,0:T(8,128)(2,1)S(1)}, u32[]{:S(2)}, u32[]{:S(2)}) collective-permute-start(bf16[4,80,512]{2,1,0:T(8,128)(2,1)S(1)} %get-tuple-element.22), channel_id=1, source_target_pairs={{0,2},{1,3},{2,0},{3,1},{4,6},{5,7},{6,4},{7,5},{8,10},{9,11},{10,... | collective-permute-start | bytes 983048 | tf_op jit(solution)/shard_map/ppermute | solution.py:17
  7.0 14.6 %collective-permute-start.2 = (bf16[4,80,512]{2,1,0:T(8,128)(2,1)S(1)}, bf16[4,80,512]{2,1,0:T(8,128)(2,1)S(1)}, u32[]{:S(2)}, u32[]{:S(2)}) collective-permute-start(bf16[4,80,512]{2,1,0:T(8,128)(2,1)S(1)} %get-tuple-element.23), channel_id=1, source_target_pairs={{0,3},{1,0},{2,1},{3,2},{4,7},{5,4},{6,5},{7,6},{8,11},{9,8},{10,9... | collective-permute-start | bytes 983048 | tf_op jit(solution)/shard_map/ppermute | solution.py:17
  8.5 18.9 %collective-permute-start.17 = (bf16[96,1024]{1,0:T(8,128)(2,1)S(1)}, bf16[96,1024]{1,0:T(8,128)(2,1)S(1)}, u32[]{:S(2)}, u32[]{:S(2)}) collective-permute-start(bf16[96,1024]{1,0:T(8,128)(2,1)S(1)} %bitcast.30), channel_id=1, source_target_pairs={{0,12},{1,13},{2,14},{3,15},{4,8},{5,9},{6,10},{7,11},{8,4},{9,5},... | collective-permute-start | bytes 589832 | tf_op jit(solution)/shard_map/ppermute | solution.py:22
  13.1 23.2 %collective-permute-start.16 = (bf16[96,1024]{1,0:T(8,128)(2,1)S(1)}, bf16[96,1024]{1,0:T(8,128)(2,1)S(1)}, u32[]{:S(2)}, u32[]{:S(2)}) collective-permute-start(bf16[96,1024]{1,0:T(8,128)(2,1)S(1)} %bitcast.31), channel_id=1, source_target_pairs={{0,8},{1,9},{2,10},{3,11},{4,12},{5,13},{6,14},{7,15},{8,0},{9,1},... | collective-permute-start | bytes 589832 | tf_op jit(solution)/shard_map/ppermute | solution.py:22
  13.5 22.9 %collective-permute-start.15 = (bf16[96,1024]{1,0:T(8,128)(2,1)S(1)}, bf16[96,1024]{1,0:T(8,128)(2,1)S(1)}, u32[]{:S(2)}, u32[]{:S(2)}) collective-permute-start(bf16[96,1024]{1,0:T(8,128)(2,1)S(1)} %bitcast.32), channel_id=1, source_target_pairs={{0,4},{1,5},{2,6},{3,7},{4,0},{5,1},{6,2},{7,3},{8,12},{9,13},{10,... | collective-permute-start | bytes 589832 | tf_op jit(solution)/shard_map/ppermute | solution.py:22
  22.2 16.3 %collective-permute-start.3 = (bf16[144,512]{1,0:T(8,128)(2,1)S(1)}, bf16[144,512]{1,0:T(8,128)(2,1)S(1)}, u32[]{:S(2)}, u32[]{:S(2)}) collective-permute-start(bf16[144,512]{1,0:T(8,128)(2,1)S(1)} %get-tuple-element.25), channel_id=1, source_target_pairs={{0,4},{1,5},{2,6},{3,7},{4,0},{5,1},{6,2},{7,3},{8,12},{9,13},{10,... | collective-permute-start | bytes 442376 | tf_op jit(solution)/shard_map/ppermute | solution.py:22
  24.3 15.1 %collective-permute-start.4 = (bf16[144,512]{1,0:T(8,128)(2,1)S(1)}, bf16[144,512]{1,0:T(8,128)(2,1)S(1)}, u32[]{:S(2)}, u32[]{:S(2)}) collective-permute-start(bf16[144,512]{1,0:T(8,128)(2,1)S(1)} %get-tuple-element.26), channel_id=1, source_target_pairs={{0,8},{1,9},{2,10},{3,11},{4,12},{5,13},{6,14},{7,15},{8,0},{9,1},... | collective-permute-start | bytes 442376 | tf_op jit(solution)/shard_map/ppermute | solution.py:22
  27.4 12.0 %collective-permute-start.5 = (bf16[144,512]{1,0:T(8,128)(2,1)S(1)}, bf16[144,512]{1,0:T(8,128)(2,1)S(1)}, u32[]{:S(2)}, u32[]{:S(2)}) collective-permute-start(bf16[144,512]{1,0:T(8,128)(2,1)S(1)} %get-tuple-element.27), channel_id=1, source_target_pairs={{0,12},{1,13},{2,14},{3,15},{4,8},{5,9},{6,10},{7,11},{8,4},{9,5},... | collective-permute-start | bytes 442376 | tf_op jit(solution)/shard_map/ppermute | solution.py:22
  36.3 21.8 %collective-permute-start.21 = (bf16[2,96,1024]{2,1,0:T(8,128)(2,1)S(1)}, bf16[2,96,1024]{2,1,0:T(8,128)(2,1)S(1)}, u32[]{:S(2)}, u32[]{:S(2)}) collective-permute-start(bf16[2,96,1024]{2,1,0:T(8,128)(2,1)S(1)} %pad_maximum_fusion.1.refs_9_), channel_id=1, source_target_pairs={{0,3},{1,0},{2,1},{3,2},{4,7},{5,4},{6,5},{7,6},{8,11},{9,8},{10,9... | collective-permute-start | bytes 1179656 | tf_op jit(solution)/shard_map/ppermute | solution.py:17
  36.4 22.8 %collective-permute-start.18 = (bf16[2,96,1024]{2,1,0:T(8,128)(2,1)S(1)}, bf16[2,96,1024]{2,1,0:T(8,128)(2,1)S(1)}, u32[]{:S(2)}, u32[]{:S(2)}) collective-permute-start(bf16[2,96,1024]{2,1,0:T(8,128)(2,1)S(1)} %pad_maximum_fusion.refs_8_), channel_id=1, source_target_pairs={{0,1},{1,2},{2,3},{3,0},{4,5},{5,6},{6,7},{7,4},{8,9},{9,10},{10,1... | collective-permute-start | bytes 1179656 | tf_op jit(solution)/shard_map/ppermute | solution.py:17
  40.1 13.5 %collective-permute-start.7 = (bf16[144,512]{1,0:T(8,128)(2,1)S(1)}, bf16[144,512]{1,0:T(8,128)(2,1)S(1)}, u32[]{:S(2)}, u32[]{:S(2)}) collective-permute-start(bf16[144,512]{1,0:T(8,128)(2,1)S(1)} %pick_z.1), channel_id=1, source_target_pairs={{0,8},{1,9},{2,10},{3,11},{4,12},{5,13},{6,14},{7,15},{8,0},{9,1},... | collective-permute-start | bytes 442376 | tf_op jit(solution)/shard_map/ppermute | solution.py:22
  43.6 11.0 %collective-permute-start.8 = (bf16[144,512]{1,0:T(8,128)(2,1)S(1)}, bf16[144,512]{1,0:T(8,128)(2,1)S(1)}, u32[]{:S(2)}, u32[]{:S(2)}) collective-permute-start(bf16[144,512]{1,0:T(8,128)(2,1)S(1)} %pick_z.1), channel_id=1, source_target_pairs={{0,12},{1,13},{2,14},{3,15},{4,8},{5,9},{6,10},{7,11},{8,4},{9,5},... | collective-permute-start | bytes 442376 | tf_op jit(solution)/shard_map/ppermute | solution.py:22
  44.8 12.1 %collective-permute-start.6 = (bf16[144,512]{1,0:T(8,128)(2,1)S(1)}, bf16[144,512]{1,0:T(8,128)(2,1)S(1)}, u32[]{:S(2)}, u32[]{:S(2)}) collective-permute-start(bf16[144,512]{1,0:T(8,128)(2,1)S(1)} %pick_z.1), channel_id=1, source_target_pairs={{0,4},{1,5},{2,6},{3,7},{4,0},{5,1},{6,2},{7,3},{8,12},{9,13},{10,... | collective-permute-start | bytes 442376 | tf_op jit(solution)/shard_map/ppermute | solution.py:22
  53.6 13.1 %collective-permute-start.19 = (bf16[2,96,1024]{2,1,0:T(8,128)(2,1)S(1)}, bf16[2,96,1024]{2,1,0:T(8,128)(2,1)S(1)}, u32[]{:S(2)}, u32[]{:S(2)}) collective-permute-start(bf16[2,96,1024]{2,1,0:T(8,128)(2,1)S(1)} %pad_maximum_fusion.1.refs_9_), channel_id=1, source_target_pairs={{0,1},{1,2},{2,3},{3,0},{4,5},{5,6},{6,7},{7,4},{8,9},{9,10},{10,1... | collective-permute-start | bytes 1179656 | tf_op jit(solution)/shard_map/ppermute | solution.py:17
  54.6 12.1 %collective-permute-start.20 = (bf16[2,96,1024]{2,1,0:T(8,128)(2,1)S(1)}, bf16[2,96,1024]{2,1,0:T(8,128)(2,1)S(1)}, u32[]{:S(2)}, u32[]{:S(2)}) collective-permute-start(bf16[2,96,1024]{2,1,0:T(8,128)(2,1)S(1)} %pad_maximum_fusion.refs_8_), channel_id=1, source_target_pairs={{0,3},{1,0},{2,1},{3,2},{4,7},{5,4},{6,5},{7,6},{8,11},{9,8},{10,9... | collective-permute-start | bytes 1179656 | tf_op jit(solution)/shard_map/ppermute | solution.py:17
  56.9 16.0 %collective-permute-start.12 = (bf16[2,144,512]{2,1,0:T(8,128)(2,1)S(1)}, bf16[2,144,512]{2,1,0:T(8,128)(2,1)S(1)}, u32[]{:S(2)}, u32[]{:S(2)}) collective-permute-start(bf16[2,144,512]{2,1,0:T(8,128)(2,1)S(1)} %pad_maximum_fusion.3.refs_1_), channel_id=1, source_target_pairs={{0,3},{1,0},{2,1},{3,2},{4,7},{5,4},{6,5},{7,6},{8,11},{9,8},{10,9... | collective-permute-start | bytes 884744 | tf_op jit(solution)/shard_map/ppermute | solution.py:17
  58.1 18.2 %collective-permute-start.10 = (bf16[2,144,512]{2,1,0:T(8,128)(2,1)S(1)}, bf16[2,144,512]{2,1,0:T(8,128)(2,1)S(1)}, u32[]{:S(2)}, u32[]{:S(2)}) collective-permute-start(bf16[2,144,512]{2,1,0:T(8,128)(2,1)S(1)} %pad_maximum_fusion.3.refs_1_), channel_id=1, source_target_pairs={{0,1},{1,2},{2,3},{3,0},{4,5},{5,6},{6,7},{7,4},{8,9},{9,10},{10,1... | collective-permute-start | bytes 884744 | tf_op jit(solution)/shard_map/ppermute | solution.py:17
  59.3 20.0 %collective-permute-start.9 = (bf16[2,144,512]{2,1,0:T(8,128)(2,1)S(1)}, bf16[2,144,512]{2,1,0:T(8,128)(2,1)S(1)}, u32[]{:S(2)}, u32[]{:S(2)}) collective-permute-start(bf16[2,144,512]{2,1,0:T(8,128)(2,1)S(1)} %pad_maximum_fusion.2.refs_0_), channel_id=1, source_target_pairs={{0,1},{1,2},{2,3},{3,0},{4,5},{5,6},{6,7},{7,4},{8,9},{9,10},{10,1... | collective-permute-start | bytes 884744 | tf_op jit(solution)/shard_map/ppermute | solution.py:17
  66.6 21.0 %collective-permute-start.22 = (bf16[2,96,1024]{2,1,0:T(8,128)(2,1)S(1)}, bf16[2,96,1024]{2,1,0:T(8,128)(2,1)S(1)}, u32[]{:S(2)}, u32[]{:S(2)}) collective-permute-start(bf16[2,96,1024]{2,1,0:T(8,128)(2,1)S(1)} %get-tuple-element.28), channel_id=1, source_target_pairs={{0,1},{1,2},{2,3},{3,0},{4,5},{5,6},{6,7},{7,4},{8,9},{9,10},{10,1... | collective-permute-start | bytes 1179656 | tf_op jit(solution)/shard_map/ppermute | solution.py:17
  66.7 21.0 %collective-permute-start.23 = (bf16[2,96,1024]{2,1,0:T(8,128)(2,1)S(1)}, bf16[2,96,1024]{2,1,0:T(8,128)(2,1)S(1)}, u32[]{:S(2)}, u32[]{:S(2)}) collective-permute-start(bf16[2,96,1024]{2,1,0:T(8,128)(2,1)S(1)} %get-tuple-element.29), channel_id=1, source_target_pairs={{0,3},{1,0},{2,1},{3,2},{4,7},{5,4},{6,5},{7,6},{8,11},{9,8},{10,9... | collective-permute-start | bytes 1179656 | tf_op jit(solution)/shard_map/ppermute | solution.py:17
  72.9 14.7 %collective-permute-start.11 = (bf16[2,144,512]{2,1,0:T(8,128)(2,1)S(1)}, bf16[2,144,512]{2,1,0:T(8,128)(2,1)S(1)}, u32[]{:S(2)}, u32[]{:S(2)}) collective-permute-start(bf16[2,144,512]{2,1,0:T(8,128)(2,1)S(1)} %pad_maximum_fusion.2.refs_0_), channel_id=1, source_target_pairs={{0,3},{1,0},{2,1},{3,2},{4,7},{5,4},{6,5},{7,6},{8,11},{9,8},{10,9... | collective-permute-start | bytes 884744 | tf_op jit(solution)/shard_map/ppermute | solution.py:17
  76.3 15.1 %collective-permute-start.14 = (bf16[2,144,512]{2,1,0:T(8,128)(2,1)S(1)}, bf16[2,144,512]{2,1,0:T(8,128)(2,1)S(1)}, u32[]{:S(2)}, u32[]{:S(2)}) collective-permute-start(bf16[2,144,512]{2,1,0:T(8,128)(2,1)S(1)} %collective-permute-done.12.refs_5_), channel_id=1, source_target_pairs={{0,3},{1,0},{2,1},{3,2},{4,7},{5,4},{6,5},{7,6},{8,11},{9,8},{10,9... | collective-permute-start | bytes 884744 | tf_op jit(solution)/shard_map/ppermute | solution.py:17
  79.3 12.2 %collective-permute-start.13 = (bf16[2,144,512]{2,1,0:T(8,128)(2,1)S(1)}, bf16[2,144,512]{2,1,0:T(8,128)(2,1)S(1)}, u32[]{:S(2)}, u32[]{:S(2)}) collective-permute-start(bf16[2,144,512]{2,1,0:T(8,128)(2,1)S(1)} %collective-permute-done.9.refs_2_), channel_id=1, source_target_pairs={{0,1},{1,2},{2,3},{3,0},{4,5},{5,6},{6,7},{7,4},{8,9},{9,10},{10,1... | collective-permute-start | bytes 884744 | tf_op jit(solution)/shard_map/ppermute | solution.py:17
  101.5 11.2 %collective-permute-start.25 = (bf16[2,256,128]{2,1,0:T(8,128)(2,1)S(1)}, bf16[2,256,128]{2,1,0:T(8,128)(2,1)S(1)}, u32[]{:S(2)}, u32[]{:S(2)}) collective-permute-start(bf16[2,256,128]{2,1,0:T(8,128)(2,1)S(1)} %get-tuple-element.31), channel_id=1, source_target_pairs={{0,128},{16,144},{32,160},{48,176},{64,192},{80,208},{96,224},{112... | collective-permute-start | bytes 393224 | tf_op jit(solution)/shard_map/ppermute | solution.py:27
  (22 other events, 369.6 us)

commit v5 on v4

--- a/solution.py
+++ b/solution.py
@@ -20,6 +20,13 @@
 def hop_z(value, bits):
     perm = [(z * 4 + x, (z ^ bits) * 4 + x) for z in range(4) for x in range(4)]
     return lax.ppermute(value, "dev", perm)
+
+
+def hops_z(values):
+    out = []
+    for bits, value in zip((1, 2, 3), values):
+        out.append(hop_z(value, bits))
+    return out
 
 
 def hop_y(value, dy):
@@ -288,7 +295,7 @@
     far = hop_x(chunks[2], 2)
     chunks = [chunks[0], hop_x(chunks[1], 1), far, hop_x(chunks[3], 3)]
     pieces = pick(panel_owner.T, chunks)
-    pieces = [pieces[0]] + [hop_z(pieces[bits], bits) for bits in (1, 2, 3)]
+    pieces = [pieces[0]] + hops_z(pieces[1:])
     piece = pick_z(panel_owner.T, pieces)
     tile = make_tile(gather_panel(piece), strips, interface_cols)
 
@@ -303,7 +310,7 @@
     partial = jnp.dot(schur, block_x, preferred_element_type=F32).astype(BF16)
     moved = [part.astype(F32) for part in [partial] + [hop_x(partial, dx) for dx in (1, 2, 3)]]
     row_sum = ((moved[0] + moved[2]) + (moved[1] + moved[3])).astype(BF16)
-    moved = [part.astype(F32) for part in [row_sum] + [hop_z(row_sum, bits) for bits in (1, 2, 3)]]
+    moved = [part.astype(F32) for part in [row_sum] + hops_z([row_sum] * 3)]
     product = (moved[0] + moved[1]) + (moved[2] + moved[3])
     return (schur, product)
 

time: 146 us -> 146 us (level)
  no operation moved by 1% of the time
where the time goes in v5:
time: 146 us; the launch traced here: 144 us
  waiting for transfers between devices  72.6 us (50%)
  starting transfers between devices  62.2 us (43%)
  Pallas kernels  5.64 us (4%)
  local copies, waits for them, and re-layouts  1.72 us (1%)
    ppermute x18, waiting for transfers between devices, hop_x(): return lax.ppermute(value, 'dev', perm)  35.9 us
    ppermute x12, waiting for transfers between devices, hop_z(): return lax.ppermute(value, 'dev', perm)  27.6 us
    ppermute x18, starting transfers between devices, hop_x(): return lax.ppermute(value, 'dev', perm)  24.9 us
    ppermute x12, starting transfers between devices, hop_z(): return lax.ppermute(value, 'dev', perm)  24.3 us
    ppermute x6, starting transfers between devices, hop_y(): return lax.ppermute(value, 'grp', perm)  8.43 us
    ppermute x2, waiting for transfers between devices, swap_grp(): return lax.ppermute(value, 'grp', [(g, g ^ bits) for g in range(16)])  6.39 us
    ppermute x2, starting transfers between devices, swap_grp(): return lax.ppermute(value, 'grp', [(g, g ^ bits) for g in range(16)])  4.61 us
  transfers between devices with their start and end apart: 38, of which 19 were waited for; matrix products, arithmetic and copies ran while one was open for 0% of the time, Pallas kernels for 1%

profile of v5, /device:TPU:8, one launch (start us, length us, event | category | flops | bytes accessed | tf_op | source)
XLA Modules:
  0.0 144.4 jit_solution(8689314071477758382)
XLA Ops:
  4.4 2.6 %collective-permute-start.1 = (bf16[4,80,512]{2,1,0:T(8,128)(2,1)S(1)}, bf16[4,80,512]{2,1,0:T(8,128)(2,1)S(1)}, u32[]{:S(2)}, u32[]{:S(2)}) collective-permute-start(bf16[4,80,512]{2,1,0:T(8,128)(2,1)S(1)} %get-tuple-element.22), channel_id=1, source_target_pairs={{0,2},{1,3},{2,0},{3,1},{4,6},{5,7},{6,4},{7,5},{8,10},{9,11},{10,... | collective-permute-start | bytes 983048 | tf_op jit(solution)/shard_map/ppermute | solution.py:17
  8.5 4.6 %collective-permute-start.17 = (bf16[96,1024]{1,0:T(8,128)(2,1)S(1)}, bf16[96,1024]{1,0:T(8,128)(2,1)S(1)}, u32[]{:S(2)}, u32[]{:S(2)}) collective-permute-start(bf16[96,1024]{1,0:T(8,128)(2,1)S(1)} %bitcast.30), channel_id=1, source_target_pairs={{0,12},{1,13},{2,14},{3,15},{4,8},{5,9},{6,10},{7,11},{8,4},{9,5},... | collective-permute-start | bytes 589832 | tf_op jit(solution)/shard_map/ppermute | solution.py:22
  15.4 6.2 %collective-permute-done.1.refs_2_ = bf16[4,80,512]{2,1,0:T(8,128)(2,1)S(1)} collective-permute-done((bf16[4,80,512]{2,1,0:T(8,128)(2,1)S(1)}, bf16[4,80,512]{2,1,0:T(8,128)(2,1)S(1)}, u32[]{:S(2)}, u32[]{:S(2)}) %collective-permute-start.1) | collective-permute-done | bytes 327712 | tf_op jit(solution)/shard_map/ppermute | solution.py:17
  24.3 3.1 %collective-permute-start.4 = (bf16[144,512]{1,0:T(8,128)(2,1)S(1)}, bf16[144,512]{1,0:T(8,128)(2,1)S(1)}, u32[]{:S(2)}, u32[]{:S(2)}) collective-permute-start(bf16[144,512]{1,0:T(8,128)(2,1)S(1)} %get-tuple-element.26), channel_id=1, source_target_pairs={{0,8},{1,9},{2,10},{3,11},{4,12},{5,13},{6,14},{7,15},{8,0},{9,1},... | collective-permute-start | bytes 442376 | tf_op jit(solution)/shard_map/ppermute | solution.py:22
  27.4 8.8 %collective-permute-done.16 = bf16[96,1024]{1,0:T(8,128)(2,1)S(1)} collective-permute-done((bf16[96,1024]{1,0:T(8,128)(2,1)S(1)}, bf16[96,1024]{1,0:T(8,128)(2,1)S(1)}, u32[]{:S(2)}, u32[]{:S(2)}) %collective-permute-start.16) | collective-permute-done | bytes 196640 | tf_op jit(solution)/shard_map/ppermute | solution.py:22
  40.1 3.5 %collective-permute-start.7 = (bf16[144,512]{1,0:T(8,128)(2,1)S(1)}, bf16[144,512]{1,0:T(8,128)(2,1)S(1)}, u32[]{:S(2)}, u32[]{:S(2)}) collective-permute-start(bf16[144,512]{1,0:T(8,128)(2,1)S(1)} %pick_z.1), channel_id=1, source_target_pairs={{0,8},{1,9},{2,10},{3,11},{4,12},{5,13},{6,14},{7,15},{8,0},{9,1},... | collective-permute-start | bytes 442376 | tf_op jit(solution)/shard_map/ppermute | solution.py:22
  44.8 8.8 %collective-permute-done.7 = bf16[144,512]{1,0:T(8,128)(2,1)S(1)} collective-permute-done((bf16[144,512]{1,0:T(8,128)(2,1)S(1)}, bf16[144,512]{1,0:T(8,128)(2,1)S(1)}, u32[]{:S(2)}, u32[]{:S(2)}) %collective-permute-start.7) | collective-permute-done | bytes 147488 | tf_op jit(solution)/shard_map/ppermute | solution.py:22
  59.4 7.2 %collective-permute-done.19.refs_11_ = bf16[2,96,1024]{2,1,0:T(8,128)(2,1)S(1)} collective-permute-done((bf16[2,96,1024]{2,1,0:T(8,128)(2,1)S(1)}, bf16[2,96,1024]{2,1,0:T(8,128)(2,1)S(1)}, u32[]{:S(2)}, u32[]{:S(2)}) %collective-permute-start.19) | collective-permute-done | bytes 393248 | tf_op jit(solution)/shard_map/ppermute | solution.py:17
  66.7 3.4 %collective-permute-start.23 = (bf16[2,96,1024]{2,1,0:T(8,128)(2,1)S(1)}, bf16[2,96,1024]{2,1,0:T(8,128)(2,1)S(1)}, u32[]{:S(2)}, u32[]{:S(2)}) collective-permute-start(bf16[2,96,1024]{2,1,0:T(8,128)(2,1)S(1)} %get-tuple-element.29), channel_id=1, source_target_pairs={{0,3},{1,0},{2,1},{3,2},{4,7},{5,4},{6,5},{7,6},{8,11},{9,8},{10,9... | collective-permute-start | bytes 1179656 | tf_op jit(solution)/shard_map/ppermute | solution.py:17
  70.0 2.9 %collective-permute-done.12.refs_5_ = bf16[2,144,512]{2,1,0:T(8,128)(2,1)S(1)} collective-permute-done((bf16[2,144,512]{2,1,0:T(8,128)(2,1)S(1)}, bf16[2,144,512]{2,1,0:T(8,128)(2,1)S(1)}, u32[]{:S(2)}, u32[]{:S(2)}) %collective-permute-start.12) | collective-permute-done | bytes 294944 | tf_op jit(solution)/shard_map/ppermute | solution.py:17
  72.9 3.4 %collective-permute-start.11 = (bf16[2,144,512]{2,1,0:T(8,128)(2,1)S(1)}, bf16[2,144,512]{2,1,0:T(8,128)(2,1)S(1)}, u32[]{:S(2)}, u32[]{:S(2)}) collective-permute-start(bf16[2,144,512]{2,1,0:T(8,128)(2,1)S(1)} %pad_maximum_fusion.2.refs_0_), channel_id=1, source_target_pairs={{0,3},{1,0},{2,1},{3,2},{4,7},{5,4},{6,5},{7,6},{8,11},{9,8},{10,9... | collective-permute-start | bytes 884744 | tf_op jit(solution)/shard_map/ppermute | solution.py:17
  76.4 2.9 %collective-permute-done.9.refs_2_ = bf16[2,144,512]{2,1,0:T(8,128)(2,1)S(1)} collective-permute-done((bf16[2,144,512]{2,1,0:T(8,128)(2,1)S(1)}, bf16[2,144,512]{2,1,0:T(8,128)(2,1)S(1)}, u32[]{:S(2)}, u32[]{:S(2)}) %collective-permute-start.9) | collective-permute-done | bytes 294944 | tf_op jit(solution)/shard_map/ppermute | solution.py:17
  79.3 8.4 %collective-permute-done.11.refs_4_ = bf16[2,144,512]{2,1,0:T(8,128)(2,1)S(1)} collective-permute-done((bf16[2,144,512]{2,1,0:T(8,128)(2,1)S(1)}, bf16[2,144,512]{2,1,0:T(8,128)(2,1)S(1)}, u32[]{:S(2)}, u32[]{:S(2)}) %collective-permute-start.11) | collective-permute-done | bytes 294944 | tf_op jit(solution)/shard_map/ppermute | solution.py:17
  87.6 3.8 %collective-permute-done.14.refs_7_ = bf16[2,144,512]{2,1,0:T(8,128)(2,1)S(1)} collective-permute-done((bf16[2,144,512]{2,1,0:T(8,128)(2,1)S(1)}, bf16[2,144,512]{2,1,0:T(8,128)(2,1)S(1)}, u32[]{:S(2)}, u32[]{:S(2)}) %collective-permute-start.14) | collective-permute-done | bytes 294944 | tf_op jit(solution)/shard_map/ppermute | solution.py:17
  91.5 2.5 %tile.1.own = bf16[8,256,128]{2,1,0:T(8,128)(2,1)S(1)} custom-call(bf16[2,144,512]{2,1,0:T(8,128)(2,1)S(1)} %pad_maximum_fusion.2.refs_0_, bf16[2,144,512]{2,1,0:T(8,128)(2,1)S(1)} %pad_maximum_fusion.3.refs_1_, bf16[2,144,512]{2,1,0:T(8,128)(2,1)S(1)} %collective-permute-done.9.refs_2_, bf16[2,144,512]{2,1,0:T(8,128)(2,1)S(1)} %collective-permute-done.10.refs_3_, ...), custom_call_target="tpu_custom_call" | custom-call | flops 1500000000 | bytes 8000000 | tf_op jit(solution)/shard_map/tile/pallas_call | solution.py:235
  97.2 2.3 %collective-permute-start.28 = (bf16[2,256,128]{2,1,0:T(8,128)(2,1)S(1)}, bf16[2,256,128]{2,1,0:T(8,128)(2,1)S(1)}, u32[]{:S(2)}, u32[]{:S(2)}) collective-permute-start(bf16[2,256,128]{2,1,0:T(8,128)(2,1)S(1)} %get-tuple-element.35), channel_id=1, source_target_pairs={{0,128},{16,144},{32,160},{48,176},{64,192},{80,208},{96,224},{112... | collective-permute-start | bytes 393224 | tf_op jit(solution)/shard_map/ppermute | solution.py:34
  103.0 2.6 %collective-permute-start.26 = (bf16[2,256,128]{2,1,0:T(8,128)(2,1)S(1)}, bf16[2,256,128]{2,1,0:T(8,128)(2,1)S(1)}, u32[]{:S(2)}, u32[]{:S(2)}) collective-permute-start(bf16[2,256,128]{2,1,0:T(8,128)(2,1)S(1)} %get-tuple-element.32), channel_id=1, source_target_pairs={{0,64},{16,80},{32,96},{48,112},{64,128},{80,144},{96,160},{112,17... | collective-permute-start | bytes 393224 | tf_op jit(solution)/shard_map/ppermute | solution.py:34
  105.6 2.5 %collective-permute-done.29 = bf16[2,256,128]{2,1,0:T(8,128)(2,1)S(1)} collective-permute-done((bf16[2,256,128]{2,1,0:T(8,128)(2,1)S(1)}, bf16[2,256,128]{2,1,0:T(8,128)(2,1)S(1)}, u32[]{:S(2)}, u32[]{:S(2)}) %collective-permute-start.29) | collective-permute-done | bytes 131104 | tf_op jit(solution)/shard_map/ppermute | solution.py:34
  108.2 4.5 %collective-permute-start.31 = (bf16[2,256,128]{2,1,0:T(8,128)(2,1)S(1)}, bf16[2,256,128]{2,1,0:T(8,128)(2,1)S(1)}, u32[]{:S(2)}, u32[]{:S(2)}) collective-permute-start(bf16[2,256,128]{2,1,0:T(8,128)(2,1)S(1)} %add_convert_fusion.1), channel_id=1, source_target_pairs={{0,32},{16,48},{32,0},{48,16},{64,96},{80,112},{96,64},{112,80},{1... | collective-permute-start | bytes 393224 | tf_op jit(solution)/shard_map/ppermute | solution.py:38
  112.9 4.5 %collective-permute-done.31 = bf16[2,256,128]{2,1,0:T(8,128)(2,1)S(1)} collective-permute-done((bf16[2,256,128]{2,1,0:T(8,128)(2,1)S(1)}, bf16[2,256,128]{2,1,0:T(8,128)(2,1)S(1)}, u32[]{:S(2)}, u32[]{:S(2)}) %collective-permute-start.31) | collective-permute-done | bytes 131104 | tf_op jit(solution)/shard_map/ppermute | solution.py:38
  122.5 2.7 %collective-permute-done.32 = bf16[256,256]{1,0:T(8,128)(2,1)S(1)} collective-permute-done((bf16[256,256]{1,0:T(8,128)(2,1)S(1)}, bf16[256,256]{1,0:T(8,128)(2,1)S(1)}, u32[]{:S(2)}, u32[]{:S(2)}) %collective-permute-start.32) | collective-permute-done | bytes 131104 | tf_op jit(solution)/shard_map/ppermute | solution.py:17
  126.7 4.5 %collective-permute-start.35 = (bf16[256,256]{1,0:T(8,128)(2,1)S(1)}, bf16[256,256]{1,0:T(8,128)(2,1)S(1)}, u32[]{:S(2)}, u32[]{:S(2)}) collective-permute-start(bf16[256,256]{1,0:T(8,128)(2,1)S(1)} %add_convert_fusion), channel_id=1, source_target_pairs={{0,4},{1,5},{2,6},{3,7},{4,0},{5,1},{6,2},{7,3},{8,12},{9,13},{10,... | collective-permute-start | bytes 393224 | tf_op jit(solution)/shard_map/ppermute | solution.py:22
  134.6 2.7 %collective-permute-done.35 = bf16[256,256]{1,0:T(8,128)(2,1)S(1)} collective-permute-done((bf16[256,256]{1,0:T(8,128)(2,1)S(1)}, bf16[256,256]{1,0:T(8,128)(2,1)S(1)}, u32[]{:S(2)}, u32[]{:S(2)}) %collective-permute-start.35) | collective-permute-done | bytes 131104 | tf_op jit(solution)/shard_map/ppermute | solution.py:22
  138.2 5.4 %collective-permute-done.37 = bf16[256,256]{1,0:T(8,128)(2,1)S(1)} collective-permute-done((bf16[256,256]{1,0:T(8,128)(2,1)S(1)}, bf16[256,256]{1,0:T(8,128)(2,1)S(1)}, u32[]{:S(2)}, u32[]{:S(2)}) %collective-permute-start.37) | collective-permute-done | bytes 131104 | tf_op jit(solution)/shard_map/ppermute | solution.py:22
  (88 shorter events, 39.6 us)
Async XLA Ops:
  4.4 17.1 %collective-permute-start.1 = (bf16[4,80,512]{2,1,0:T(8,128)(2,1)S(1)}, bf16[4,80,512]{2,1,0:T(8,128)(2,1)S(1)}, u32[]{:S(2)}, u32[]{:S(2)}) collective-permute-start(bf16[4,80,512]{2,1,0:T(8,128)(2,1)S(1)} %get-tuple-element.22), channel_id=1, source_target_pairs={{0,2},{1,3},{2,0},{3,1},{4,6},{5,7},{6,4},{7,5},{8,10},{9,11},{10,... | collective-permute-start | bytes 983048 | tf_op jit(solution)/shard_map/ppermute | solution.py:17
  7.0 14.6 %collective-permute-start.2 = (bf16[4,80,512]{2,1,0:T(8,128)(2,1)S(1)}, bf16[4,80,512]{2,1,0:T(8,128)(2,1)S(1)}, u32[]{:S(2)}, u32[]{:S(2)}) collective-permute-start(bf16[4,80,512]{2,1,0:T(8,128)(2,1)S(1)} %get-tuple-element.23), channel_id=1, source_target_pairs={{0,3},{1,0},{2,1},{3,2},{4,7},{5,4},{6,5},{7,6},{8,11},{9,8},{10,9... | collective-permute-start | bytes 983048 | tf_op jit(solution)/shard_map/ppermute | solution.py:17
  8.5 18.9 %collective-permute-start.17 = (bf16[96,1024]{1,0:T(8,128)(2,1)S(1)}, bf16[96,1024]{1,0:T(8,128)(2,1)S(1)}, u32[]{:S(2)}, u32[]{:S(2)}) collective-permute-start(bf16[96,1024]{1,0:T(8,128)(2,1)S(1)} %bitcast.30), channel_id=1, source_target_pairs={{0,12},{1,13},{2,14},{3,15},{4,8},{5,9},{6,10},{7,11},{8,4},{9,5},... | collective-permute-start | bytes 589832 | tf_op jit(solution)/shard_map/ppermute | solution.py:22
  13.1 23.2 %collective-permute-start.16 = (bf16[96,1024]{1,0:T(8,128)(2,1)S(1)}, bf16[96,1024]{1,0:T(8,128)(2,1)S(1)}, u32[]{:S(2)}, u32[]{:S(2)}) collective-permute-start(bf16[96,1024]{1,0:T(8,128)(2,1)S(1)} %bitcast.31), channel_id=1, source_target_pairs={{0,8},{1,9},{2,10},{3,11},{4,12},{5,13},{6,14},{7,15},{8,0},{9,1},... | collective-permute-start | bytes 589832 | tf_op jit(solution)/shard_map/ppermute | solution.py:22
  13.5 22.9 %collective-permute-start.15 = (bf16[96,1024]{1,0:T(8,128)(2,1)S(1)}, bf16[96,1024]{1,0:T(8,128)(2,1)S(1)}, u32[]{:S(2)}, u32[]{:S(2)}) collective-permute-start(bf16[96,1024]{1,0:T(8,128)(2,1)S(1)} %bitcast.32), channel_id=1, source_target_pairs={{0,4},{1,5},{2,6},{3,7},{4,0},{5,1},{6,2},{7,3},{8,12},{9,13},{10,... | collective-permute-start | bytes 589832 | tf_op jit(solution)/shard_map/ppermute | solution.py:22
  22.2 16.3 %collective-permute-start.3 = (bf16[144,512]{1,0:T(8,128)(2,1)S(1)}, bf16[144,512]{1,0:T(8,128)(2,1)S(1)}, u32[]{:S(2)}, u32[]{:S(2)}) collective-permute-start(bf16[144,512]{1,0:T(8,128)(2,1)S(1)} %get-tuple-element.25), channel_id=1, source_target_pairs={{0,4},{1,5},{2,6},{3,7},{4,0},{5,1},{6,2},{7,3},{8,12},{9,13},{10,... | collective-permute-start | bytes 442376 | tf_op jit(solution)/shard_map/ppermute | solution.py:22
  24.3 15.1 %collective-permute-start.4 = (bf16[144,512]{1,0:T(8,128)(2,1)S(1)}, bf16[144,512]{1,0:T(8,128)(2,1)S(1)}, u32[]{:S(2)}, u32[]{:S(2)}) collective-permute-start(bf16[144,512]{1,0:T(8,128)(2,1)S(1)} %get-tuple-element.26), channel_id=1, source_target_pairs={{0,8},{1,9},{2,10},{3,11},{4,12},{5,13},{6,14},{7,15},{8,0},{9,1},... | collective-permute-start | bytes 442376 | tf_op jit(solution)/shard_map/ppermute | solution.py:22
  27.4 12.0 %collective-permute-start.5 = (bf16[144,512]{1,0:T(8,128)(2,1)S(1)}, bf16[144,512]{1,0:T(8,128)(2,1)S(1)}, u32[]{:S(2)}, u32[]{:S(2)}) collective-permute-start(bf16[144,512]{1,0:T(8,128)(2,1)S(1)} %get-tuple-element.27), channel_id=1, source_target_pairs={{0,12},{1,13},{2,14},{3,15},{4,8},{5,9},{6,10},{7,11},{8,4},{9,5},... | collective-permute-start | bytes 442376 | tf_op jit(solution)/shard_map/ppermute | solution.py:22
  36.3 21.8 %collective-permute-start.21 = (bf16[2,96,1024]{2,1,0:T(8,128)(2,1)S(1)}, bf16[2,96,1024]{2,1,0:T(8,128)(2,1)S(1)}, u32[]{:S(2)}, u32[]{:S(2)}) collective-permute-start(bf16[2,96,1024]{2,1,0:T(8,128)(2,1)S(1)} %pad_maximum_fusion.1.refs_9_), channel_id=1, source_target_pairs={{0,3},{1,0},{2,1},{3,2},{4,7},{5,4},{6,5},{7,6},{8,11},{9,8},{10,9... | collective-permute-start | bytes 1179656 | tf_op jit(solution)/shard_map/ppermute | solution.py:17
  36.4 22.8 %collective-permute-start.18 = (bf16[2,96,1024]{2,1,0:T(8,128)(2,1)S(1)}, bf16[2,96,1024]{2,1,0:T(8,128)(2,1)S(1)}, u32[]{:S(2)}, u32[]{:S(2)}) collective-permute-start(bf16[2,96,1024]{2,1,0:T(8,128)(2,1)S(1)} %pad_maximum_fusion.refs_8_), channel_id=1, source_target_pairs={{0,1},{1,2},{2,3},{3,0},{4,5},{5,6},{6,7},{7,4},{8,9},{9,10},{10,1... | collective-permute-start | bytes 1179656 | tf_op jit(solution)/shard_map/ppermute | solution.py:17
  40.1 13.5 %collective-permute-start.7 = (bf16[144,512]{1,0:T(8,128)(2,1)S(1)}, bf16[144,512]{1,0:T(8,128)(2,1)S(1)}, u32[]{:S(2)}, u32[]{:S(2)}) collective-permute-start(bf16[144,512]{1,0:T(8,128)(2,1)S(1)} %pick_z.1), channel_id=1, source_target_pairs={{0,8},{1,9},{2,10},{3,11},{4,12},{5,13},{6,14},{7,15},{8,0},{9,1},... | collective-permute-start | bytes 442376 | tf_op jit(solution)/shard_map/ppermute | solution.py:22
  43.6 11.0 %collective-permute-start.8 = (bf16[144,512]{1,0:T(8,128)(2,1)S(1)}, bf16[144,512]{1,0:T(8,128)(2,1)S(1)}, u32[]{:S(2)}, u32[]{:S(2)}) collective-permute-start(bf16[144,512]{1,0:T(8,128)(2,1)S(1)} %pick_z.1), channel_id=1, source_target_pairs={{0,12},{1,13},{2,14},{3,15},{4,8},{5,9},{6,10},{7,11},{8,4},{9,5},... | collective-permute-start | bytes 442376 | tf_op jit(solution)/shard_map/ppermute | solution.py:22
  44.8 12.1 %collective-permute-start.6 = (bf16[144,512]{1,0:T(8,128)(2,1)S(1)}, bf16[144,512]{1,0:T(8,128)(2,1)S(1)}, u32[]{:S(2)}, u32[]{:S(2)}) collective-permute-start(bf16[144,512]{1,0:T(8,128)(2,1)S(1)} %pick_z.1), channel_id=1, source_target_pairs={{0,4},{1,5},{2,6},{3,7},{4,0},{5,1},{6,2},{7,3},{8,12},{9,13},{10,... | collective-permute-start | bytes 442376 | tf_op jit(solution)/shard_map/ppermute | solution.py:22
  53.6 13.1 %collective-permute-start.19 = (bf16[2,96,1024]{2,1,0:T(8,128)(2,1)S(1)}, bf16[2,96,1024]{2,1,0:T(8,128)(2,1)S(1)}, u32[]{:S(2)}, u32[]{:S(2)}) collective-permute-start(bf16[2,96,1024]{2,1,0:T(8,128)(2,1)S(1)} %pad_maximum_fusion.1.refs_9_), channel_id=1, source_target_pairs={{0,1},{1,2},{2,3},{3,0},{4,5},{5,6},{6,7},{7,4},{8,9},{9,10},{10,1... | collective-permute-start | bytes 1179656 | tf_op jit(solution)/shard_map/ppermute | solution.py:17
  54.6 12.1 %collective-permute-start.20 = (bf16[2,96,1024]{2,1,0:T(8,128)(2,1)S(1)}, bf16[2,96,1024]{2,1,0:T(8,128)(2,1)S(1)}, u32[]{:S(2)}, u32[]{:S(2)}) collective-permute-start(bf16[2,96,1024]{2,1,0:T(8,128)(2,1)S(1)} %pad_maximum_fusion.refs_8_), channel_id=1, source_target_pairs={{0,3},{1,0},{2,1},{3,2},{4,7},{5,4},{6,5},{7,6},{8,11},{9,8},{10,9... | collective-permute-start | bytes 1179656 | tf_op jit(solution)/shard_map/ppermute | solution.py:17
  56.9 16.0 %collective-permute-start.12 = (bf16[2,144,512]{2,1,0:T(8,128)(2,1)S(1)}, bf16[2,144,512]{2,1,0:T(8,128)(2,1)S(1)}, u32[]{:S(2)}, u32[]{:S(2)}) collective-permute-start(bf16[2,144,512]{2,1,0:T(8,128)(2,1)S(1)} %pad_maximum_fusion.3.refs_1_), channel_id=1, source_target_pairs={{0,3},{1,0},{2,1},{3,2},{4,7},{5,4},{6,5},{7,6},{8,11},{9,8},{10,9... | collective-permute-start | bytes 884744 | tf_op jit(solution)/shard_map/ppermute | solution.py:17
  58.1 18.2 %collective-permute-start.10 = (bf16[2,144,512]{2,1,0:T(8,128)(2,1)S(1)}, bf16[2,144,512]{2,1,0:T(8,128)(2,1)S(1)}, u32[]{:S(2)}, u32[]{:S(2)}) collective-permute-start(bf16[2,144,512]{2,1,0:T(8,128)(2,1)S(1)} %pad_maximum_fusion.3.refs_1_), channel_id=1, source_target_pairs={{0,1},{1,2},{2,3},{3,0},{4,5},{5,6},{6,7},{7,4},{8,9},{9,10},{10,1... | collective-permute-start | bytes 884744 | tf_op jit(solution)/shard_map/ppermute | solution.py:17
  59.3 20.0 %collective-permute-start.9 = (bf16[2,144,512]{2,1,0:T(8,128)(2,1)S(1)}, bf16[2,144,512]{2,1,0:T(8,128)(2,1)S(1)}, u32[]{:S(2)}, u32[]{:S(2)}) collective-permute-start(bf16[2,144,512]{2,1,0:T(8,128)(2,1)S(1)} %pad_maximum_fusion.2.refs_0_), channel_id=1, source_target_pairs={{0,1},{1,2},{2,3},{3,0},{4,5},{5,6},{6,7},{7,4},{8,9},{9,10},{10,1... | collective-permute-start | bytes 884744 | tf_op jit(solution)/shard_map/ppermute | solution.py:17
  66.6 21.0 %collective-permute-start.22 = (bf16[2,96,1024]{2,1,0:T(8,128)(2,1)S(1)}, bf16[2,96,1024]{2,1,0:T(8,128)(2,1)S(1)}, u32[]{:S(2)}, u32[]{:S(2)}) collective-permute-start(bf16[2,96,1024]{2,1,0:T(8,128)(2,1)S(1)} %get-tuple-element.28), channel_id=1, source_target_pairs={{0,1},{1,2},{2,3},{3,0},{4,5},{5,6},{6,7},{7,4},{8,9},{9,10},{10,1... | collective-permute-start | bytes 1179656 | tf_op jit(solution)/shard_map/ppermute | solution.py:17
  66.7 21.0 %collective-permute-start.23 = (bf16[2,96,1024]{2,1,0:T(8,128)(2,1)S(1)}, bf16[2,96,1024]{2,1,0:T(8,128)(2,1)S(1)}, u32[]{:S(2)}, u32[]{:S(2)}) collective-permute-start(bf16[2,96,1024]{2,1,0:T(8,128)(2,1)S(1)} %get-tuple-element.29), channel_id=1, source_target_pairs={{0,3},{1,0},{2,1},{3,2},{4,7},{5,4},{6,5},{7,6},{8,11},{9,8},{10,9... | collective-permute-start | bytes 1179656 | tf_op jit(solution)/shard_map/ppermute | solution.py:17
  72.9 14.7 %collective-permute-start.11 = (bf16[2,144,512]{2,1,0:T(8,128)(2,1)S(1)}, bf16[2,144,512]{2,1,0:T(8,128)(2,1)S(1)}, u32[]{:S(2)}, u32[]{:S(2)}) collective-permute-start(bf16[2,144,512]{2,1,0:T(8,128)(2,1)S(1)} %pad_maximum_fusion.2.refs_0_), channel_id=1, source_target_pairs={{0,3},{1,0},{2,1},{3,2},{4,7},{5,4},{6,5},{7,6},{8,11},{9,8},{10,9... | collective-permute-start | bytes 884744 | tf_op jit(solution)/shard_map/ppermute | solution.py:17
  76.3 15.1 %collective-permute-start.14 = (bf16[2,144,512]{2,1,0:T(8,128)(2,1)S(1)}, bf16[2,144,512]{2,1,0:T(8,128)(2,1)S(1)}, u32[]{:S(2)}, u32[]{:S(2)}) collective-permute-start(bf16[2,144,512]{2,1,0:T(8,128)(2,1)S(1)} %collective-permute-done.12.refs_5_), channel_id=1, source_target_pairs={{0,3},{1,0},{2,1},{3,2},{4,7},{5,4},{6,5},{7,6},{8,11},{9,8},{10,9... | collective-permute-start | bytes 884744 | tf_op jit(solution)/shard_map/ppermute | solution.py:17
  79.3 12.2 %collective-permute-start.13 = (bf16[2,144,512]{2,1,0:T(8,128)(2,1)S(1)}, bf16[2,144,512]{2,1,0:T(8,128)(2,1)S(1)}, u32[]{:S(2)}, u32[]{:S(2)}) collective-permute-start(bf16[2,144,512]{2,1,0:T(8,128)(2,1)S(1)} %collective-permute-done.9.refs_2_), channel_id=1, source_target_pairs={{0,1},{1,2},{2,3},{3,0},{4,5},{5,6},{6,7},{7,4},{8,9},{9,10},{10,1... | collective-permute-start | bytes 884744 | tf_op jit(solution)/shard_map/ppermute | solution.py:17
  101.5 11.2 %collective-permute-start.25 = (bf16[2,256,128]{2,1,0:T(8,128)(2,1)S(1)}, bf16[2,256,128]{2,1,0:T(8,128)(2,1)S(1)}, u32[]{:S(2)}, u32[]{:S(2)}) collective-permute-start(bf16[2,256,128]{2,1,0:T(8,128)(2,1)S(1)} %get-tuple-element.31), channel_id=1, source_target_pairs={{0,128},{16,144},{32,160},{48,176},{64,192},{80,208},{96,224},{112... | collective-permute-start | bytes 393224 | tf_op jit(solution)/shard_map/ppermute | solution.py:34
  (22 other events, 369.6 us)

commit v6 on v5

--- a/solution.py
+++ b/solution.py
@@ -308,10 +308,10 @@
     schur = masked.reshape(256, 256).astype(BF16)
 
     partial = jnp.dot(schur, block_x, preferred_element_type=F32).astype(BF16)
-    moved = [part.astype(F32) for part in [partial] + [hop_x(partial, dx) for dx in (1, 2, 3)]]
-    row_sum = ((moved[0] + moved[2]) + (moved[1] + moved[3])).astype(BF16)
-    moved = [part.astype(F32) for part in [row_sum] + hops_z([row_sum] * 3)]
-    product = (moved[0] + moved[1]) + (moved[2] + moved[3])
+    moved = [part.astype(F32) for part in [partial] + hops_z([partial] * 3)]
+    line_sum = ((moved[0] + moved[1]) + (moved[2] + moved[3])).astype(BF16)
+    moved = [part.astype(F32) for part in [line_sum] + [hop_x(line_sum, dx) for dx in (1, 2, 3)]]
+    product = (moved[0] + moved[2]) + (moved[1] + moved[3])
     return (schur, product)
 
 

time: 146 us -> 145 us (level)
  no operation moved by 1% of the time
where the time goes in v6:
time: 145 us; the launch traced here: 144 us
  waiting for transfers between devices  72.8 us (50%)
  starting transfers between devices  61.2 us (42%)
  Pallas kernels  5.64 us (4%)
  local copies, waits for them, and re-layouts  1.72 us (1%)
    ppermute x18, waiting for transfers between devices, hop_x(): return lax.ppermute(value, 'dev', perm)  36 us
    ppermute x12, waiting for transfers between devices, hop_z(): return lax.ppermute(value, 'dev', perm)  27.6 us
    ppermute x18, starting transfers between devices, hop_x(): return lax.ppermute(value, 'dev', perm)  25.1 us
    ppermute x12, starting transfers between devices, hop_z(): return lax.ppermute(value, 'dev', perm)  23 us
    ppermute x6, starting transfers between devices, hop_y(): return lax.ppermute(value, 'grp', perm)  8.43 us
    ppermute x2, waiting for transfers between devices, swap_grp(): return lax.ppermute(value, 'grp', [(g, g ^ bits) for g in range(16)])  6.39 us
    ppermute x2, starting transfers between devices, swap_grp(): return lax.ppermute(value, 'grp', [(g, g ^ bits) for g in range(16)])  4.61 us
  transfers between devices with their start and end apart: 38, of which 19 were waited for; matrix products, arithmetic and copies ran while one was open for 0% of the time, Pallas kernels for 1%

profile of v6, /device:TPU:8, one launch (start us, length us, event | category | flops | bytes accessed | tf_op | source)
XLA Modules:
  0.0 143.5 jit_solution(17755614000345867146)
XLA Ops:
  4.4 2.6 %collective-permute-start.1 = (bf16[4,80,512]{2,1,0:T(8,128)(2,1)S(1)}, bf16[4,80,512]{2,1,0:T(8,128)(2,1)S(1)}, u32[]{:S(2)}, u32[]{:S(2)}) collective-permute-start(bf16[4,80,512]{2,1,0:T(8,128)(2,1)S(1)} %get-tuple-element.22), channel_id=1, source_target_pairs={{0,2},{1,3},{2,0},{3,1},{4,6},{5,7},{6,4},{7,5},{8,10},{9,11},{10,... | collective-permute-start | bytes 983048 | tf_op jit(solution)/shard_map/ppermute | solution.py:17
  8.5 4.6 %collective-permute-start.17 = (bf16[96,1024]{1,0:T(8,128)(2,1)S(1)}, bf16[96,1024]{1,0:T(8,128)(2,1)S(1)}, u32[]{:S(2)}, u32[]{:S(2)}) collective-permute-start(bf16[96,1024]{1,0:T(8,128)(2,1)S(1)} %bitcast.30), channel_id=1, source_target_pairs={{0,12},{1,13},{2,14},{3,15},{4,8},{5,9},{6,10},{7,11},{8,4},{9,5},... | collective-permute-start | bytes 589832 | tf_op jit(solution)/shard_map/ppermute | solution.py:22
  15.4 6.2 %collective-permute-done.1.refs_2_ = bf16[4,80,512]{2,1,0:T(8,128)(2,1)S(1)} collective-permute-done((bf16[4,80,512]{2,1,0:T(8,128)(2,1)S(1)}, bf16[4,80,512]{2,1,0:T(8,128)(2,1)S(1)}, u32[]{:S(2)}, u32[]{:S(2)}) %collective-permute-start.1) | collective-permute-done | bytes 327712 | tf_op jit(solution)/shard_map/ppermute | solution.py:17
  24.3 3.1 %collective-permute-start.4 = (bf16[144,512]{1,0:T(8,128)(2,1)S(1)}, bf16[144,512]{1,0:T(8,128)(2,1)S(1)}, u32[]{:S(2)}, u32[]{:S(2)}) collective-permute-start(bf16[144,512]{1,0:T(8,128)(2,1)S(1)} %get-tuple-element.26), channel_id=1, source_target_pairs={{0,8},{1,9},{2,10},{3,11},{4,12},{5,13},{6,14},{7,15},{8,0},{9,1},... | collective-permute-start | bytes 442376 | tf_op jit(solution)/shard_map/ppermute | solution.py:22
  27.4 8.8 %collective-permute-done.16 = bf16[96,1024]{1,0:T(8,128)(2,1)S(1)} collective-permute-done((bf16[96,1024]{1,0:T(8,128)(2,1)S(1)}, bf16[96,1024]{1,0:T(8,128)(2,1)S(1)}, u32[]{:S(2)}, u32[]{:S(2)}) %collective-permute-start.16) | collective-permute-done | bytes 196640 | tf_op jit(solution)/shard_map/ppermute | solution.py:22
  40.1 3.5 %collective-permute-start.7 = (bf16[144,512]{1,0:T(8,128)(2,1)S(1)}, bf16[144,512]{1,0:T(8,128)(2,1)S(1)}, u32[]{:S(2)}, u32[]{:S(2)}) collective-permute-start(bf16[144,512]{1,0:T(8,128)(2,1)S(1)} %pick_z.1), channel_id=1, source_target_pairs={{0,8},{1,9},{2,10},{3,11},{4,12},{5,13},{6,14},{7,15},{8,0},{9,1},... | collective-permute-start | bytes 442376 | tf_op jit(solution)/shard_map/ppermute | solution.py:22
  44.8 8.8 %collective-permute-done.7 = bf16[144,512]{1,0:T(8,128)(2,1)S(1)} collective-permute-done((bf16[144,512]{1,0:T(8,128)(2,1)S(1)}, bf16[144,512]{1,0:T(8,128)(2,1)S(1)}, u32[]{:S(2)}, u32[]{:S(2)}) %collective-permute-start.7) | collective-permute-done | bytes 147488 | tf_op jit(solution)/shard_map/ppermute | solution.py:22
  59.4 7.2 %collective-permute-done.19.refs_11_ = bf16[2,96,1024]{2,1,0:T(8,128)(2,1)S(1)} collective-permute-done((bf16[2,96,1024]{2,1,0:T(8,128)(2,1)S(1)}, bf16[2,96,1024]{2,1,0:T(8,128)(2,1)S(1)}, u32[]{:S(2)}, u32[]{:S(2)}) %collective-permute-start.19) | collective-permute-done | bytes 393248 | tf_op jit(solution)/shard_map/ppermute | solution.py:17
  66.7 3.4 %collective-permute-start.23 = (bf16[2,96,1024]{2,1,0:T(8,128)(2,1)S(1)}, bf16[2,96,1024]{2,1,0:T(8,128)(2,1)S(1)}, u32[]{:S(2)}, u32[]{:S(2)}) collective-permute-start(bf16[2,96,1024]{2,1,0:T(8,128)(2,1)S(1)} %get-tuple-element.29), channel_id=1, source_target_pairs={{0,3},{1,0},{2,1},{3,2},{4,7},{5,4},{6,5},{7,6},{8,11},{9,8},{10,9... | collective-permute-start | bytes 1179656 | tf_op jit(solution)/shard_map/ppermute | solution.py:17
  70.0 2.9 %collective-permute-done.12.refs_5_ = bf16[2,144,512]{2,1,0:T(8,128)(2,1)S(1)} collective-permute-done((bf16[2,144,512]{2,1,0:T(8,128)(2,1)S(1)}, bf16[2,144,512]{2,1,0:T(8,128)(2,1)S(1)}, u32[]{:S(2)}, u32[]{:S(2)}) %collective-permute-start.12) | collective-permute-done | bytes 294944 | tf_op jit(solution)/shard_map/ppermute | solution.py:17
  72.9 3.4 %collective-permute-start.11 = (bf16[2,144,512]{2,1,0:T(8,128)(2,1)S(1)}, bf16[2,144,512]{2,1,0:T(8,128)(2,1)S(1)}, u32[]{:S(2)}, u32[]{:S(2)}) collective-permute-start(bf16[2,144,512]{2,1,0:T(8,128)(2,1)S(1)} %pad_maximum_fusion.2.refs_0_), channel_id=1, source_target_pairs={{0,3},{1,0},{2,1},{3,2},{4,7},{5,4},{6,5},{7,6},{8,11},{9,8},{10,9... | collective-permute-start | bytes 884744 | tf_op jit(solution)/shard_map/ppermute | solution.py:17
  76.4 2.9 %collective-permute-done.9.refs_2_ = bf16[2,144,512]{2,1,0:T(8,128)(2,1)S(1)} collective-permute-done((bf16[2,144,512]{2,1,0:T(8,128)(2,1)S(1)}, bf16[2,144,512]{2,1,0:T(8,128)(2,1)S(1)}, u32[]{:S(2)}, u32[]{:S(2)}) %collective-permute-start.9) | collective-permute-done | bytes 294944 | tf_op jit(solution)/shard_map/ppermute | solution.py:17
  79.3 8.4 %collective-permute-done.11.refs_4_ = bf16[2,144,512]{2,1,0:T(8,128)(2,1)S(1)} collective-permute-done((bf16[2,144,512]{2,1,0:T(8,128)(2,1)S(1)}, bf16[2,144,512]{2,1,0:T(8,128)(2,1)S(1)}, u32[]{:S(2)}, u32[]{:S(2)}) %collective-permute-start.11) | collective-permute-done | bytes 294944 | tf_op jit(solution)/shard_map/ppermute | solution.py:17
  87.6 3.8 %collective-permute-done.14.refs_7_ = bf16[2,144,512]{2,1,0:T(8,128)(2,1)S(1)} collective-permute-done((bf16[2,144,512]{2,1,0:T(8,128)(2,1)S(1)}, bf16[2,144,512]{2,1,0:T(8,128)(2,1)S(1)}, u32[]{:S(2)}, u32[]{:S(2)}) %collective-permute-start.14) | collective-permute-done | bytes 294944 | tf_op jit(solution)/shard_map/ppermute | solution.py:17
  91.5 2.5 %tile.1.own = bf16[8,256,128]{2,1,0:T(8,128)(2,1)S(1)} custom-call(bf16[2,144,512]{2,1,0:T(8,128)(2,1)S(1)} %pad_maximum_fusion.2.refs_0_, bf16[2,144,512]{2,1,0:T(8,128)(2,1)S(1)} %pad_maximum_fusion.3.refs_1_, bf16[2,144,512]{2,1,0:T(8,128)(2,1)S(1)} %collective-permute-done.9.refs_2_, bf16[2,144,512]{2,1,0:T(8,128)(2,1)S(1)} %collective-permute-done.10.refs_3_, ...), custom_call_target="tpu_custom_call" | custom-call | flops 1500000000 | bytes 8000000 | tf_op jit(solution)/shard_map/tile/pallas_call | solution.py:235
  97.2 2.3 %collective-permute-start.28 = (bf16[2,256,128]{2,1,0:T(8,128)(2,1)S(1)}, bf16[2,256,128]{2,1,0:T(8,128)(2,1)S(1)}, u32[]{:S(2)}, u32[]{:S(2)}) collective-permute-start(bf16[2,256,128]{2,1,0:T(8,128)(2,1)S(1)} %get-tuple-element.35), channel_id=1, source_target_pairs={{0,128},{16,144},{32,160},{48,176},{64,192},{80,208},{96,224},{112... | collective-permute-start | bytes 393224 | tf_op jit(solution)/shard_map/ppermute | solution.py:34
  103.0 2.6 %collective-permute-start.26 = (bf16[2,256,128]{2,1,0:T(8,128)(2,1)S(1)}, bf16[2,256,128]{2,1,0:T(8,128)(2,1)S(1)}, u32[]{:S(2)}, u32[]{:S(2)}) collective-permute-start(bf16[2,256,128]{2,1,0:T(8,128)(2,1)S(1)} %get-tuple-element.32), channel_id=1, source_target_pairs={{0,64},{16,80},{32,96},{48,112},{64,128},{80,144},{96,160},{112,17... | collective-permute-start | bytes 393224 | tf_op jit(solution)/shard_map/ppermute | solution.py:34
  105.6 2.5 %collective-permute-done.29 = bf16[2,256,128]{2,1,0:T(8,128)(2,1)S(1)} collective-permute-done((bf16[2,256,128]{2,1,0:T(8,128)(2,1)S(1)}, bf16[2,256,128]{2,1,0:T(8,128)(2,1)S(1)}, u32[]{:S(2)}, u32[]{:S(2)}) %collective-permute-start.29) | collective-permute-done | bytes 131104 | tf_op jit(solution)/shard_map/ppermute | solution.py:34
  108.2 4.5 %collective-permute-start.31 = (bf16[2,256,128]{2,1,0:T(8,128)(2,1)S(1)}, bf16[2,256,128]{2,1,0:T(8,128)(2,1)S(1)}, u32[]{:S(2)}, u32[]{:S(2)}) collective-permute-start(bf16[2,256,128]{2,1,0:T(8,128)(2,1)S(1)} %add_convert_fusion.1), channel_id=1, source_target_pairs={{0,32},{16,48},{32,0},{48,16},{64,96},{80,112},{96,64},{112,80},{1... | collective-permute-start | bytes 393224 | tf_op jit(solution)/shard_map/ppermute | solution.py:38
  112.9 4.5 %collective-permute-done.31 = bf16[2,256,128]{2,1,0:T(8,128)(2,1)S(1)} collective-permute-done((bf16[2,256,128]{2,1,0:T(8,128)(2,1)S(1)}, bf16[2,256,128]{2,1,0:T(8,128)(2,1)S(1)}, u32[]{:S(2)}, u32[]{:S(2)}) %collective-permute-start.31) | collective-permute-done | bytes 131104 | tf_op jit(solution)/shard_map/ppermute | solution.py:38
  118.0 3.4 %collective-permute-start.32 = (bf16[256,256]{1,0:T(8,128)(2,1)S(1)}, bf16[256,256]{1,0:T(8,128)(2,1)S(1)}, u32[]{:S(2)}, u32[]{:S(2)}) collective-permute-start(bf16[256,256]{1,0:T(8,128)(2,1)S(1)} %convolution_convert_fusion), channel_id=1, source_target_pairs={{0,4},{1,5},{2,6},{3,7},{4,0},{5,1},{6,2},{7,3},{8,12},{9,13},{10,... | collective-permute-start | bytes 393224 | tf_op jit(solution)/shard_map/ppermute | solution.py:22
  124.7 2.7 %collective-permute-done.32 = bf16[256,256]{1,0:T(8,128)(2,1)S(1)} collective-permute-done((bf16[256,256]{1,0:T(8,128)(2,1)S(1)}, bf16[256,256]{1,0:T(8,128)(2,1)S(1)}, u32[]{:S(2)}, u32[]{:S(2)}) %collective-permute-start.32) | collective-permute-done | bytes 131104 | tf_op jit(solution)/shard_map/ppermute | solution.py:22
  129.0 4.8 %collective-permute-done.34 = bf16[256,256]{1,0:T(8,128)(2,1)S(1)} collective-permute-done((bf16[256,256]{1,0:T(8,128)(2,1)S(1)}, bf16[256,256]{1,0:T(8,128)(2,1)S(1)}, u32[]{:S(2)}, u32[]{:S(2)}) %collective-permute-start.34) | collective-permute-done | bytes 131104 | tf_op jit(solution)/shard_map/ppermute | solution.py:22
  138.6 2.8 %collective-permute-done.35 = bf16[256,256]{1,0:T(8,128)(2,1)S(1)} collective-permute-done((bf16[256,256]{1,0:T(8,128)(2,1)S(1)}, bf16[256,256]{1,0:T(8,128)(2,1)S(1)}, u32[]{:S(2)}, u32[]{:S(2)}) %collective-permute-start.35) | collective-permute-done | bytes 131104 | tf_op jit(solution)/shard_map/ppermute | solution.py:17
  (88 shorter events, 40.3 us)
Async XLA Ops:
  4.4 17.1 %collective-permute-start.1 = (bf16[4,80,512]{2,1,0:T(8,128)(2,1)S(1)}, bf16[4,80,512]{2,1,0:T(8,128)(2,1)S(1)}, u32[]{:S(2)}, u32[]{:S(2)}) collective-permute-start(bf16[4,80,512]{2,1,0:T(8,128)(2,1)S(1)} %get-tuple-element.22), channel_id=1, source_target_pairs={{0,2},{1,3},{2,0},{3,1},{4,6},{5,7},{6,4},{7,5},{8,10},{9,11},{10,... | collective-permute-start | bytes 983048 | tf_op jit(solution)/shard_map/ppermute | solution.py:17
  7.0 14.6 %collective-permute-start.2 = (bf16[4,80,512]{2,1,0:T(8,128)(2,1)S(1)}, bf16[4,80,512]{2,1,0:T(8,128)(2,1)S(1)}, u32[]{:S(2)}, u32[]{:S(2)}) collective-permute-start(bf16[4,80,512]{2,1,0:T(8,128)(2,1)S(1)} %get-tuple-element.23), channel_id=1, source_target_pairs={{0,3},{1,0},{2,1},{3,2},{4,7},{5,4},{6,5},{7,6},{8,11},{9,8},{10,9... | collective-permute-start | bytes 983048 | tf_op jit(solution)/shard_map/ppermute | solution.py:17
  8.5 18.9 %collective-permute-start.17 = (bf16[96,1024]{1,0:T(8,128)(2,1)S(1)}, bf16[96,1024]{1,0:T(8,128)(2,1)S(1)}, u32[]{:S(2)}, u32[]{:S(2)}) collective-permute-start(bf16[96,1024]{1,0:T(8,128)(2,1)S(1)} %bitcast.30), channel_id=1, source_target_pairs={{0,12},{1,13},{2,14},{3,15},{4,8},{5,9},{6,10},{7,11},{8,4},{9,5},... | collective-permute-start | bytes 589832 | tf_op jit(solution)/shard_map/ppermute | solution.py:22
  13.1 23.2 %collective-permute-start.16 = (bf16[96,1024]{1,0:T(8,128)(2,1)S(1)}, bf16[96,1024]{1,0:T(8,128)(2,1)S(1)}, u32[]{:S(2)}, u32[]{:S(2)}) collective-permute-start(bf16[96,1024]{1,0:T(8,128)(2,1)S(1)} %bitcast.31), channel_id=1, source_target_pairs={{0,8},{1,9},{2,10},{3,11},{4,12},{5,13},{6,14},{7,15},{8,0},{9,1},... | collective-permute-start | bytes 589832 | tf_op jit(solution)/shard_map/ppermute | solution.py:22
  13.5 22.9 %collective-permute-start.15 = (bf16[96,1024]{1,0:T(8,128)(2,1)S(1)}, bf16[96,1024]{1,0:T(8,128)(2,1)S(1)}, u32[]{:S(2)}, u32[]{:S(2)}) collective-permute-start(bf16[96,1024]{1,0:T(8,128)(2,1)S(1)} %bitcast.32), channel_id=1, source_target_pairs={{0,4},{1,5},{2,6},{3,7},{4,0},{5,1},{6,2},{7,3},{8,12},{9,13},{10,... | collective-permute-start | bytes 589832 | tf_op jit(solution)/shard_map/ppermute | solution.py:22
  22.2 16.3 %collective-permute-start.3 = (bf16[144,512]{1,0:T(8,128)(2,1)S(1)}, bf16[144,512]{1,0:T(8,128)(2,1)S(1)}, u32[]{:S(2)}, u32[]{:S(2)}) collective-permute-start(bf16[144,512]{1,0:T(8,128)(2,1)S(1)} %get-tuple-element.25), channel_id=1, source_target_pairs={{0,4},{1,5},{2,6},{3,7},{4,0},{5,1},{6,2},{7,3},{8,12},{9,13},{10,... | collective-permute-start | bytes 442376 | tf_op jit(solution)/shard_map/ppermute | solution.py:22
  24.3 15.1 %collective-permute-start.4 = (bf16[144,512]{1,0:T(8,128)(2,1)S(1)}, bf16[144,512]{1,0:T(8,128)(2,1)S(1)}, u32[]{:S(2)}, u32[]{:S(2)}) collective-permute-start(bf16[144,512]{1,0:T(8,128)(2,1)S(1)} %get-tuple-element.26), channel_id=1, source_target_pairs={{0,8},{1,9},{2,10},{3,11},{4,12},{5,13},{6,14},{7,15},{8,0},{9,1},... | collective-permute-start | bytes 442376 | tf_op jit(solution)/shard_map/ppermute | solution.py:22
  27.4 12.0 %collective-permute-start.5 = (bf16[144,512]{1,0:T(8,128)(2,1)S(1)}, bf16[144,512]{1,0:T(8,128)(2,1)S(1)}, u32[]{:S(2)}, u32[]{:S(2)}) collective-permute-start(bf16[144,512]{1,0:T(8,128)(2,1)S(1)} %get-tuple-element.27), channel_id=1, source_target_pairs={{0,12},{1,13},{2,14},{3,15},{4,8},{5,9},{6,10},{7,11},{8,4},{9,5},... | collective-permute-start | bytes 442376 | tf_op jit(solution)/shard_map/ppermute | solution.py:22
  36.3 21.8 %collective-permute-start.21 = (bf16[2,96,1024]{2,1,0:T(8,128)(2,1)S(1)}, bf16[2,96,1024]{2,1,0:T(8,128)(2,1)S(1)}, u32[]{:S(2)}, u32[]{:S(2)}) collective-permute-start(bf16[2,96,1024]{2,1,0:T(8,128)(2,1)S(1)} %pad_maximum_fusion.1.refs_9_), channel_id=1, source_target_pairs={{0,3},{1,0},{2,1},{3,2},{4,7},{5,4},{6,5},{7,6},{8,11},{9,8},{10,9... | collective-permute-start | bytes 1179656 | tf_op jit(solution)/shard_map/ppermute | solution.py:17
  36.4 22.8 %collective-permute-start.18 = (bf16[2,96,1024]{2,1,0:T(8,128)(2,1)S(1)}, bf16[2,96,1024]{2,1,0:T(8,128)(2,1)S(1)}, u32[]{:S(2)}, u32[]{:S(2)}) collective-permute-start(bf16[2,96,1024]{2,1,0:T(8,128)(2,1)S(1)} %pad_maximum_fusion.refs_8_), channel_id=1, source_target_pairs={{0,1},{1,2},{2,3},{3,0},{4,5},{5,6},{6,7},{7,4},{8,9},{9,10},{10,1... | collective-permute-start | bytes 1179656 | tf_op jit(solution)/shard_map/ppermute | solution.py:17
  40.1 13.5 %collective-permute-start.7 = (bf16[144,512]{1,0:T(8,128)(2,1)S(1)}, bf16[144,512]{1,0:T(8,128)(2,1)S(1)}, u32[]{:S(2)}, u32[]{:S(2)}) collective-permute-start(bf16[144,512]{1,0:T(8,128)(2,1)S(1)} %pick_z.1), channel_id=1, source_target_pairs={{0,8},{1,9},{2,10},{3,11},{4,12},{5,13},{6,14},{7,15},{8,0},{9,1},... | collective-permute-start | bytes 442376 | tf_op jit(solution)/shard_map/ppermute | solution.py:22
  43.6 11.0 %collective-permute-start.8 = (bf16[144,512]{1,0:T(8,128)(2,1)S(1)}, bf16[144,512]{1,0:T(8,128)(2,1)S(1)}, u32[]{:S(2)}, u32[]{:S(2)}) collective-permute-start(bf16[144,512]{1,0:T(8,128)(2,1)S(1)} %pick_z.1), channel_id=1, source_target_pairs={{0,12},{1,13},{2,14},{3,15},{4,8},{5,9},{6,10},{7,11},{8,4},{9,5},... | collective-permute-start | bytes 442376 | tf_op jit(solution)/shard_map/ppermute | solution.py:22
  44.8 12.1 %collective-permute-start.6 = (bf16[144,512]{1,0:T(8,128)(2,1)S(1)}, bf16[144,512]{1,0:T(8,128)(2,1)S(1)}, u32[]{:S(2)}, u32[]{:S(2)}) collective-permute-start(bf16[144,512]{1,0:T(8,128)(2,1)S(1)} %pick_z.1), channel_id=1, source_target_pairs={{0,4},{1,5},{2,6},{3,7},{4,0},{5,1},{6,2},{7,3},{8,12},{9,13},{10,... | collective-permute-start | bytes 442376 | tf_op jit(solution)/shard_map/ppermute | solution.py:22
  53.6 13.1 %collective-permute-start.19 = (bf16[2,96,1024]{2,1,0:T(8,128)(2,1)S(1)}, bf16[2,96,1024]{2,1,0:T(8,128)(2,1)S(1)}, u32[]{:S(2)}, u32[]{:S(2)}) collective-permute-start(bf16[2,96,1024]{2,1,0:T(8,128)(2,1)S(1)} %pad_maximum_fusion.1.refs_9_), channel_id=1, source_target_pairs={{0,1},{1,2},{2,3},{3,0},{4,5},{5,6},{6,7},{7,4},{8,9},{9,10},{10,1... | collective-permute-start | bytes 1179656 | tf_op jit(solution)/shard_map/ppermute | solution.py:17
  54.6 12.1 %collective-permute-start.20 = (bf16[2,96,1024]{2,1,0:T(8,128)(2,1)S(1)}, bf16[2,96,1024]{2,1,0:T(8,128)(2,1)S(1)}, u32[]{:S(2)}, u32[]{:S(2)}) collective-permute-start(bf16[2,96,1024]{2,1,0:T(8,128)(2,1)S(1)} %pad_maximum_fusion.refs_8_), channel_id=1, source_target_pairs={{0,3},{1,0},{2,1},{3,2},{4,7},{5,4},{6,5},{7,6},{8,11},{9,8},{10,9... | collective-permute-start | bytes 1179656 | tf_op jit(solution)/shard_map/ppermute | solution.py:17
  56.9 16.0 %collective-permute-start.12 = (bf16[2,144,512]{2,1,0:T(8,128)(2,1)S(1)}, bf16[2,144,512]{2,1,0:T(8,128)(2,1)S(1)}, u32[]{:S(2)}, u32[]{:S(2)}) collective-permute-start(bf16[2,144,512]{2,1,0:T(8,128)(2,1)S(1)} %pad_maximum_fusion.3.refs_1_), channel_id=1, source_target_pairs={{0,3},{1,0},{2,1},{3,2},{4,7},{5,4},{6,5},{7,6},{8,11},{9,8},{10,9... | collective-permute-start | bytes 884744 | tf_op jit(solution)/shard_map/ppermute | solution.py:17
  58.1 18.2 %collective-permute-start.10 = (bf16[2,144,512]{2,1,0:T(8,128)(2,1)S(1)}, bf16[2,144,512]{2,1,0:T(8,128)(2,1)S(1)}, u32[]{:S(2)}, u32[]{:S(2)}) collective-permute-start(bf16[2,144,512]{2,1,0:T(8,128)(2,1)S(1)} %pad_maximum_fusion.3.refs_1_), channel_id=1, source_target_pairs={{0,1},{1,2},{2,3},{3,0},{4,5},{5,6},{6,7},{7,4},{8,9},{9,10},{10,1... | collective-permute-start | bytes 884744 | tf_op jit(solution)/shard_map/ppermute | solution.py:17
  59.3 20.0 %collective-permute-start.9 = (bf16[2,144,512]{2,1,0:T(8,128)(2,1)S(1)}, bf16[2,144,512]{2,1,0:T(8,128)(2,1)S(1)}, u32[]{:S(2)}, u32[]{:S(2)}) collective-permute-start(bf16[2,144,512]{2,1,0:T(8,128)(2,1)S(1)} %pad_maximum_fusion.2.refs_0_), channel_id=1, source_target_pairs={{0,1},{1,2},{2,3},{3,0},{4,5},{5,6},{6,7},{7,4},{8,9},{9,10},{10,1... | collective-permute-start | bytes 884744 | tf_op jit(solution)/shard_map/ppermute | solution.py:17
  66.6 21.0 %collective-permute-start.22 = (bf16[2,96,1024]{2,1,0:T(8,128)(2,1)S(1)}, bf16[2,96,1024]{2,1,0:T(8,128)(2,1)S(1)}, u32[]{:S(2)}, u32[]{:S(2)}) collective-permute-start(bf16[2,96,1024]{2,1,0:T(8,128)(2,1)S(1)} %get-tuple-element.28), channel_id=1, source_target_pairs={{0,1},{1,2},{2,3},{3,0},{4,5},{5,6},{6,7},{7,4},{8,9},{9,10},{10,1... | collective-permute-start | bytes 1179656 | tf_op jit(solution)/shard_map/ppermute | solution.py:17
  66.7 21.0 %collective-permute-start.23 = (bf16[2,96,1024]{2,1,0:T(8,128)(2,1)S(1)}, bf16[2,96,1024]{2,1,0:T(8,128)(2,1)S(1)}, u32[]{:S(2)}, u32[]{:S(2)}) collective-permute-start(bf16[2,96,1024]{2,1,0:T(8,128)(2,1)S(1)} %get-tuple-element.29), channel_id=1, source_target_pairs={{0,3},{1,0},{2,1},{3,2},{4,7},{5,4},{6,5},{7,6},{8,11},{9,8},{10,9... | collective-permute-start | bytes 1179656 | tf_op jit(solution)/shard_map/ppermute | solution.py:17
  72.9 14.7 %collective-permute-start.11 = (bf16[2,144,512]{2,1,0:T(8,128)(2,1)S(1)}, bf16[2,144,512]{2,1,0:T(8,128)(2,1)S(1)}, u32[]{:S(2)}, u32[]{:S(2)}) collective-permute-start(bf16[2,144,512]{2,1,0:T(8,128)(2,1)S(1)} %pad_maximum_fusion.2.refs_0_), channel_id=1, source_target_pairs={{0,3},{1,0},{2,1},{3,2},{4,7},{5,4},{6,5},{7,6},{8,11},{9,8},{10,9... | collective-permute-start | bytes 884744 | tf_op jit(solution)/shard_map/ppermute | solution.py:17
  76.3 15.1 %collective-permute-start.14 = (bf16[2,144,512]{2,1,0:T(8,128)(2,1)S(1)}, bf16[2,144,512]{2,1,0:T(8,128)(2,1)S(1)}, u32[]{:S(2)}, u32[]{:S(2)}) collective-permute-start(bf16[2,144,512]{2,1,0:T(8,128)(2,1)S(1)} %collective-permute-done.12.refs_5_), channel_id=1, source_target_pairs={{0,3},{1,0},{2,1},{3,2},{4,7},{5,4},{6,5},{7,6},{8,11},{9,8},{10,9... | collective-permute-start | bytes 884744 | tf_op jit(solution)/shard_map/ppermute | solution.py:17
  79.3 12.2 %collective-permute-start.13 = (bf16[2,144,512]{2,1,0:T(8,128)(2,1)S(1)}, bf16[2,144,512]{2,1,0:T(8,128)(2,1)S(1)}, u32[]{:S(2)}, u32[]{:S(2)}) collective-permute-start(bf16[2,144,512]{2,1,0:T(8,128)(2,1)S(1)} %collective-permute-done.9.refs_2_), channel_id=1, source_target_pairs={{0,1},{1,2},{2,3},{3,0},{4,5},{5,6},{6,7},{7,4},{8,9},{9,10},{10,1... | collective-permute-start | bytes 884744 | tf_op jit(solution)/shard_map/ppermute | solution.py:17
  101.5 11.2 %collective-permute-start.25 = (bf16[2,256,128]{2,1,0:T(8,128)(2,1)S(1)}, bf16[2,256,128]{2,1,0:T(8,128)(2,1)S(1)}, u32[]{:S(2)}, u32[]{:S(2)}) collective-permute-start(bf16[2,256,128]{2,1,0:T(8,128)(2,1)S(1)} %get-tuple-element.31), channel_id=1, source_target_pairs={{0,128},{16,144},{32,160},{48,176},{64,192},{80,208},{96,224},{112... | collective-permute-start | bytes 393224 | tf_op jit(solution)/shard_map/ppermute | solution.py:34
  (22 other events, 369.2 us)
